TPU v7x, 32 devices: a whole 2x2x4 slice. The times are simulated.
32 devices in a mesh: fsdp: 32 (over z, y, x, core).
Axes of the slice: x: 2, y: 2, z: 4, core: 2. Of those that a mesh axis runs over, the one named last changes fastest.
Arguments:
- tokens: bfloat16 [32768, 768], P('fsdp'), may hold values from -6 to 6
- cotangent: bfloat16 [32768, 768], P('fsdp'), may hold values from -6 to 6
- packed_slot: int32 [32768], replicated, may hold values from 0 to 32767, as said below
- seq_lengths: int32 [32, 4], P('fsdp'), may hold values from 1 to 512, 1024 in all within a row
- query_weight: bfloat16 [589824], P('fsdp'), may hold values from -0.21875 to 0.21875
- query_bias: bfloat16 [768], P('fsdp'), may hold values from -3 to 3
- key_weight: bfloat16 [589824], P('fsdp'), may hold values from -0.21875 to 0.21875
- value_weight: bfloat16 [589824], P('fsdp'), may hold values from -0.21875 to 0.21875
- value_bias: bfloat16 [768], P('fsdp'), may hold values from -3 to 3
- output_weight: bfloat16 [589824], P('fsdp'), may hold values from -0.875 to 0.875
- output_bias: bfloat16 [768], P('fsdp'), may hold values from -3 to 3
- attention_gain: bfloat16 [768], P('fsdp'), may hold values from 0.5 to 1.5
- attention_shift: bfloat16 [768], P('fsdp'), may hold values from -3 to 3
- inner_weight: bfloat16 [2359296], P('fsdp'), may hold values from -0.21875 to 0.21875
- inner_bias: bfloat16 [3072], P('fsdp'), may hold values from -3 to 3
- outer_weight: bfloat16 [2359296], P('fsdp'), may hold values from -0.109375 to 0.109375
- outer_bias: bfloat16 [768], P('fsdp'), may hold values from -3 to 3
- final_gain: bfloat16 [768], P('fsdp'), may hold values from 0.5 to 1.5
- final_shift: bfloat16 [768], P('fsdp'), may hold values from -3 to 3
Outputs:
- layer_out: bfloat16 [32768, 768], P('fsdp')
- tokens_grad: bfloat16 [32768, 768], P('fsdp')
- query_weight_grad: float32 [589824], P('fsdp')
- query_bias_grad: float32 [768], P('fsdp')
- key_weight_grad: float32 [589824], P('fsdp')
- value_weight_grad: float32 [589824], P('fsdp')
- value_bias_grad: float32 [768], P('fsdp')
- output_weight_grad: float32 [589824], P('fsdp')
- output_bias_grad: float32 [768], P('fsdp')
- attention_gain_grad: float32 [768], P('fsdp')
- attention_shift_grad: float32 [768], P('fsdp')
- inner_weight_grad: float32 [2359296], P('fsdp')
- inner_bias_grad: float32 [3072], P('fsdp')
- outer_weight_grad: float32 [2359296], P('fsdp')
- outer_bias_grad: float32 [768], P('fsdp')
- final_gain_grad: float32 [768], P('fsdp')
- final_shift_grad: float32 [768], P('fsdp')
Inputs may be any that keep to these rules, and one draw needn't show every extreme that they name: `packed_slot`: a permutation of the 32768 rows; of each aligned block of 1024 given rows exactly 32 have their packed row in each aligned block of 1024 packed rows. `seq_lengths`: each row sums to 1024 and its largest entry is 512.
All inputs are finite; a program needn't handle non-finite values.
Results may differ from a plain program's by a relative error of at most 0.013.
Values may be sent and summed in bfloat16 or wider, within the bound.
A program may use at most 192 MiB of HBM per device.

v0:
```python
from functools import partial

import jax
import jax.numpy as jnp
from jax import lax
from jax.sharding import PartitionSpec as P

HD = 64


EPSILON = 1e-12
NEG_LARGE = -1e30


def layer_norm(hidden, norm_gain, norm_shift):
    centered = hidden - jnp.mean(hidden, axis=-1, keepdims=True)
    variance = jnp.mean(centered * centered, axis=-1, keepdims=True)
    return centered * lax.rsqrt(variance + EPSILON) * norm_gain + norm_shift


def bf_dot(left, right):
    return jnp.dot(left, right, preferred_element_type=jnp.float32)


def column_sum(matrix):
    return jnp.sum(matrix.astype(jnp.float32), axis=0)


def on_device(
    tokens,
    cotangent,
    packed_slot,
    seq_lengths,
    query_weight,
    query_bias,
    key_weight,
    value_weight,
    value_bias,
    output_weight,
    output_bias,
    attention_gain,
    attention_shift,
    inner_weight,
    inner_bias,
    outer_weight,
    outer_bias,
    final_gain,
    final_shift,
):
    devices = lax.axis_size("fsdp")
    device_index = lax.axis_index("fsdp")
    tok_rows = tokens.shape[0]
    model_width = tokens.shape[1]
    hidden_width = inner_bias.shape[0] * devices
    peer_rows = tok_rows // devices
    total_rows = packed_slot.shape[0]
    head_count = model_width // HD
    shapes = (
        (model_width, model_width),
        (model_width,),
        (model_width, model_width),
        (model_width, model_width),
        (model_width,),
        (model_width, model_width),
        (model_width,),
        (model_width,),
        (model_width,),
        (model_width, hidden_width),
        (hidden_width,),
        (hidden_width, model_width),
        (model_width,),
        (model_width,),
        (model_width,),
    )
    gathered = (
        lax.all_gather(query_weight, "fsdp", axis=0, tiled=True),
        lax.all_gather(query_bias, "fsdp", axis=0, tiled=True),
        lax.all_gather(key_weight, "fsdp", axis=0, tiled=True),
        lax.all_gather(value_weight, "fsdp", axis=0, tiled=True),
        lax.all_gather(value_bias, "fsdp", axis=0, tiled=True),
        lax.all_gather(output_weight, "fsdp", axis=0, tiled=True),
        lax.all_gather(output_bias, "fsdp", axis=0, tiled=True),
        lax.all_gather(attention_gain, "fsdp", axis=0, tiled=True),
        lax.all_gather(attention_shift, "fsdp", axis=0, tiled=True),
        lax.all_gather(inner_weight, "fsdp", axis=0, tiled=True),
        lax.all_gather(inner_bias, "fsdp", axis=0, tiled=True),
        lax.all_gather(outer_weight, "fsdp", axis=0, tiled=True),
        lax.all_gather(outer_bias, "fsdp", axis=0, tiled=True),
        lax.all_gather(final_gain, "fsdp", axis=0, tiled=True),
        lax.all_gather(final_shift, "fsdp", axis=0, tiled=True),
    )
    params = tuple((piece.reshape(shape) for piece, shape in zip(gathered, shapes)))
    (
        wq_full,
        bq_full,
        wk_full,
        wv_full,
        bv_full,
        wo_full,
        bo_full,
        ga_full,
        sa_full,
        wi_full,
        bi_full,
        wu_full,
        bu_full,
        gf_full,
        sf_full,
    ) = params
    own_slots = lax.dynamic_slice_in_dim(packed_slot, device_index * tok_rows, tok_rows)
    send_order = jnp.argsort(own_slots, stable=True)
    outgoing = tokens[send_order].reshape(devices, peer_rows, model_width)
    outgoing_cot = cotangent[send_order].reshape(devices, peer_rows, model_width)
    arrived, arrived_cot = (
        lax.all_to_all(outgoing, "fsdp", split_axis=0, concat_axis=0, tiled=True),
        lax.all_to_all(outgoing_cot, "fsdp", split_axis=0, concat_axis=0, tiled=True),
    )
    inverse = (
        jnp.zeros((total_rows,), jnp.int32)
        .at[packed_slot]
        .set(jnp.arange(total_rows, dtype=jnp.int32))
    )
    sources = lax.dynamic_slice_in_dim(inverse, device_index * tok_rows, tok_rows) // tok_rows
    receive_order = jnp.argsort(sources, stable=True)
    counting = jnp.arange(tok_rows, dtype=jnp.int32)
    place_index = jnp.zeros((tok_rows,), jnp.int32).at[receive_order].set(counting)
    packed_rows = arrived.reshape(tok_rows, model_width)[place_index]
    packed_cot = arrived_cot.reshape(tok_rows, model_width)[place_index]
    ends = jnp.cumsum(seq_lengths[0], dtype=jnp.int32)
    segment = jnp.sum(
        (counting[:, None] >= ends[None, :]).astype(jnp.int32), axis=1, dtype=jnp.int32
    )
    visible = segment[:, None] == segment[None, :]

    def split_heads(matrix):
        return matrix.reshape(tok_rows, head_count, HD).transpose(1, 0, 2)

    def merge_heads(stacked):
        return stacked.transpose(1, 0, 2).reshape(tok_rows, model_width)

    def masked_scores(query_head, key_head):
        scores = bf_dot(query_head, key_head.T) * 0.125
        return jnp.where(visible, scores, NEG_LARGE)

    def head_forward(inputs):
        query_head, key_head, value_head = inputs
        scores = masked_scores(query_head, key_head)
        row_max = jnp.max(scores, axis=-1, keepdims=True)
        raised = jnp.exp(scores - row_max)
        row_total = jnp.sum(raised, axis=-1, keepdims=True)
        probs = raised / row_total
        head_out = bf_dot(probs.astype(jnp.bfloat16), value_head)
        return (head_out, (row_max + jnp.log(row_total))[:, 0])

    queries = (bf_dot(packed_rows, wq_full) + bq_full.astype(jnp.float32)).astype(jnp.bfloat16)
    key_rows = bf_dot(packed_rows, wk_full).astype(jnp.bfloat16)
    values = (bf_dot(packed_rows, wv_full) + bv_full.astype(jnp.float32)).astype(jnp.bfloat16)
    query_heads = split_heads(queries)
    key_heads = split_heads(key_rows)
    value_heads = split_heads(values)
    head_outs, log_totals = lax.map(head_forward, (query_heads, key_heads, value_heads))
    attended = merge_heads(head_outs).astype(jnp.bfloat16)
    branch = bf_dot(attended, wo_full) + bo_full.astype(jnp.float32)
    first_sum = packed_rows.astype(jnp.float32) + branch
    normed, first_back = jax.vjp(
        layer_norm, first_sum, ga_full.astype(jnp.float32), sa_full.astype(jnp.float32)
    )
    normed_low = normed.astype(jnp.bfloat16)
    inner_pre = bf_dot(normed_low, wi_full) + bi_full.astype(jnp.float32)
    activated_full, gelu_back = jax.vjp(partial(jax.nn.gelu, approximate=False), inner_pre)
    activated = activated_full.astype(jnp.bfloat16)
    feed_out = bf_dot(activated, wu_full) + bu_full.astype(jnp.float32)
    result, final_back = jax.vjp(
        layer_norm, normed + feed_out, gf_full.astype(jnp.float32), sf_full.astype(jnp.float32)
    )
    regathered = (
        lax.all_gather(query_weight, "fsdp", axis=0, tiled=True),
        lax.all_gather(query_bias, "fsdp", axis=0, tiled=True),
        lax.all_gather(key_weight, "fsdp", axis=0, tiled=True),
        lax.all_gather(value_weight, "fsdp", axis=0, tiled=True),
        lax.all_gather(value_bias, "fsdp", axis=0, tiled=True),
        lax.all_gather(output_weight, "fsdp", axis=0, tiled=True),
        lax.all_gather(output_bias, "fsdp", axis=0, tiled=True),
        lax.all_gather(attention_gain, "fsdp", axis=0, tiled=True),
        lax.all_gather(attention_shift, "fsdp", axis=0, tiled=True),
        lax.all_gather(inner_weight, "fsdp", axis=0, tiled=True),
        lax.all_gather(inner_bias, "fsdp", axis=0, tiled=True),
        lax.all_gather(outer_weight, "fsdp", axis=0, tiled=True),
        lax.all_gather(outer_bias, "fsdp", axis=0, tiled=True),
        lax.all_gather(final_gain, "fsdp", axis=0, tiled=True),
        lax.all_gather(final_shift, "fsdp", axis=0, tiled=True),
    )
    params = tuple((piece.reshape(shape) for piece, shape in zip(regathered, shapes)))
    (
        wq_full,
        bq_full,
        wk_full,
        wv_full,
        bv_full,
        wo_full,
        bo_full,
        ga_full,
        sa_full,
        wi_full,
        bi_full,
        wu_full,
        bu_full,
        gf_full,
        sf_full,
    ) = params
    second_grad, final_gain_grad, final_shift_grad = final_back(packed_cot.astype(jnp.float32))
    outer_low = second_grad.astype(jnp.bfloat16)
    outer_weight_grad = bf_dot(activated.T, outer_low)
    outer_bias_grad = column_sum(outer_low)
    (inner_grad,) = gelu_back(bf_dot(outer_low, wu_full.T))
    inner_low = inner_grad.astype(jnp.bfloat16)
    inner_weight_grad = bf_dot(normed_low.T, inner_low)
    inner_bias_grad = column_sum(inner_low)
    normed_grad = second_grad + bf_dot(inner_low, wi_full.T)
    first_grad, attention_gain_grad, attention_shift_grad = first_back(normed_grad)
    branch_low = first_grad.astype(jnp.bfloat16)
    output_weight_grad = bf_dot(attended.T, branch_low)
    output_bias_grad = column_sum(branch_low)
    attended_grad = bf_dot(branch_low, wo_full.T).astype(jnp.bfloat16)

    def head_backward(inputs):
        query_head, key_head, value_head, grad_head, log_total = inputs
        probs = jnp.exp(masked_scores(query_head, key_head) - log_total[:, None])
        value_grad = bf_dot(probs.astype(jnp.bfloat16).T, grad_head)
        prob_grad = bf_dot(grad_head, value_head.T)
        score_grad = probs * (prob_grad - jnp.sum(probs * prob_grad, axis=-1, keepdims=True))
        score_low = score_grad.astype(jnp.bfloat16)
        query_grad = bf_dot(score_low, key_head) * 0.125
        key_grad = bf_dot(score_low.T, query_head) * 0.125
        return (query_grad, key_grad, value_grad)

    query_grads, key_grads, value_grads = lax.map(
        head_backward, (query_heads, key_heads, value_heads, split_heads(attended_grad), log_totals)
    )
    queries_grad = merge_heads(query_grads).astype(jnp.bfloat16)
    keys_grad = merge_heads(key_grads).astype(jnp.bfloat16)
    values_grad = merge_heads(value_grads).astype(jnp.bfloat16)
    query_weight_grad = bf_dot(packed_rows.T, queries_grad)
    query_bias_grad = column_sum(queries_grad)
    key_weight_grad = bf_dot(packed_rows.T, keys_grad)
    value_weight_grad = bf_dot(packed_rows.T, values_grad)
    value_bias_grad = column_sum(values_grad)
    rows_grad = (
        first_grad
        + bf_dot(queries_grad, wq_full.T)
        + bf_dot(keys_grad, wk_full.T)
        + bf_dot(values_grad, wv_full.T)
    )
    owned = (
        lax.psum_scatter(query_weight_grad.reshape(-1), "fsdp", scatter_dimension=0, tiled=True),
        lax.psum_scatter(query_bias_grad, "fsdp", scatter_dimension=0, tiled=True),
        lax.psum_scatter(key_weight_grad.reshape(-1), "fsdp", scatter_dimension=0, tiled=True),
        lax.psum_scatter(value_weight_grad.reshape(-1), "fsdp", scatter_dimension=0, tiled=True),
        lax.psum_scatter(value_bias_grad, "fsdp", scatter_dimension=0, tiled=True),
        lax.psum_scatter(output_weight_grad.reshape(-1), "fsdp", scatter_dimension=0, tiled=True),
        lax.psum_scatter(output_bias_grad, "fsdp", scatter_dimension=0, tiled=True),
        lax.psum_scatter(attention_gain_grad, "fsdp", scatter_dimension=0, tiled=True),
        lax.psum_scatter(attention_shift_grad, "fsdp", scatter_dimension=0, tiled=True),
        lax.psum_scatter(inner_weight_grad.reshape(-1), "fsdp", scatter_dimension=0, tiled=True),
        lax.psum_scatter(inner_bias_grad, "fsdp", scatter_dimension=0, tiled=True),
        lax.psum_scatter(outer_weight_grad.reshape(-1), "fsdp", scatter_dimension=0, tiled=True),
        lax.psum_scatter(outer_bias_grad, "fsdp", scatter_dimension=0, tiled=True),
        lax.psum_scatter(final_gain_grad, "fsdp", scatter_dimension=0, tiled=True),
        lax.psum_scatter(final_shift_grad, "fsdp", scatter_dimension=0, tiled=True),
    )
    back_out = result.astype(jnp.bfloat16)[receive_order].reshape(devices, peer_rows, model_width)
    back_grad = rows_grad.astype(jnp.bfloat16)[receive_order].reshape(
        devices, peer_rows, model_width
    )
    returned_out, returned_grad = (
        lax.all_to_all(back_out, "fsdp", split_axis=0, concat_axis=0, tiled=True),
        lax.all_to_all(back_grad, "fsdp", split_axis=0, concat_axis=0, tiled=True),
    )
    restore = jnp.zeros((tok_rows,), jnp.int32).at[send_order].set(counting)
    layer_out = returned_out.reshape(tok_rows, model_width)[restore]
    tokens_grad = returned_grad.reshape(tok_rows, model_width)[restore]
    return (
        layer_out,
        tokens_grad,
        owned[0],
        owned[1],
        owned[2],
        owned[3],
        owned[4],
        owned[5],
        owned[6],
        owned[7],
        owned[8],
        owned[9],
        owned[10],
        owned[11],
        owned[12],
        owned[13],
        owned[14],
    )


def solution(mesh):
    in_specs = (
        P("fsdp", None),
        P("fsdp", None),
        P(),
        P("fsdp", None),
        P("fsdp"),
        P("fsdp"),
        P("fsdp"),
        P("fsdp"),
        P("fsdp"),
        P("fsdp"),
        P("fsdp"),
        P("fsdp"),
        P("fsdp"),
        P("fsdp"),
        P("fsdp"),
        P("fsdp"),
        P("fsdp"),
        P("fsdp"),
        P("fsdp"),
    )
    out_specs = (
        P("fsdp", None),
        P("fsdp", None),
        P("fsdp"),
        P("fsdp"),
        P("fsdp"),
        P("fsdp"),
        P("fsdp"),
        P("fsdp"),
        P("fsdp"),
        P("fsdp"),
        P("fsdp"),
        P("fsdp"),
        P("fsdp"),
        P("fsdp"),
        P("fsdp"),
        P("fsdp"),
        P("fsdp"),
    )
    return jax.shard_map(
        on_device, mesh=mesh, in_specs=in_specs, out_specs=out_specs, check_vma=False
    )
```

profile of v0, /device:TPU:0, one launch (start us, length us, event | category | flops | bytes accessed | tf_op | source)
XLA Modules:
  0.0 1244.8 jit_solution(14233803023378397401)
XLA Ops:
  11.3 4.4 sort.31
  16.3 5.2 gather_fusion.4
  21.5 7.3 all-to-all-start.2
  28.8 5.2 gather_fusion
  34.1 37.1 %all-to-all-done.2 = bf16[32,32,768]{2,1,0:T(8,128)(2,1)S(1)} async-done(((bf16[32,32,768]{2,1,0:T(8,128)(2,1)}), bf16[32,32,768]{2,1,0:T(8,128)(2,1)S(1)}, u32[]{:S(2)}, u32[]{:S(2)}) %all-to-all-start.2) | async-done | bytes 1572896 | tf_op jit(solution)/shard_map/all_to_all | solution.py:116
  71.2 4.0 all-to-all-start
  78.0 57.8 %all-reduce.26 = (bf16[768]{0:T(1024)(128)(2,1)S(1)}, bf16[768]{0:T(1024)(128)(2,1)S(1)}, bf16[768]{0:T(1024)(128)(2,1)S(1)}, bf16[768]{0:T(1024)(128)(2,1)S(1)}...) all-reduce(bf16[768]{0:T(1024)(128)(2,1)S(1)} %dynamic-update-slice, ...), channel_id=1, replica_groups=mesh['fsdp'=32] {'fsdp'}, use_global_device_ids=true, to_apply=%add | all-reduce | flops 9216 | bytes 36864
  140.7 120.1 %scatter_custom_fusion = s32[32768]{0:T(1024)S(1)} fusion(s32[32768]{0:T(1024)S(1)} %compare_select_fusion, s32[32768]{0:T(1024)S(1)} %iota.19, s32[]{:T(128)} %constant.70.clone.1), kind=kCustom, calls=%fused_computation.117 | custom fusion | bytes 131076 | tf_op jit(solution)/shard_map/scatter | solution.py:121
  260.8 4.4 sort.32
  265.8 4.5 scatter_custom_fusion.1
  271.0 3.4 reshape.249
  274.4 3.3 reshape.251
  277.7 3.3 reshape.255
  281.1 3.3 reshape.257
  284.4 5.2 gather_fusion.5
  292.5 4.0 gather_fusion.1
  303.6 3.9 convolution_convert_fusion.1
  307.5 4.2 copy.62
  314.3 4.1 copy.63
  318.6 78.5 %while.28 = (s32[]{:T(128)}, bf16[12,1024,64]{1,2,0:T(8,128)(2,1)S(1)}, f32[12,1024]{1,0:T(8,128)}, bf16[12,1024,64]{2,1,0:T(8,128)(2,1)}, bf16[12,1024,64]{2,1,...) while((s32[]{:T(128)}, ...), condition=%wide.region_9.10_spmd.clone, body=%wide.region_6.9_spmd.clone.sunk | while | flops 284163072 | bytes 13695081 | solution.py:161
  397.1 5.1 fusion.81
  404.4 8.2 reshape.258
  412.7 38.0 %multiply_convert_fusion.1 = (bf16[1024,3072]{1,0:T(8,128)(2,1)}, f32[1024,3072]{1,0:T(8,128)}, f32[1024,3072]{1,0:T(8,128)}) fusion(f32[3072]{0:T(1024)S(1)} %convert_element_type.155, bf16[768,3072]{1,0:T(8,128)(2,1)} %reshape.258, f32[1024,768]{0,1:T(8,128)} %get-tuple-element.244, f32[768]{0:T(1024)S(1)} %copy-done.28, ...), kind=kOutput, calls=%fused_computation.71 | convolution fusion | flops 5043388416 | bytes 39348224 | tf_op jit(solution)/shard_map/dot_general | solution.py:22
  450.7 9.2 reshape.259
  459.9 9.9 fusion.82
  473.8 3.3 convert_reduce_fusion.2
  477.1 17.0 %convert_reduce_fusion = (f32[3072]{0:T(1024)S(1)}, bf16[1024,3072]{1,0:T(8,128)(2,1)}) fusion(f32[1024,3072]{1,0:T(8,128)} %get-tuple-element.231, bf16[1024,768]{0,1:T(8,128)(2,1)S(1)} %get-tuple-element.225, bf16[3072,768]{1,0:T(8,128)(2,1)} %reshape.259, f32[1024,3072]{1,0:T(8,128)} %get-tuple-element.245, f32[3072]{0:T(1024)S(1)} %convert_element_type.155), kind=kOutput, calls=%fused_computation.69 | convolution fusion | flops 4885312512 | bytes 37773312 | tf_op jit(solution)/shard_map/dot_general | solution.py:22
  494.1 10.8 multiply_reduce_fusion.1
  515.1 9.8 convolution_bitcast_fusion
  525.0 7.6 fusion.87
  537.1 142.4 %while.29 = (s32[]{:T(128)}, bf16[12,1024,64]{1,2,0:T(8,128)(2,1)S(1)}, bf16[12,1024,64]{1,2,0:T(8,128)(2,1)}, bf16[12,1024,64]{1,2,0:T(8,128)(2,1)S(1)}, bf16[1...) while((s32[]{:T(128)}, ...), condition=%wide.region_21.22_spmd.clone, body=%wide.region_19.21_spmd.clone.sunk | while | flops 681704448 | bytes 34112632 | solution.py:237
  679.5 5.4 fusion.83
  688.2 4.8 fusion.84
  693.0 3.4 reshape.268
  699.2 3.2 reshape.269
  705.6 9.6 copy.76
  715.2 10.8 reshape.272
  727.8 5.2 gather_fusion.2
  733.0 4.0 all-to-all-start.1
  737.1 3.3 fusion.89
  747.0 5.2 gather_fusion.6
  752.2 39.5 %all-to-all-done.1 = bf16[32,32,768]{2,1,0:T(8,128)(2,1)S(1)} async-done(((bf16[32,32,768]{2,1,0:T(8,128)(2,1)}), bf16[32,32,768]{2,1,0:T(8,128)(2,1)S(1)}, u32[]{:S(2)}, u32[]{:S(2)}) %all-to-all-start.1) | async-done | bytes 1572896 | tf_op jit(solution)/shard_map/all_to_all | solution.py:276
  791.8 3.5 all-to-all-start.3
  795.3 4.4 scatter_custom_fusion.2
  802.5 68.6 %all-reduce.24 = (f32[768]{0:T(1024)S(1)}, f32[768]{0:T(1024)S(1)}, f32[768]{0:T(1024)S(1)}, f32[768]{0:T(1024)S(1)}, f32[768]{0:T(1024)S(1)}, /*index=5*/f32[30...) all-reduce(f32[768]{0:T(1024)S(1)} %reduce_sum.226, ...), channel_id=3, replica_groups=mesh['fsdp'=32] {'fsdp'}, use_global_device_ids=true, to_apply=%region_24.25.clone | all-reduce | flops 9216 | bytes 73728
  876.3 5.2 gather_fusion.3
  881.6 5.2 gather_fusion.7
  886.8 341.2 %all-reduce.29.cloned.1.call-done = (f32[589824]{0:T(1024)}, f32[589824]{0:T(1024)}, f32[589824]{0:T(1024)}, f32[589824]{0:T(1024)}, f32[2359296]{0:T(1024)}, /*index=5*/f32[2359296]{0:T(1024)}) async-done(((f32[589824]{0:T(1024)}, f32[589824]{0:T(1024)}, f32[589824]{0:T(1024)}, f32[589824]{0:T(1024)}, f32[2359296]{0:T(1024)}, /*index=5*/f32[2359296]{0:T(1024)}), (f32[589824]{0:T(1024)}, f32[589824]{0:T(1024)}, ...) | async-done | bytes 28311568
  (353 shorter events, 302.2 us)
Async XLA Ops:
  7.2 9.1 copy-start
  7.2 263.8 %all-gather.7.cloned.1.call-start = ((), (), s32[]{:S(2)}) async-start(), calls=%async_computation.4 | async-start | bytes 1216512 | tf_op jit(solution)/shard_map/all_gather | solution.py:76
  7.9 266.5 %all-gather.9.cloned.1.call-start = ((), (), s32[]{:S(2)}) async-start(), calls=%async_computation.5 | async-start | bytes 1216512 | tf_op jit(solution)/shard_map/all_gather | solution.py:78
  8.7 269.1 %all-gather.11.cloned.1.call-start = ((), (), s32[]{:S(2)}) async-start(), calls=%async_computation.6 | async-start | bytes 1216512 | tf_op jit(solution)/shard_map/all_gather | solution.py:79
  9.4 271.7 %all-gather.13.cloned.1.call-start = ((), (), s32[]{:S(2)}) async-start(), calls=%async_computation.7 | async-start | bytes 1216512 | tf_op jit(solution)/shard_map/all_gather | solution.py:81
  10.0 394.4 %all-gather.15.cloned.1.call-start = ((), (), s32[]{:S(2)}) async-start(), calls=%async_computation.8 | async-start | bytes 4866048 | tf_op jit(solution)/shard_map/all_gather | solution.py:85
  21.5 7.3 copy-start.2
  21.5 49.7 %all-to-all-start.2 = ((bf16[32,32,768]{2,1,0:T(8,128)(2,1)}), bf16[32,32,768]{2,1,0:T(8,128)(2,1)S(1)}, u32[]{:S(2)}, u32[]{:S(2)}) async-start(bf16[32,32,768]{2,1,0:T(8,128)(2,1)} %bitcast.176), calls=%async_computation.2 | async-start | bytes 3145728 | tf_op jit(solution)/shard_map/all_to_all | solution.py:116
  34.0 41.8 %copy-start.33 = (bf16[24]{0:T(256)(128)(2,1)S(1)}, bf16[24]{0:T(256)(128)(2,1)}, u32[]{:S(2)}) copy-start(bf16[24]{0:T(256)(128)(2,1)} %param.28) | copy-start | bytes 148
  34.0 42.1 %copy-start.34 = (bf16[24]{0:T(256)(128)(2,1)S(1)}, bf16[24]{0:T(256)(128)(2,1)}, u32[]{:S(2)}) copy-start(bf16[24]{0:T(256)(128)(2,1)} %param.31) | copy-start | bytes 148
  34.0 42.3 %copy-start.35 = (bf16[24]{0:T(256)(128)(2,1)S(1)}, bf16[24]{0:T(256)(128)(2,1)}, u32[]{:S(2)}) copy-start(bf16[24]{0:T(256)(128)(2,1)} %param.33) | copy-start | bytes 148
  34.0 42.5 %copy-start.36 = (bf16[24]{0:T(256)(128)(2,1)S(1)}, bf16[24]{0:T(256)(128)(2,1)}, u32[]{:S(2)}) copy-start(bf16[24]{0:T(256)(128)(2,1)} %param.35) | copy-start | bytes 148
  34.0 42.8 %copy-start.37 = (bf16[24]{0:T(256)(128)(2,1)S(1)}, bf16[24]{0:T(256)(128)(2,1)}, u32[]{:S(2)}) copy-start(bf16[24]{0:T(256)(128)(2,1)} %param.34) | copy-start | bytes 148
  34.0 43.0 %copy-start.38 = (bf16[24]{0:T(256)(128)(2,1)S(1)}, bf16[24]{0:T(256)(128)(2,1)}, u32[]{:S(2)}) copy-start(bf16[24]{0:T(256)(128)(2,1)} %param.39) | copy-start | bytes 148
  34.0 43.2 %copy-start.39 = (bf16[24]{0:T(256)(128)(2,1)S(1)}, bf16[24]{0:T(256)(128)(2,1)}, u32[]{:S(2)}) copy-start(bf16[24]{0:T(256)(128)(2,1)} %param.41) | copy-start | bytes 148
  34.0 43.4 %copy-start.40 = (bf16[24]{0:T(256)(128)(2,1)S(1)}, bf16[24]{0:T(256)(128)(2,1)}, u32[]{:S(2)}) copy-start(bf16[24]{0:T(256)(128)(2,1)} %param.40) | copy-start | bytes 148
  34.1 43.7 %copy-start.41 = (bf16[96]{0:T(256)(128)(2,1)S(1)}, bf16[96]{0:T(256)(128)(2,1)}, u32[]{:S(2)}) copy-start(bf16[96]{0:T(256)(128)(2,1)} %param.37) | copy-start | bytes 580
  34.1 104.1 %copy-start.42 = (s32[1,4]{1,0:T(1,128)S(1)}, s32[1,4]{1,0:T(1,128)}, u32[]{:S(2)}) copy-start(s32[1,4]{1,0:T(1,128)} %param.26) | copy-start | bytes 52
  34.1 106.6 %copy-start.21 = (s32[32768]{0:T(1024)S(1)}, s32[32768]{0:T(1024)}, u32[]{:S(2)}) copy-start(s32[32768]{0:T(1024)} %param.25) | copy-start | bytes 393220
  71.2 221.3 %all-to-all-start = ((bf16[32,32,768]{2,1,0:T(8,128)(2,1)}), bf16[32,32,768]{2,1,0:T(8,128)(2,1)S(1)}, u32[]{:S(2)}, u32[]{:S(2)}) async-start(bf16[32,32,768]{2,1,0:T(8,128)(2,1)} %bitcast.173), calls=%async_computation | async-start | bytes 3145728 | tf_op jit(solution)/shard_map/all_to_all | solution.py:115
  75.2 375.5 %all-gather.17.cloned.1.call-start = ((), (), s32[]{:S(2)}) async-start(), calls=%async_computation.9 | async-start | bytes 4866048 | tf_op jit(solution)/shard_map/all_gather | solution.py:87
  75.7 1152.3 %all-reduce.29.cloned.1.call-start = ((), (), s32[]{:S(2)}) async-start(), calls=%async_computation.10 | async-start | bytes 56623104
  296.5 15.2 %copy-start.9 = (bf16[1024,768]{1,0:T(8,128)(2,1)}, bf16[1024,768]{1,0:T(8,128)(2,1)S(1)}, u32[]{:S(2)}) copy-start(bf16[1024,768]{1,0:T(8,128)(2,1)S(1)} %gather_fusion.1) | copy-start | bytes 4718596
  307.5 4.2 copy-start.11
  307.5 4.2 copy-start.31
  318.5 78.5 %copy-start.15 = (bf16[1024,768]{0,1:T(8,128)(2,1)S(1)}, bf16[1024,768]{0,1:T(8,128)(2,1)}, u32[]{:S(2)}) copy-start(bf16[1024,768]{0,1:T(8,128)(2,1)} %copy.60) | copy-start | bytes 4718596
  318.5 78.5 %copy-start.30 = (f32[768]{0:T(1024)S(1)}, f32[768]{0:T(1024)}, u32[]{:S(2)}) copy-start(f32[768]{0:T(1024)} %convert_element_type.151) | copy-start | bytes 9220
  397.0 5.1 copy-start.13
  397.0 5.1 copy-start.16
  404.4 8.3 copy-start.28
  450.7 9.2 copy-start.29
  459.9 9.9 copy-start.5
  459.9 9.9 copy-start.22
  507.6 4.7 copy-start.3
  509.7 5.4 slice-start
  512.3 12.7 %slice-start.2 = ((s8[6291456]{0:T(1024)(128)(4,1)}), s8[4194304]{0:T(1024)(128)(4,1)S(1)}, s32[]{:S(2)}) async-start(s8[6291456]{0:T(1024)(128)(4,1)} %bitcast.191), calls=%async_computation.13 | async-start | bytes 8388608
  515.1 9.8 slice-start.3
  525.0 7.6 copy-start.18
  679.5 5.5 copy-start.7
  679.5 62.3 %copy-start.6 = (bf16[12,1024,64]{1,2,0:T(8,128)(2,1)}, bf16[12,1024,64]{1,2,0:T(8,128)(2,1)S(1)}, u32[]{:S(2)}) copy-start(bf16[12,1024,64]{1,2,0:T(8,128)(2,1)S(1)} %get-tuple-element.117) | copy-start | bytes 4718596
  693.0 3.4 copy-start.10
  733.0 58.8 %all-to-all-start.1 = ((bf16[32,32,768]{2,1,0:T(8,128)(2,1)}), bf16[32,32,768]{2,1,0:T(8,128)(2,1)S(1)}, u32[]{:S(2)}, u32[]{:S(2)}) async-start(bf16[32,32,768]{2,1,0:T(8,128)(2,1)} %bitcast.175), calls=%async_computation.1 | async-start | bytes 3145728 | tf_op jit(solution)/shard_map/all_to_all | solution.py:276
  737.0 3.3 copy-start.8
  791.8 10.7 copy-start.25
  791.8 10.7 copy-start.26
  791.8 10.7 copy-start.27
  791.8 89.8 %all-to-all-start.3 = ((bf16[32,32,768]{2,1,0:T(8,128)(2,1)}), bf16[32,32,768]{2,1,0:T(8,128)(2,1)S(1)}, u32[]{:S(2)}, u32[]{:S(2)}) async-start(bf16[32,32,768]{2,1,0:T(8,128)(2,1)} %bitcast.174), calls=%async_computation.3 | async-start | bytes 3145728 | tf_op jit(solution)/shard_map/all_to_all | solution.py:277
  881.6 355.9 %copy-start.1 = (bf16[1024,768]{1,0:T(8,128)(2,1)S(1)}, bf16[1024,768]{1,0:T(8,128)(2,1)}, u32[]{:S(2)}) copy-start(bf16[1024,768]{1,0:T(8,128)(2,1)} %param.24) | copy-start | bytes 4718596
  (10 other events, 22.5 us)
Sparse Core Ops, SparseCore 0:
  10.9 61.9 all-gather.6
  75.9 56.5 all-gather.8
  135.4 52.9 all-gather.10
  191.1 52.9 all-gather.12
  246.8 62.7 all-gather.14
  312.4 62.4 all-gather.16
  726.2 501.8 all-reduce.28
where the time goes:
time: 1260 us; the launch traced here: 1240 us
  waiting for transfers between devices  422 us (33%)
  local copies, waits for them, and re-layouts  304 us (24%)
  matrix products  301 us (24%)
  blocking collectives  126 us (10%)
  other arithmetic  56.6 us (4%)
  starting transfers between devices  19.1 us (2%)
  between operations  15.2 us (1%)
    unnamed x8, waiting for transfers between devices  345 us
    dot_general x102, matrix products, bf_dot(): return jnp.dot(left, right, preferred_element_type=jnp.float32)  301 us
    unnamed x2, blocking collectives  126 us
    scatter x1, local copies, waits for them, and re-layouts, on_device(): inverse = jnp.zeros((total_rows,), jnp.int32).at[packed_slot].set(jnp.ara...  120 us
    all_to_all x1, waiting for transfers between devices, on_device(): lax.all_to_all(back_out, 'fsdp', split_axis=0, concat_axis=0, tiled=True)  39.5 us
    all_to_all x1, waiting for transfers between devices, on_device(): lax.all_to_all(outgoing_cot, 'fsdp', split_axis=0, concat_axis=0, tiled=T...  37.1 us
    reshape x6, local copies, waits for them, and re-layouts, on_device(): piece.reshape(shape)  30.9 us
    unnamed x128, local copies, waits for them, and re-layouts  29.3 us
  transfers between devices with their start and end apart: 11, of which 3 were waited for; matrix products, arithmetic and copies ran while one was open for 30% of the time, Pallas kernels for 0%

commit v1 on v0

v1 whole, which is shorter than its diff:
```python
from functools import partial

import jax
import jax.numpy as jnp
from jax import lax
from jax.experimental import pallas as pl
from jax.experimental.pallas import tpu as pltpu
from jax.sharding import PartitionSpec as P

HD = 64
LANES = 128
EPSILON = 1e-12
NEG_LARGE = -1e30
MIB = 1 << 20
F32 = jnp.float32
BF16 = jnp.bfloat16
MESH = pl.DeviceIdType.MESH


def dot_nn(a, b):
    return lax.dot_general(a, b, (((1,), (0,)), ((), ())), preferred_element_type=F32)


def dot_nt(a, b):
    return lax.dot_general(a, b, (((1,), (1,)), ((), ())), preferred_element_type=F32)


def dot_tn(a, b):
    return lax.dot_general(a, b, (((0,), (0,)), ((), ())), preferred_element_type=F32)


def full_spec(shape, **kw):
    return pl.BlockSpec(shape, lambda *_: (0,) * len(shape), **kw)


def held_spec(shape):
    return full_spec(shape, pipeline_mode=pl.Buffered(1))


def params(mib, *axes, **kw):
    return pltpu.CompilerParams(
        dimension_semantics=axes or None, vmem_limit_bytes=mib * MIB, **kw
    )


def grid_of(devices):
    return {32: (4, 2, 2, 2), 128: (4, 4, 4, 2)}.get(devices, (devices, 1, 1, 1))


def gather_kernel(sizes, half, w4, wi, wu, vec, g4, gi, gu, gv, local_sem, sa, ra, sb, rb, sc, rc, sk, rk):
    na, nb, nc, nk = sizes
    me = lax.axis_index("fsdp")
    k = me % nk
    c = (me // nk) % nc
    b = (me // (nk * nc)) % nb
    a = me // (nk * nc * nb)

    def at(ja, jb, jc, jk=0):
        aa = (a + na - ja) % na
        bb = (b + nb - jb) % nb
        cc = (c + nc - jc) % nc
        kk = (k + nk - jk) % nk
        return ((aa * nb + bb) * nc + cc) * nk + kk

    rest = wu.shape[0] - half
    own = (w4, wi, wu.at[pl.ds(0, half)], wu.at[pl.ds(half, rest)], vec)

    def slot(dev):
        return (
            g4.at[:, dev],
            gi.at[dev],
            gu.at[dev, pl.ds(0, half)],
            gu.at[dev, pl.ds(half, rest)],
            gv.at[dev],
        )

    peers = [at(-j, 0, 0) for j in range(1, na)]
    peers += [at(0, -j, 0) for j in range(1, nb)]
    peers += [at(0, 0, -j) for j in range(1, nc)]
    peers += [at(0, 0, 0, -j) for j in range(1, nk)]
    barrier = pltpu.get_barrier_semaphore()
    for peer in peers:
        pl.semaphore_signal(barrier, inc=1, device_id=(peer,), device_id_type=MESH)
    pl.semaphore_wait(barrier, len(peers))

    started = []

    def send(source, target, send_sem, recv_sem, peer):
        copy = pltpu.make_async_remote_copy(
            src_ref=source, dst_ref=target, send_sem=send_sem, recv_sem=recv_sem,
            device_id=(peer,), device_id_type=MESH,
        )
        copy.start()
        started.append(copy)

    def arrive(piece, send_sem, recv_sem):
        pltpu.make_async_remote_copy(
            src_ref=piece, dst_ref=piece, send_sem=send_sem, recv_sem=recv_sem,
            device_id=(me,), device_id_type=MESH,
        ).wait_recv()

    mine = slot(me)
    local = []
    for p in range(5):
        for j in range(1, na):
            send(own[p], mine[p], sa.at[p, j], ra.at[p, j], at(-j, 0, 0))
    for p in range(5):
        copy = pltpu.make_async_copy(own[p], mine[p], local_sem.at[p])
        copy.start()
        local.append(copy)
    first = (0, 4, 2)
    second = (1, 3)

    def source_of(p, ja, jb, jc):
        if ja == 0 and jb == 0 and jc == 0:
            return own[p], mine[p]
        piece = slot(at(ja, jb, jc))[p]
        return piece, piece

    def to_b(p, ja, jc):
        source, target = source_of(p, ja, 0, jc)
        for j in range(1, nb):
            send(source, target, sb.at[p, ja, jc, j], rb.at[p, ja, jc, j], at(0, -j, 0))

    def to_c(p, ja, jb):
        source, target = source_of(p, ja, jb, 0)
        for j in range(1, nc):
            send(source, target, sc.at[p, ja, jb, j], rc.at[p, ja, jb, j], at(0, 0, -j))

    def to_k(p, ja, jb, jc):
        source, target = source_of(p, ja, jb, jc)
        for j in range(1, nk):
            send(source, target, sk.at[p, ja, jb, jc, j], rk.at[p, ja, jb, jc, j], at(0, 0, 0, -j))

    for ja in range(na):
        for p in first + second:
            if ja:
                arrive(slot(at(ja, 0, 0))[p], sa.at[p, ja], ra.at[p, ja])
            if p in first:
                to_b(p, ja, 0)
                to_c(p, ja, 0)
            else:
                to_c(p, ja, 0)
                to_b(p, ja, 0)
            to_k(p, ja, 0, 0)
    for ja in range(na):
        for p in first + second:
            if p in first:
                for j in range(1, nb):
                    arrive(slot(at(ja, j, 0))[p], sb.at[p, ja, 0, j], rb.at[p, ja, 0, j])
                    to_c(p, ja, j)
                    to_k(p, ja, j, 0)
            else:
                for j in range(1, nc):
                    arrive(slot(at(ja, 0, j))[p], sc.at[p, ja, 0, j], rc.at[p, ja, 0, j])
                    to_b(p, ja, j)
                    to_k(p, ja, 0, j)
    for ja in range(na):
        for p in first + second:
            if p in first:
                for j in range(nb):
                    for i in range(1, nc):
                        arrive(slot(at(ja, j, i))[p], sc.at[p, ja, j, i], rc.at[p, ja, j, i])
                        to_k(p, ja, j, i)
            else:
                for i in range(nc):
                    for j in range(1, nb):
                        arrive(slot(at(ja, j, i))[p], sb.at[p, ja, i, j], rb.at[p, ja, i, j])
                        to_k(p, ja, j, i)
    for ja in range(na):
        for jb in range(nb):
            for jc in range(nc):
                for p in first + second:
                    for j in range(1, nk):
                        arrive(
                            slot(at(ja, jb, jc, j))[p],
                            sk.at[p, ja, jb, jc, j],
                            rk.at[p, ja, jb, jc, j],
                        )
    for copy in local:
        copy.wait()
    for copy in started:
        copy.wait_send()


def gather_parameters(devices, w4, wi, wu, vec):
    sizes = grid_of(devices)
    na, nb, nc, nk = sizes
    rows = w4.shape[1]
    dma = pltpu.SemaphoreType.DMA
    anywhere = pl.BlockSpec(memory_space=pl.ANY)
    return pl.pallas_call(
        partial(gather_kernel, sizes, wu.shape[0] // 16 * 8),
        out_shape=(
            jax.ShapeDtypeStruct((4, devices) + w4.shape[1:], BF16),
            jax.ShapeDtypeStruct((devices,) + wi.shape, BF16),
            jax.ShapeDtypeStruct((devices,) + wu.shape, BF16),
            jax.ShapeDtypeStruct((devices,) + vec.shape, BF16),
        ),
        in_specs=[anywhere] * 4,
        out_specs=[anywhere] * 4,
        scratch_shapes=[dma((5,))]
        + [dma((5, na))] * 2
        + [dma((5, na, nc, nb))] * 2
        + [dma((5, na, nb, nc))] * 2
        + [dma((5, na, nb, nc, nk))] * 2,
        compiler_params=pltpu.CompilerParams(collective_id=1, has_side_effects=True),
    )(w4, wi, wu, vec)


def permute_kernel(tile, where_ref, rows_ref, out_ref):
    count = where_ref.shape[1]
    target = lax.broadcasted_iota(jnp.int32, (tile, count), 0) + pl.program_id(0) * tile
    chosen = jnp.where(where_ref[...] == target, 1.0, 0.0).astype(BF16)
    out_ref[...] = dot_nn(chosen, rows_ref[...]).astype(BF16)


def permute_rows(where_row, rows):
    count, width = rows.shape
    tile = count // 4
    return pl.pallas_call(
        partial(permute_kernel, tile),
        grid=(4,),
        out_shape=jax.ShapeDtypeStruct(rows.shape, BF16),
        in_specs=[full_spec((1, count)), full_spec((count, width))],
        out_specs=pl.BlockSpec((tile, width), lambda i: (i, 0)),
        compiler_params=params(32, "arbitrary"),
        name="permute_rows",
    )(where_row, rows)


def unpermute_kernel(from_ref, rows_ref, out_ref):
    tile, count = out_ref.shape[0], rows_ref.shape[0]
    lane = lax.broadcasted_iota(jnp.int32, (tile, count), 1)
    chosen = jnp.where(from_ref[...] == lane, 1.0, 0.0).astype(BF16)
    out_ref[...] = dot_nn(chosen, rows_ref[...]).astype(BF16)


def unpermute_rows(from_col, rows):
    count, width = rows.shape
    tile = count // 4
    return pl.pallas_call(
        unpermute_kernel,
        grid=(4,),
        out_shape=jax.ShapeDtypeStruct(rows.shape, BF16),
        in_specs=[pl.BlockSpec((tile, 1), lambda i: (i, 0)), full_spec((count, width))],
        out_specs=pl.BlockSpec((tile, width), lambda i: (i, 0)),
        compiler_params=params(32, "arbitrary"),
        name="unpermute_rows",
    )(from_col, rows)


LOW = 32


def source_kernel(slots_ref, out_ref):
    devices, count = slots_ref.shape
    high = out_ref.shape[0]

    def body(s, total):
        local = slots_ref[pl.ds(s, 1), :]
        in_high = lax.broadcasted_iota(jnp.int32, (high, count), 0) == (local >> 5)
        in_low = lax.broadcasted_iota(jnp.int32, (LOW, count), 0) == (local & (LOW - 1))
        weight = jnp.where(in_high, s.astype(F32), 0.0).astype(BF16)
        return total + dot_nt(weight, jnp.where(in_low, 1.0, 0.0).astype(BF16))

    out_ref[...] = lax.fori_loop(0, devices, body, jnp.zeros((high, LOW), F32))


def source_devices(local_slots, count):
    return pl.pallas_call(
        source_kernel,
        out_shape=jax.ShapeDtypeStruct((count // LOW, LOW), F32),
        in_specs=[pl.BlockSpec(memory_space=pltpu.VMEM)],
        out_specs=pl.BlockSpec(memory_space=pltpu.VMEM),
        name="source_devices",
    )(local_slots)


def project_kernel(place_ref, arrived_ref, wq_ref, wk_ref, wv_ref, vec_ref, rows_ref, q_ref, k_ref, v_ref):
    tile, count = rows_ref.shape[0], arrived_ref.shape[0]
    lane = lax.broadcasted_iota(jnp.int32, (tile, count), 1)
    chosen = jnp.where(place_ref[...] == lane, 1.0, 0.0).astype(BF16)
    rows = dot_nn(chosen, arrived_ref[...]).astype(BF16)
    rows_ref[...] = rows
    vec = vec_ref[...]
    q_ref[...] = ((dot_nn(rows, wq_ref[...]) + vec[0:1]).astype(BF16).astype(F32) * 0.125).astype(BF16)
    k_ref[...] = dot_nn(rows, wk_ref[...]).astype(BF16)
    v_ref[...] = (dot_nn(rows, wv_ref[...]) + vec[1:2]).astype(BF16)


def project(place_col, arrived, w4, vec):
    count, width = arrived.shape
    tile = count // 4
    row_spec = pl.BlockSpec((tile, width), lambda i: (i, 0))

    def weight(n):
        return pl.BlockSpec((pl.Squeezed(), width, width), lambda i: (n, 0, 0), pipeline_mode=pl.Buffered(1))

    return pl.pallas_call(
        project_kernel,
        grid=(4,),
        out_shape=[jax.ShapeDtypeStruct((count, width), BF16)] * 4,
        in_specs=[pl.BlockSpec((tile, 1), lambda i: (i, 0)), held_spec((count, width)),
                  weight(0), weight(1), weight(2), held_spec(vec.shape)],
        out_specs=[row_spec] * 4,
        compiler_params=params(40, "arbitrary"),
        cost_estimate=pl.CostEstimate(flops=8 * count * width * width, bytes_accessed=14 * MIB, transcendentals=0),
        name="project",
    )(place_col, arrived, w4, w4, w4, vec)


def split3(column):
    high = column.astype(BF16).astype(F32)
    rest = column - high
    mid = rest.astype(BF16).astype(F32)
    return high, mid, rest - mid


def feature_lanes(rows):
    lane = lax.broadcasted_iota(jnp.int32, (rows, LANES), 1)
    return lane < HD, lane & (HD - 1)


def key_features(lane, segment, segments):
    return jnp.where(lane == segment, 1.0, jnp.where((lane >= segments) & (lane < segments + 3), 1.0, 0.0))


def query_features(lane, segment, segments):
    return jnp.where((lane < segments) & (lane != segment), NEG_LARGE, 0.0)


def with_column(features, lane, start, column):
    high, mid, last = split3(column)
    features = jnp.where(lane == start, high, features)
    features = jnp.where(lane == start + 1, mid, features)
    return jnp.where(lane == start + 2, last, features)


def attend_kernel(segments, seg_ref, q_ref, seg_all_ref, k_ref, v_ref, out_ref, lse_ref, k0, k1):
    count, tile = k_ref.shape[0], q_ref.shape[0]
    first_all, lane_all = feature_lanes(count)

    @pl.when(pl.program_id(1) == 0)
    def _():
        extra = key_features(lane_all, seg_all_ref[...], segments).astype(BF16)
        k0[...] = jnp.where(first_all, k_ref[...], extra)
        k1[...] = jnp.where(first_all, extra, k_ref[...])

    first, lane = feature_lanes(tile)
    extra = query_features(lane, seg_ref[...], segments).astype(BF16)
    queries = q_ref[...]
    values = v_ref[...]
    outs, logs = [], []
    for mask, keys in ((first, k0), (~first, k1)):
        scores = dot_nt(jnp.where(mask, queries, extra), keys[...])
        top = jnp.max(scores, axis=1, keepdims=True)
        raised = jnp.exp(scores - top)
        total = jnp.sum(raised, axis=1, keepdims=True)
        outs.append(dot_nn(raised.astype(BF16), values) * (1.0 / total))
        logs.append(top + jnp.log(total))
    out_ref[...] = jnp.where(first, outs[0], outs[1]).astype(BF16)
    lse_ref[...] = jnp.where(first, logs[0], logs[1])


def attend(segments, segment_col, q, k, v):
    count, width = q.shape
    pairs = width // LANES
    tile = count // 4
    tile_spec = pl.BlockSpec((tile, LANES), lambda h, i: (i, h))
    all_spec = pl.BlockSpec((count, LANES), lambda h, i: (0, h))
    return pl.pallas_call(
        partial(attend_kernel, segments),
        grid=(pairs, 4),
        out_shape=[jax.ShapeDtypeStruct((count, width), BF16), jax.ShapeDtypeStruct((count, width), F32)],
        in_specs=[pl.BlockSpec((tile, 1), lambda h, i: (i, 0)), tile_spec, held_spec((count, 1)), all_spec, all_spec],
        out_specs=[tile_spec, tile_spec],
        scratch_shapes=[pltpu.VMEM((count, LANES), BF16)] * 2,
        compiler_params=params(40, "arbitrary", "arbitrary"),
        cost_estimate=pl.CostEstimate(flops=8 * count * count * width, bytes_accessed=10 * MIB, transcendentals=count * count * 12),
        name="attend",
    )(segment_col, q, segment_col, k, v)


def attend_back_kernel(segments, seg_ref, q_ref, o_ref, g_ref, lse_ref, seg_all_ref, k_ref, v_ref,
                       dq_ref, dk_ref, dv_ref, sums_ref, k0, k1, v0, v1, dk_sum, dv_sum):
    count, tile = k_ref.shape[0], q_ref.shape[0]
    first_all, lane_all = feature_lanes(count)
    step, last = pl.program_id(1), pl.num_programs(1) - 1

    @pl.when(step == 0)
    def _():
        extra = key_features(lane_all, seg_all_ref[...], segments).astype(BF16)
        k0[...] = jnp.where(first_all, k_ref[...], extra)
        k1[...] = jnp.where(first_all, extra, k_ref[...])
        v0[...] = jnp.where(first_all, v_ref[...], extra)
        v1[...] = jnp.where(first_all, extra, v_ref[...])
        dk_sum[...] = jnp.zeros_like(dk_sum)
        dv_sum[...] = jnp.zeros_like(dv_sum)
        sums_ref[...] = jnp.zeros_like(sums_ref)

    first, lane = feature_lanes(tile)
    hidden = query_features(lane, seg_ref[...], segments)
    queries, grads = q_ref[...], g_ref[...]
    product = grads.astype(F32) * o_ref[...].astype(F32)
    lses = lse_ref[...]
    dqs, dks, dvs = [], [], []
    for mask, keys, values, at in ((first, k0, v0, 0), (~first, k1, v1, HD)):
        lse = lses[:, at:at + 1]
        delta = jnp.sum(jnp.where(mask, product, 0.0), axis=1, keepdims=True)
        query = jnp.where(mask, queries, with_column(hidden, lane, segments, -lse).astype(BF16))
        grad = jnp.where(mask, grads, with_column(jnp.zeros_like(hidden), lane, segments, -delta).astype(BF16))
        probs = jnp.exp(dot_nt(keys[...], query))
        score = (probs * dot_nt(values[...], grad)).astype(BF16)
        dvs.append(dot_nn(probs.astype(BF16), grad))
        dks.append(dot_nn(score, query))
        dqs.append(dot_tn(score, keys[...]))
    dq = (jnp.where(first, dqs[0], dqs[1]) * 0.125).astype(BF16)
    dq_ref[...] = dq
    dk_sum[...] += jnp.where(first_all, dks[0], dks[1])
    dv_sum[...] += jnp.where(first_all, dvs[0], dvs[1])
    sums_ref[0:1, :] += jnp.sum(dq.astype(F32), axis=0, keepdims=True)

    @pl.when(step == last)
    def _():
        dk_ref[...] = dk_sum[...].astype(BF16)
        dv = dv_sum[...].astype(BF16)
        dv_ref[...] = dv
        sums_ref[1:2, :] += jnp.sum(dv.astype(F32), axis=0, keepdims=True)


def attend_back(segments, segment_col, q, out, grad, lse, k, v):
    count, width = q.shape
    pairs = width // LANES
    tile = count // 4
    tile_spec = pl.BlockSpec((tile, LANES), lambda h, i: (i, h))
    all_spec = pl.BlockSpec((count, LANES), lambda h, i: (0, h))
    return pl.pallas_call(
        partial(attend_back_kernel, segments),
        grid=(pairs, 4),
        out_shape=[jax.ShapeDtypeStruct((count, width), BF16)] * 3 + [jax.ShapeDtypeStruct((8, width), F32)],
        in_specs=[pl.BlockSpec((tile, 1), lambda h, i: (i, 0))] + [tile_spec] * 4 + [held_spec((count, 1)), all_spec, all_spec],
        out_specs=[tile_spec, all_spec, all_spec, pl.BlockSpec((8, LANES), lambda h, i: (0, h))],
        scratch_shapes=[pltpu.VMEM((count, LANES), BF16)] * 4 + [pltpu.VMEM((count, LANES), F32)] * 2,
        compiler_params=params(48, "arbitrary", "arbitrary"),
        cost_estimate=pl.CostEstimate(flops=20 * count * count * width, bytes_accessed=16 * MIB, transcendentals=count * count * 12),
        name="attend_back",
    )(segment_col, q, out, grad, lse, segment_col, k, v)


def normalize(hidden):
    centered = hidden - jnp.mean(hidden, axis=1, keepdims=True)
    variance = jnp.mean(centered * centered, axis=1, keepdims=True)
    inverse = lax.rsqrt(variance + EPSILON)
    return centered * inverse, inverse


def normalize_back(grad, normal, inverse):
    return inverse * (
        grad
        - jnp.mean(grad, axis=1, keepdims=True)
        - normal * jnp.mean(grad * normal, axis=1, keepdims=True)
    )


def column_sum(matrix):
    return jnp.sum(matrix.astype(F32), axis=0, keepdims=True)


def feed_kernel(chunk, place_ref, rows_ref, att_ref, cot_ref, wo_ref, wi_ref, wu_ref, vec_ref, bi_ref,
                out_ref, act_ref, inner_ref, normed_ref, outer_ref, low_ref, first_ref, agrad_ref,
                sums_ref, bisum_ref, slope_ref):
    tile, count = rows_ref.shape[0], cot_ref.shape[0]
    hidden_width = wi_ref.shape[1]
    step = pl.program_id(0)

    @pl.when(step == 0)
    def _():
        sums_ref[...] = jnp.zeros_like(sums_ref)
        bisum_ref[...] = jnp.zeros_like(bisum_ref)

    vec = vec_ref[...]
    bo, ga, sa, bu, gf, sf = (vec[i:i + 1] for i in range(2, 8))
    first_sum = rows_ref[...].astype(F32) + dot_nn(att_ref[...], wo_ref[...]) + bo
    normal1, inverse1 = normalize(first_sum)
    normed = normal1 * ga + sa
    normed_low = normed.astype(BF16)
    normed_ref[...] = normed_low
    second = normed + bu
    for at in range(0, hidden_width, chunk):
        pre = dot_nn(normed_low, wi_ref[:, at:at + chunk]) + bi_ref[:, at:at + chunk]
        share = 0.5 + 0.5 * lax.erf(pre * 0.7071067811865476)
        act = (pre * share).astype(BF16)
        act_ref[:, at:at + chunk] = act
        slope_ref[:, at:at + chunk] = share + pre * (jnp.exp(pre * pre * -0.5) * 0.3989422804014327)
        second = second + dot_nn(act, wu_ref[at:at + chunk, :])
    normal2, inverse2 = normalize(second)
    out_ref[...] = (normal2 * gf + sf).astype(BF16)
    lane = lax.broadcasted_iota(jnp.int32, (tile, count), 1)
    chosen = jnp.where(place_ref[...] == lane, 1.0, 0.0).astype(BF16)
    cot = dot_nn(chosen, cot_ref[...])
    second_grad = normalize_back(cot * gf, normal2, inverse2)
    outer_low = second_grad.astype(BF16)
    outer_ref[...] = outer_low
    normed_grad = second_grad
    for at in range(0, hidden_width, chunk):
        act_grad = dot_nt(outer_low, wu_ref[at:at + chunk, :])
        inner_low = (act_grad * slope_ref[:, at:at + chunk]).astype(BF16)
        inner_ref[:, at:at + chunk] = inner_low
        bisum_ref[0:1, at:at + chunk] += column_sum(inner_low)
        normed_grad = normed_grad + dot_nt(inner_low, wi_ref[:, at:at + chunk])
    first_grad = normalize_back(normed_grad * ga, normal1, inverse1)
    first_ref[...] = first_grad
    branch_low = first_grad.astype(BF16)
    low_ref[...] = branch_low
    agrad_ref[...] = dot_nt(branch_low, wo_ref[...]).astype(BF16)
    sums_ref[2:3, :] += column_sum(branch_low)
    sums_ref[3:4, :] += column_sum(normed_grad * normal1)
    sums_ref[4:5, :] += column_sum(normed_grad)
    sums_ref[5:6, :] += column_sum(outer_low)
    sums_ref[6:7, :] += column_sum(cot * normal2)
    sums_ref[7:8, :] += column_sum(cot)


def feed_forward(place_col, rows, attended, arrived_cot, w4, wi, wu, vec, bi):
    count, width = rows.shape
    hidden_width = wi.shape[1]
    tile = count // 4
    row_spec = pl.BlockSpec((tile, width), lambda i: (i, 0))
    wide_spec = pl.BlockSpec((tile, hidden_width), lambda i: (i, 0))

    def rows_of(n, dtype):
        return jax.ShapeDtypeStruct((count, n), dtype)

    return pl.pallas_call(
        partial(feed_kernel, 512),
        grid=(4,),
        out_shape=[
            rows_of(width, BF16), rows_of(hidden_width, BF16), rows_of(hidden_width, BF16), rows_of(width, BF16),
            rows_of(width, BF16), rows_of(width, BF16), rows_of(width, F32), rows_of(width, BF16),
            jax.ShapeDtypeStruct((8, width), F32), jax.ShapeDtypeStruct((8, hidden_width), F32),
        ],
        in_specs=[
            pl.BlockSpec((tile, 1), lambda i: (i, 0)), row_spec, row_spec, held_spec((count, width)),
            pl.BlockSpec((pl.Squeezed(), width, width), lambda i: (3, 0, 0), pipeline_mode=pl.Buffered(1)),
            held_spec(wi.shape), held_spec(wu.shape), held_spec(vec.shape), held_spec(bi.shape),
        ],
        out_specs=[row_spec, wide_spec, wide_spec] + [row_spec] * 5
        + [full_spec((8, width)), full_spec((8, hidden_width))],
        scratch_shapes=[pltpu.VMEM((tile, hidden_width), F32)],
        compiler_params=params(56, "arbitrary"),
        cost_estimate=pl.CostEstimate(flops=12 * count * width * hidden_width, bytes_accessed=36 * MIB, transcendentals=2 * count * hidden_width),
        name="feed_forward",
    )(place_col, rows, attended, arrived_cot, w4, wi, wu, vec, bi)


def rows_grad_kernel(tile, where_ref, first_ref, dq_ref, dk_ref, dv_ref, wq_ref, wk_ref, wv_ref, out_ref, total_ref):
    step = pl.program_id(0)
    tiles = total_ref.shape[0] // tile

    @pl.when(step < tiles)
    def _():
        total = (
            first_ref[...]
            + dot_nt(dq_ref[...], wq_ref[...])
            + dot_nt(dk_ref[...], wk_ref[...])
            + dot_nt(dv_ref[...], wv_ref[...])
        )
        total_ref[pl.ds(pl.multiple_of(step * tile, tile), tile), :] = total.astype(BF16)

    @pl.when(step >= tiles)
    def _():
        count = where_ref.shape[1]
        target = lax.broadcasted_iota(jnp.int32, (tile, count), 0) + (step - tiles) * tile
        chosen = jnp.where(where_ref[...] == target, 1.0, 0.0).astype(BF16)
        out_ref[...] = dot_nn(chosen, total_ref[...]).astype(BF16)


def rows_grad(where_row, first_grad, dq, dk, dv, w4):
    count, width = dq.shape
    tiles = 4
    tile = count // tiles
    row_spec = pl.BlockSpec((tile, width), lambda i: (jnp.minimum(i, tiles - 1), 0))

    def weight(n):
        return pl.BlockSpec((pl.Squeezed(), width, width), lambda i: (n, 0, 0), pipeline_mode=pl.Buffered(1))

    return pl.pallas_call(
        partial(rows_grad_kernel, tile),
        grid=(2 * tiles,),
        out_shape=jax.ShapeDtypeStruct((count, width), BF16),
        in_specs=[held_spec((1, count)), row_spec, row_spec, row_spec, row_spec, weight(0), weight(1), weight(2)],
        out_specs=pl.BlockSpec((tile, width), lambda i: (jnp.maximum(i - tiles, 0), 0)),
        scratch_shapes=[pltpu.VMEM((count, width), BF16)],
        compiler_params=params(40, "arbitrary"),
        name="rows_grad",
    )(where_row, first_grad, dq, dk, dv, w4, w4, w4)


def scatter_sum(pieces):
    return lax.psum_scatter(pieces, "fsdp", scatter_dimension=0, tiled=True)


def on_device(tokens, cotangent, packed_slot, seq_lengths, query_weight, query_bias, key_weight, value_weight,
              value_bias, output_weight, output_bias, attention_gain, attention_shift, inner_weight, inner_bias,
              outer_weight, outer_bias, final_gain, final_shift):
    devices = lax.axis_size("fsdp")
    me = lax.axis_index("fsdp")
    count, width = tokens.shape
    hidden_width = inner_bias.shape[0] * devices
    peer_rows = count // devices
    segments = seq_lengths.shape[1]
    share = width // devices
    counting = jnp.arange(count, dtype=jnp.int32)

    def exchange(rows):
        pieces = rows.reshape(devices, peer_rows, width)
        return lax.all_to_all(pieces, "fsdp", split_axis=0, concat_axis=0, tiled=True).reshape(count, width)

    own_slots = lax.dynamic_slice_in_dim(packed_slot, me * count, count)
    rank = jnp.sum((own_slots[None, :] < own_slots[:, None]).astype(jnp.int32), axis=1)
    rank_row, rank_col = rank.reshape(1, count), rank.reshape(count, 1)
    arrived = exchange(permute_rows(rank_row, tokens))
    arrived_cot = exchange(permute_rows(rank_row, cotangent))

    w4 = jnp.stack([w.reshape(share, width) for w in (query_weight, key_weight, value_weight, output_weight)])
    small = (query_bias, value_bias, output_bias, attention_gain, attention_shift, outer_bias, final_gain, final_shift)
    vec = jnp.concatenate(small + (inner_bias,))
    used = vec.shape[0]
    vec = jnp.pad(vec, (0, 8 * LANES - used)).reshape(8, LANES)
    g4, gi, gu, gv = gather_parameters(
        devices, w4, inner_weight.reshape(share, hidden_width), outer_weight.reshape(hidden_width // devices, width), vec
    )
    w4 = g4.reshape(4, width, width)
    wi = gi.reshape(width, hidden_width)
    wu = gu.reshape(hidden_width, width)
    flat = gv.reshape(devices, 8 * LANES).astype(F32)
    vec = flat[:, : 8 * share].reshape(devices, 8, share).transpose(1, 0, 2).reshape(8, width)
    bi = flat[:, 8 * share : used].reshape(1, hidden_width)

    local_slots = packed_slot.reshape(devices, count) - me * count
    source = source_devices(local_slots, count).astype(jnp.int32).reshape(count)
    same = (source[:, None] == source[None, :]) & (counting[None, :] < counting[:, None])
    place = source * peer_rows + jnp.sum(same.astype(jnp.int32), axis=1)
    place_row, place_col = place.reshape(1, count), place.reshape(count, 1)
    ends = jnp.cumsum(seq_lengths[0], dtype=jnp.int32)
    segment = jnp.sum((counting[:, None] >= ends[None, :]).astype(jnp.int32), axis=1)
    segment_col = segment.reshape(count, 1)

    rows, q, k, v = project(place_col, arrived, w4, vec)
    attended, lse = attend(segments, segment_col, q, k, v)
    (result, activated, inner_low, normed_low, outer_low, branch_low, first_grad, attended_grad, sums, bi_sum) = feed_forward(
        place_col, rows, attended, arrived_cot, w4, wi, wu, vec, bi
    )
    layer_out = unpermute_rows(rank_col, exchange(permute_rows(place_row, result)))

    def weight_grad(left, right):
        return dot_tn(left, right).astype(BF16)

    def pieces_of(grad):
        return grad.reshape(devices, -1, grad.shape[-1])

    inner_grad = scatter_sum(pieces_of(weight_grad(normed_low, inner_low)))
    outer_grad = scatter_sum(pieces_of(weight_grad(activated, outer_low)))
    wo_grad = weight_grad(attended, branch_low)

    dq, dk, dv, more = attend_back(segments, segment_col, q, attended, attended_grad, lse, k, v)
    tokens_grad = unpermute_rows(rank_col, exchange(rows_grad(place_row, first_grad, dq, dk, dv, w4)))
    sums = sums + more
    sums = sums.reshape(8, devices, share).transpose(1, 0, 2).reshape(devices, 8 * share)
    sums = jnp.concatenate([sums, bi_sum[0].reshape(devices, hidden_width // devices)], axis=1)
    sums = jnp.pad(sums, ((0, 0), (0, width - used))).reshape(devices, 1, width).astype(BF16)
    late = jnp.concatenate(
        [pieces_of(weight_grad(rows, dq)), pieces_of(weight_grad(rows, dk)), pieces_of(weight_grad(rows, dv)),
         pieces_of(wo_grad), sums],
        axis=1,
    )
    late = scatter_sum(late)[0].astype(F32)
    wq_grad, wk_grad, wv_grad, wo_grad = (late[i * share:(i + 1) * share].reshape(-1) for i in range(4))
    sums = late[4 * share]
    small = [sums[i * share:(i + 1) * share] for i in range(8)]
    return (
        layer_out, tokens_grad, wq_grad, small[0], wk_grad, wv_grad, small[1], wo_grad, small[2], small[3], small[4],
        inner_grad.astype(F32).reshape(-1), sums[8 * share:used], outer_grad.astype(F32).reshape(-1), small[5], small[6], small[7],
    )


def solution(mesh):
    split, rows = P("fsdp"), P("fsdp", None)
    return jax.shard_map(
        on_device,
        mesh=mesh,
        in_specs=(rows, rows, P(), rows) + (split,) * 15,
        out_specs=(rows, rows) + (split,) * 15,
        check_vma=False,
    )
```

time: 1260 us -> 658 us (0.52); the launches traced: 1240 us -> 656 us
  Pallas kernels: 0 us -> 278 us
  matrix products: 301 us -> 26.5 us
  local copies, waits for them, and re-layouts: 304 us -> 48.9 us
  waiting for transfers between devices: 422 us -> 256 us
  blocking collectives: 126 us -> 0 us
  other arithmetic: 56.6 us -> 5.45 us
    unnamed x8 -> x3, waiting for transfers between devices: 345 us -> 0.05 us
    pallas_call x0 -> x12, Pallas kernels: none -> 278 us  [the longest x1 117 us: gather_parameters(): pl.pallas_call(partial(gather_kernel, sizes, wu.shape[0] // 16 * 8), out_...]
    dot_general x102 -> x6, matrix products: 301 us -> 26.5 us  [dot_tn(): lax.dot_general(a, b, (((0,), (0,)), ((), ())), preferred_element_type=F32)]
    reduce_scatter x0 -> x3, waiting for transfers between devices: none -> 142 us  [scatter_sum(): return lax.psum_scatter(pieces, 'fsdp', scatter_dimension=0, tiled=True)]
    scatter x3 -> x0, local copies, waits for them, and re-layouts: 129 us -> none  [the longest x1 120 us: on_device(): inverse = jnp.zeros((total_rows,), jnp.int32).at[packed_slot].set(jnp.ara...]
    unnamed x2 -> x0, blocking collectives: 126 us -> none
    reshape x15, local copies, waits for them, and re-layouts: 68.5 us -> 8.88 us  [the longest x4 2.55 us: on_device(): late[i * share:(i + 1) * share].reshape(-1)]
    gather x10 -> x0, local copies, waits for them, and re-layouts: 44.9 us -> none  [the longest x2 8.02 us: on_device(): packed_cot = arrived_cot.reshape(tok_rows, model_width)[place_index]]
  transfers between devices with their start and end apart: 11 -> 7, of which waited for: 3 -> 5; matrix products, arithmetic and copies ran while one was open for 30% -> 6% of each run, Pallas kernels for 0% -> 35%
where the time goes in v1:
time: 658 us; the launch traced here: 656 us
  Pallas kernels  278 us (42%)
  waiting for transfers between devices  256 us (39%)
  local copies, waits for them, and re-layouts  48.9 us (7%)
  starting transfers between devices  27.5 us (4%)
  matrix products  26.5 us (4%)
  between operations  14.4 us (2%)
    reduce_scatter x3, waiting for transfers between devices, scatter_sum(): return lax.psum_scatter(pieces, 'fsdp', scatter_dimension=0, tiled=True)  142 us
    pallas_call x1, Pallas kernels, gather_parameters(): pl.pallas_call(partial(gather_kernel, sizes, wu.shape[0] // 16 * 8), out_...  117 us
    all_to_all x4, waiting for transfers between devices, exchange(): lax.all_to_all(pieces, 'fsdp', split_axis=0, concat_axis=0, tiled=True)  114 us
    pallas_call x1, Pallas kernels, attend_back(): pl.pallas_call(partial(attend_back_kernel, segments), grid=(pairs, 4), ou...  48.9 us
    pallas_call x1, Pallas kernels, feed_forward(): pl.pallas_call(partial(feed_kernel, 512), grid=(4,), out_shape=[rows_of(w...  42 us
    unnamed x100, local copies, waits for them, and re-layouts  33.8 us
    pallas_call x1, Pallas kernels, attend(): pl.pallas_call(partial(attend_kernel, segments), grid=(pairs, 4), out_sha...  31.3 us
    all_to_all x4, starting transfers between devices, exchange(): lax.all_to_all(pieces, 'fsdp', split_axis=0, concat_axis=0, tiled=True)  27.4 us
  transfers between devices with their start and end apart: 7, of which 5 were waited for; matrix products, arithmetic and copies ran while one was open for 6% of the time, Pallas kernels for 35%

profile of v1, /device:TPU:0, one launch (start us, length us, event | category | flops | bytes accessed | tf_op | source)
XLA Modules:
  0.0 656.2 jit_solution(16393143420499403034)
XLA Ops:
  8.5 1.4 copy-done.12
  9.9 3.2 permute_rows.3
  13.1 7.3 %all-to-all-start = ((bf16[32,32,768]{2,1,0:T(8,128)(2,1)}), bf16[32,32,768]{2,1,0:T(8,128)(2,1)S(1)}, u32[]{:S(2)}, u32[]{:S(2)}) async-start(bf16[32,32,768]{2,1,0:T(8,128)(2,1)} %bitcast.4), calls=%async_computation | async-start | bytes 3145728 | tf_op jit(solution)/shard_map/all_to_all | solution.py:618
  20.4 3.3 permute_rows.4
  23.7 34.4 %all-to-all-done = bf16[32,32,768]{2,1,0:T(8,128)(2,1)S(1)} async-done(((bf16[32,32,768]{2,1,0:T(8,128)(2,1)}), bf16[32,32,768]{2,1,0:T(8,128)(2,1)S(1)}, u32[]{:S(2)}, u32[]{:S(2)}) %all-to-all-start) | async-done | bytes 1572896 | tf_op jit(solution)/shard_map/all_to_all | solution.py:618
  58.3 3.9 all-to-all-start.1
  65.5 117.3 %shard_map.314 = (bf16[4,32,24,768]{3,2,1,0:T(8,128)(2,1)}, bf16[32,24,3072]{2,1,0:T(8,128)(2,1)}, bf16[32,96,768]{2,1,0:T(8,128)(2,1)}, bf16[32,8,128]{2,1,0:T(8,128)(2,1)}) custom-call(bf16[4,24,768]{2,1,0:T(8,128)(2,1)} %pad_maximum_fusion.w4, bf16[24,3072]{1,0:T(8,128)(2,1)} %reshape.243.wi, bf16[96,768]{1,0:T(8,128)(2,1)} %reshape.244.wu, ...), custom_call_target="tpu_custom_call" | custom-call | tf_op jit(solution)/shard_map/pallas_call | solution.py:192
  184.5 6.5 source_devices.1
  194.9 2.3 copy-done
  197.3 6.9 %project.1 = (bf16[1024,768]{1,0:T(8,128)(2,1)S(1)}, bf16[1024,768]{1,0:T(8,128)(2,1)S(1)}, bf16[1024,768]{1,0:T(8,128)(2,1)S(1)}, bf16[1024,768]{1,0:T(8,128)(2,1)S(1)}) custom-call(s32[1024,1]{1,0:T(8,128)S(1)} %copy.64.place_ref, bf16[1024,768]{1,0:T(8,128)(2,1)S(1)} %bitcast.79, bf16[4,768,768]{2,1,0:T(8,128)(2,1)S(1)} %bitcast.71, ...), custom_call_target="tpu_custom_call" | custom-call | flops 4831838208 | bytes 14680064 | tf_op jit(solution)/shard_map/project/pallas_call | solution.py:300
  204.2 1.1 copy-done.19
  205.3 31.3 %attend.1 = (bf16[1024,768]{1,0:T(8,128)(2,1)S(1)}, f32[1024,768]{1,0:T(8,128)S(1)}) custom-call(s32[1024,1]{1,0:T(8,128)S(1)} %copy.62.seg_ref.seg_all_ref, bf16[1024,768]{1,0:T(8,128)(2,1)S(1)} %get-tuple-element.44.q_ref, s32[1024,1]{1,0:T(8,128)S(1)} %copy.62.seg_ref.seg_all_ref, bf16[1024,768]{1,0:T(8,128)(2,1)S(1)} %get-tuple-element.45.k_ref, ...), custom_call_target="tpu_custom_call" | custom-call | flops 6442450944 | bytes 10485760 | tf_op jit(solution)/shard_map/attend/pallas_call | solution.py:372
  236.6 1.2 copy-done.21
  237.8 1.2 copy-done.22
  239.0 1.1 copy-done.23
  240.1 1.1 copy-done.24
  241.3 1.6 copy-done.26
  242.9 42.0 %feed_forward.1 = (bf16[1024,768]{1,0:T(8,128)(2,1)}, bf16[1024,3072]{1,0:T(8,128)(2,1)}, bf16[1024,3072]{1,0:T(8,128)(2,1)}, bf16[1024,768]{1,0:T(8,128)(2,1)},...) custom-call(s32[1024,1]{1,0:T(8,128)} %copy-done.17, ...), custom_call_target="tpu_custom_call" | custom-call | flops 28991029248 | bytes 37748736 | tf_op jit(solution)/shard_map/feed_forward/pallas_call | solution.py:535
  284.9 9.4 %convolution_convert_fusion.1 = bf16[768,3072]{1,0:T(8,128)(2,1)} fusion(bf16[1024,768]{1,0:T(8,128)(2,1)} %get-tuple-element.61, bf16[1024,3072]{1,0:T(8,128)(2,1)} %get-tuple-element.62), kind=kOutput, calls=%fused_computation.1 | convolution fusion | flops 4834197504 | bytes 12582912 | tf_op jit(solution)/shard_map/dot_general | solution.py:29
  294.4 1.3 copy-done.46
  295.7 9.8 %convolution_convert_fusion = bf16[3072,768]{1,0:T(8,128)(2,1)} fusion(bf16[1024,3072]{1,0:T(8,128)(2,1)} %get-tuple-element.63, bf16[1024,768]{1,0:T(8,128)(2,1)S(1)} %copy-done.46), kind=kOutput, calls=%fused_computation | convolution fusion | flops 4834197504 | bytes 12582912 | tf_op jit(solution)/shard_map/dot_general | solution.py:29
  306.7 48.9 %attend_back.1 = (bf16[1024,768]{1,0:T(8,128)(2,1)S(1)}, bf16[1024,768]{1,0:T(8,128)(2,1)S(1)}, bf16[1024,768]{1,0:T(8,128)(2,1)S(1)}, f32[8,768]{1,0:T(8,128)S(1)}) custom-call(s32[1024,1]{1,0:T(8,128)S(1)} %copy-done.16, bf16[1024,768]{1,0:T(8,128)(2,1)} %copy-done.21, bf16[1024,768]{1,0:T(8,128)(2,1)} %copy-done.24, ...), custom_call_target="tpu_custom_call" | custom-call | flops 16106127360 | bytes 16777216 | tf_op jit(solution)/shard_map/attend_back/pallas_call | solution.py:438
  355.6 1.2 copy-done.9
  357.1 1.1 fusion.5
  358.3 2.9 convolution_convert_fusion.5
  361.2 1.1 constant_dynamic-update-slice_fusion.3
  363.0 1.4 convolution_convert_fusion.4
  364.5 1.1 constant_dynamic-update-slice_fusion.2
  366.4 1.4 convolution_convert_fusion.3
  367.8 1.1 constant_dynamic-update-slice_fusion.1
  369.6 1.4 convolution_convert_fusion.2
  371.1 1.1 constant_dynamic-update-slice_fusion
  373.1 1.8 copy-done.4
  374.9 2.6 copy-done.1
  377.5 1.4 copy-done.6
  378.9 1.4 copy-done.8
  380.3 1.4 copy-done.11
  381.7 7.9 %rows_grad.1 = bf16[1024,768]{1,0:T(8,128)(2,1)} custom-call(s32[1,1024]{1,0:T(1,128)S(1)} %add.36.where_ref, f32[1024,768]{1,0:T(8,128)S(1)} %copy-done.4, bf16[1024,768]{1,0:T(8,128)(2,1)S(1)} %copy-done.6, bf16[1024,768]{1,0:T(8,128)(2,1)S(1)} %copy-done.8, bf16[1024,768]{1,0:T(8,128)(2,1)S(1)} %copy-done.11, bf16[4,768,768]{2,1,0:T(8,128)(2,1)S(1)} %bitcast.74, ...), custom_call_target="tpu_custom_call" | custom-call | tf_op jit(solution)/shard_map/rows_grad/pallas_call | solution.py:588
  389.6 12.2 %all-to-all-start.3 = ((bf16[32,32,768]{2,1,0:T(8,128)(2,1)}), bf16[32,32,768]{2,1,0:T(8,128)(2,1)S(1)}, u32[]{:S(2)}, u32[]{:S(2)}) async-start(bf16[32,32,768]{2,1,0:T(8,128)(2,1)} %bitcast.18), calls=%async_computation.3 | async-start | bytes 3145728 | tf_op jit(solution)/shard_map/all_to_all | solution.py:618
  401.8 3.3 permute_rows.5
  405.1 35.2 %all-to-all-done.3 = bf16[32,32,768]{2,1,0:T(8,128)(2,1)S(1)} async-done(((bf16[32,32,768]{2,1,0:T(8,128)(2,1)}), bf16[32,32,768]{2,1,0:T(8,128)(2,1)S(1)}, u32[]{:S(2)}, u32[]{:S(2)}) %all-to-all-start.3) | async-done | bytes 1572896 | tf_op jit(solution)/shard_map/all_to_all | solution.py:618
  440.3 4.0 all-to-all-start.2
  446.3 3.5 unpermute_rows.3
  449.8 44.8 %all-to-all-done.2 = bf16[32,32,768]{2,1,0:T(8,128)(2,1)S(1)} async-done(((bf16[32,32,768]{2,1,0:T(8,128)(2,1)}), bf16[32,32,768]{2,1,0:T(8,128)(2,1)S(1)}, u32[]{:S(2)}, u32[]{:S(2)}) %all-to-all-start.2) | async-done | bytes 1572896 | tf_op jit(solution)/shard_map/all_to_all | solution.py:618
  495.7 3.5 unpermute_rows.2
  500.9 29.6 %reduce-scatter.8.cloned.1.call-done = bf16[1,96,768]{2,1,0:T(8,128)(2,1)} async-done(((bf16[32,96,768]{2,1,0:T(8,128)(2,1)}), bf16[1,96,768]{2,1,0:T(8,128)(2,1)}) %reduce-scatter.8.cloned.1.call-update) | async-done | bytes 147472 | tf_op jit(solution)/shard_map/reduce_scatter | solution.py:601
  530.4 1.8 reshape.281
  532.2 112.0 %reduce-scatter.4.cloned.1.call-done = bf16[1,97,768]{2,1,0:T(8,128)(2,1)} async-done(((bf16[32,97,768]{2,1,0:T(8,128)(2,1)}), bf16[1,97,768]{2,1,0:T(8,128)(2,1)}) %reduce-scatter.4.cloned.1.call-update) | async-done | bytes 149008 | tf_op jit(solution)/shard_map/reduce_scatter | solution.py:601
  (137 shorter events, 24.9 us)
Async XLA Ops:
  8.5 1.4 copy-start.12
  13.1 7.3 %copy-start.13 = (bf16[1024,768]{1,0:T(8,128)(2,1)S(1)}, bf16[1024,768]{1,0:T(8,128)(2,1)}, u32[]{:S(2)}) copy-start(bf16[1024,768]{1,0:T(8,128)(2,1)} %rows_ref.3) | copy-start | bytes 4718596
  13.1 45.0 %all-to-all-start = ((bf16[32,32,768]{2,1,0:T(8,128)(2,1)}), bf16[32,32,768]{2,1,0:T(8,128)(2,1)S(1)}, u32[]{:S(2)}, u32[]{:S(2)}) async-start(bf16[32,32,768]{2,1,0:T(8,128)(2,1)} %bitcast.4), calls=%async_computation | async-start | bytes 3145728 | tf_op jit(solution)/shard_map/all_to_all | solution.py:618
  58.1 4.1 copy-start.30
  58.2 4.2 copy-start.31
  58.2 4.2 copy-start.32
  58.2 4.3 copy-start.33
  58.2 4.4 copy-start.27
  58.2 5.1 copy-start.28
  58.2 5.9 copy-start.35
  58.2 5.9 copy-start.36
  58.2 5.9 copy-start.37
  58.2 5.9 copy-start.38
  58.2 5.9 copy-start.39
  58.2 5.9 copy-start.40
  58.3 5.9 copy-start.41
  58.3 5.9 copy-start.42
  58.3 5.9 copy-start.43
  58.3 184.6 %all-to-all-start.1 = ((bf16[32,32,768]{2,1,0:T(8,128)(2,1)}), bf16[32,32,768]{2,1,0:T(8,128)(2,1)}, u32[]{:S(2)}, u32[]{:S(2)}) async-start(bf16[32,32,768]{2,1,0:T(8,128)(2,1)} %bitcast.12), calls=%async_computation.1 | async-start | bytes 3145728 | tf_op jit(solution)/shard_map/all_to_all | solution.py:618
  62.2 121.6 %copy-start.29 = (s32[32768]{0:T(1024)S(1)}, s32[32768]{0:T(1024)}, u32[]{:S(2)}) copy-start(s32[32768]{0:T(1024)} %param.21) | copy-start | bytes 393220
  62.2 437.0 %reduce-scatter.6.cloned.1.call-start = ((), (), s32[]{:S(2)}) async-start(), calls=%async_computation.8 | async-start | bytes 4866048 | tf_op jit(solution)/shard_map/reduce_scatter | solution.py:601
  63.3 130.4 %copy-start.44 = (s32[1,4]{1,0:T(1,128)S(1)}, s32[1,4]{1,0:T(1,128)}, u32[]{:S(2)}) copy-start(s32[1,4]{1,0:T(1,128)} %param.22) | copy-start | bytes 52
  193.4 10.8 %copy-start.17 = (s32[1024,1]{1,0:T(8,128)}, s32[1024,1]{1,0:T(8,128)S(1)}, u32[]{:S(2)}) copy-start(s32[1024,1]{1,0:T(8,128)S(1)} %copy.64.place_ref) | copy-start | bytes 12292
  193.6 10.5 %copy-start.18 = (f32[8,768]{1,0:T(8,128)}, f32[8,768]{1,0:T(8,128)S(1)}, u32[]{:S(2)}) copy-start(f32[8,768]{1,0:T(8,128)S(1)} %reshape.248.vec_ref) | copy-start | bytes 73732
  194.2 11.2 %copy-start.15 = (s32[1024,1]{1,0:T(8,128)}, s32[1024,1]{1,0:T(8,128)S(1)}, u32[]{:S(2)}) copy-start(s32[1024,1]{1,0:T(8,128)S(1)} %copy.62.seg_ref.seg_all_ref) | copy-start | bytes 12292
  194.9 2.3 copy-start
  236.6 1.2 copy-start.21
  237.8 1.2 copy-start.22
  241.3 1.6 copy-start.26
  294.3 1.4 copy-start.46
  294.4 236.1 %reduce-scatter.8.cloned.1.call-start = ((), (), s32[]{:S(2)}) async-start(), calls=%async_computation.9 | async-start | bytes 4866048 | tf_op jit(solution)/shard_map/reduce_scatter | solution.py:601
  305.6 338.5 %reduce-scatter.4.cloned.1.call-start = ((), (), s32[]{:S(2)}) async-start(), calls=%async_computation.7 | async-start | bytes 5271552 | tf_op jit(solution)/shard_map/reduce_scatter | solution.py:601
  306.7 50.1 %copy-start.34 = (f32[8,768]{1,0:T(8,128)S(1)}, f32[8,768]{1,0:T(8,128)}, u32[]{:S(2)}) copy-start(f32[8,768]{1,0:T(8,128)} %get-tuple-element.58) | copy-start | bytes 73732
  355.6 1.2 copy-start.9
  356.8 4.4 copy-start.5
  356.8 5.5 copy-start.7
  361.2 1.8 copy-start.20
  364.5 1.9 copy-start.10
  366.3 2.6 copy-start.45
  367.8 1.8 copy-start.25
  373.0 1.9 copy-start.4
  374.8 2.6 copy-start.1
  377.5 1.4 copy-start.6
  378.9 1.4 copy-start.8
  380.3 1.4 copy-start.11
  389.6 12.2 %copy-start.14 = (bf16[1024,768]{1,0:T(8,128)(2,1)S(1)}, bf16[1024,768]{1,0:T(8,128)(2,1)}, u32[]{:S(2)}) copy-start(bf16[1024,768]{1,0:T(8,128)(2,1)} %get-tuple-element.50.rows_ref) | copy-start | bytes 4718596
  389.6 50.7 %all-to-all-start.3 = ((bf16[32,32,768]{2,1,0:T(8,128)(2,1)}), bf16[32,32,768]{2,1,0:T(8,128)(2,1)S(1)}, u32[]{:S(2)}, u32[]{:S(2)}) async-start(bf16[32,32,768]{2,1,0:T(8,128)(2,1)} %bitcast.18), calls=%async_computation.3 | async-start | bytes 3145728 | tf_op jit(solution)/shard_map/all_to_all | solution.py:618
  440.3 54.3 %all-to-all-start.2 = ((bf16[32,32,768]{2,1,0:T(8,128)(2,1)}), bf16[32,32,768]{2,1,0:T(8,128)(2,1)S(1)}, u32[]{:S(2)}, u32[]{:S(2)}) async-start(bf16[32,32,768]{2,1,0:T(8,128)(2,1)} %bitcast.16), calls=%async_computation.2 | async-start | bytes 3145728 | tf_op jit(solution)/shard_map/all_to_all | solution.py:618
  (6 other events, 6.6 us)
Sparse Core Ops, SparseCore 0:
  294.5 116.0 reduce-scatter.5
  417.0 113.4 reduce-scatter.7
  536.0 108.0 reduce-scatter.3

commit v2 on v1

--- a/solution.py
+++ b/solution.py
@@ -208,6 +208,171 @@
     )(w4, wi, wu, vec)
 
 
+class Place:
+    def __init__(self, sizes):
+        na, nb, nc, nk = self.sizes = sizes
+        self.me = me = lax.axis_index("fsdp")
+        self.k = me % nk
+        self.c = (me // nk) % nc
+        self.b = (me // (nk * nc)) % nb
+        self.a = me // (nk * nc * nb)
+
+    def ahead(self, axis, step):
+        own = (self.a, self.b, self.c, self.k)[axis]
+        return (own + step) % self.sizes[axis]
+
+    def device(self, axis, step):
+        na, nb, nc, nk = self.sizes
+        where = [self.a, self.b, self.c, self.k]
+        where[axis] = self.ahead(axis, step)
+        return ((where[0] * nb + where[1]) * nc + where[2]) * nk + where[3]
+
+
+def remote(source, target, send_sem, recv_sem, peer):
+    return pltpu.make_async_remote_copy(
+        src_ref=source, dst_ref=target, send_sem=send_sem, recv_sem=recv_sem,
+        device_id=(peer,), device_id_type=MESH,
+    )
+
+
+def greet_all(devices):
+    me = lax.axis_index("fsdp")
+    barrier = pltpu.get_barrier_semaphore()
+
+    def signal(j, carry):
+        pl.semaphore_signal(barrier, inc=1, device_id=((me + j) % devices,), device_id_type=MESH)
+        return carry
+
+    lax.fori_loop(1, devices, signal, 0)
+    pl.semaphore_wait(barrier, devices - 1)
+
+
+class Exchange:
+    def __init__(self, devices, source, target, sems, local_sem):
+        self.devices, self.source, self.target, self.sems, self.local_sem = devices, source, target, sems, local_sem
+        self.rows = source.shape[0] // devices
+        self.me = lax.axis_index("fsdp")
+
+    def block(self, ref, device):
+        return ref.at[pl.ds(pl.multiple_of(device * self.rows, self.rows), self.rows)]
+
+    def own(self):
+        return pltpu.make_async_copy(self.block(self.source, self.me), self.block(self.target, self.me), self.local_sem)
+
+    def outgoing(self, j):
+        peer = (self.me + j) % self.devices
+        return remote(self.block(self.source, peer), self.block(self.target, self.me), self.sems.at[0, j], self.sems.at[1, j], peer)
+
+    def incoming(self, j):
+        peer = (self.me + self.devices - j) % self.devices
+        block = self.block(self.target, peer)
+        return remote(block, block, self.sems.at[0, j], self.sems.at[1, j], peer)
+
+    def over(self, act):
+        def body(j, carry):
+            act(j)
+            return carry
+
+        lax.fori_loop(1, self.devices, body, 0)
+
+    def start(self):
+        self.own().start()
+        self.over(lambda j: self.outgoing(j).start())
+
+    def wait(self):
+        self.over(lambda j: self.incoming(j).wait_recv())
+        self.over(lambda j: self.outgoing(j).wait_send())
+        self.own().wait()
+
+
+def tree_scratch(sizes, flip, rows, columns):
+    na, nb, nc, nk = sizes
+    one, two = (nb, nc) if flip else (nc, nb)
+    shapes = [(na, nb, nc), (nk - 1, na, nb, nc), (one - 1, na, two), (two - 1, na), (na - 1,)]
+    return [pltpu.VMEM(shape + (rows, columns), BF16) for shape in shapes] + [
+        pltpu.SemaphoreType.DMA((2, 4, max(sizes))),
+        pltpu.SemaphoreType.DMA(()),
+    ]
+
+
+class Tree:
+    def __init__(self, place, flip, parts, scratch):
+        self.place, self.flip, self.parts = place, flip, parts
+        self.held, *self.landing, self.sems, self.local_sem = scratch
+        order = (3, 1, 2, 0) if flip else (3, 2, 1, 0)
+        self.axes = order
+
+    def own(self):
+        return pltpu.make_async_copy(self.parts.at[:, :, :, self.place.k], self.held, self.local_sem)
+
+    def outgoing(self, stage):
+        place, held = self.place, self.held
+        axis = self.axes[stage]
+        copies = []
+        for j in range(1, place.sizes[axis]):
+            other = place.ahead(axis, j)
+            if stage == 0:
+                source = self.parts.at[:, :, :, other]
+            elif stage == 1:
+                source = held.at[:, other] if self.flip else held.at[:, :, other]
+            elif stage == 2:
+                source = held.at[:, place.b, other] if self.flip else held.at[:, other, place.c]
+            else:
+                source = held.at[other, place.b, place.c]
+            copies.append(
+                remote(source, self.landing[stage].at[j - 1], self.sems.at[0, stage, j], self.sems.at[1, stage, j], place.device(axis, j))
+            )
+        return copies
+
+    def start(self, stage):
+        if stage == 0:
+            self.own().start()
+        for copy in self.outgoing(stage):
+            copy.start()
+
+    def settle(self, stage, out=None):
+        place, held, landing = self.place, self.held, self.landing[stage]
+        na, nb, nc, nk = place.sizes
+        if stage == 0:
+            self.own().wait()
+        for copy in self.outgoing(stage):
+            copy.wait_recv()
+        count = place.sizes[self.axes[stage]] - 1
+
+        def total(own, index):
+            value = own.astype(F32)
+            for j in range(count):
+                value = value + landing[(j,) + index].astype(F32)
+            return value
+
+        if stage == 0:
+            def add(i, carry):
+                held[i] = total(held[i], (i,)).astype(BF16)
+                return carry
+            lax.fori_loop(0, na, add, 0)
+        elif stage == 1:
+            two = nc if self.flip else nb
+            def add(i, carry):
+                for t in range(two):
+                    at = (i, place.b, t) if self.flip else (i, t, place.c)
+                    held[at] = total(held[at], (i, t)).astype(BF16)
+                return carry
+            lax.fori_loop(0, na, add, 0)
+        elif stage == 2:
+            def add(i, carry):
+                at = (i, place.b, place.c)
+                held[at] = total(held[at], (i,)).astype(BF16)
+                return carry
+            lax.fori_loop(0, na, add, 0)
+        else:
+            out[...] = total(held[place.a, place.b, place.c], ())
+
+    def drain(self):
+        for stage in range(4):
+            for copy in self.outgoing(stage):
+                copy.wait_send()
+
+
 def permute_kernel(tile, where_ref, rows_ref, out_ref):
     count = where_ref.shape[1]
     target = lax.broadcasted_iota(jnp.int32, (tile, count), 0) + pl.program_id(0) * tile
@@ -382,11 +547,37 @@
     )(segment_col, q, segment_col, k, v)
 
 
-def attend_back_kernel(segments, seg_ref, q_ref, o_ref, g_ref, lse_ref, seg_all_ref, k_ref, v_ref,
-                       dq_ref, dk_ref, dv_ref, sums_ref, k0, k1, v0, v1, dk_sum, dv_sum):
+def attend_back_kernel(segments, sizes, seg_ref, q_ref, o_ref, g_ref, lse_ref, seg_all_ref, k_ref, v_ref,
+                       leaving_ref, wi_ref, wu_ref, wo_ref,
+                       dq_ref, dk_ref, dv_ref, sums_ref, returned_ref, wi_out, wu_out, wo_out,
+                       k0, k1, v0, v1, dk_sum, dv_sum, swap_sems, swap_local, *tree_refs):
     count, tile = k_ref.shape[0], q_ref.shape[0]
     first_all, lane_all = feature_lanes(count)
     step, last = pl.program_id(1), pl.num_programs(1) - 1
+    now = pl.program_id(0) * pl.num_programs(1) + step
+
+    place = Place(sizes)
+    devices = sizes[0] * sizes[1] * sizes[2] * sizes[3]
+    swap = Exchange(devices, leaving_ref, returned_ref, swap_sems, swap_local)
+    trees = [
+        Tree(place, flip, parts, tree_refs[7 * i:7 * i + 7])
+        for i, (flip, parts) in enumerate(((False, wi_ref), (True, wu_ref), (False, wo_ref)))
+    ]
+    outs = (wi_out, wu_out, wo_out)
+
+    @pl.when(now == 0)
+    def _():
+        greet_all(devices)
+        for tree in trees:
+            tree.start(0)
+        swap.start()
+
+    for i, tree in enumerate(trees):
+        for stage, at in enumerate(((3, 16, 22), (5, 17, 22), (6, 18, 22))[i]):
+            @pl.when(now == at)
+            def _(tree=tree, stage=stage):
+                tree.settle(stage)
+                tree.start(stage + 1)
 
     @pl.when(step == 0)
     def _():
@@ -428,24 +619,44 @@
         dv_ref[...] = dv
         sums_ref[1:2, :] += jnp.sum(dv.astype(F32), axis=0, keepdims=True)
 
-
-def attend_back(segments, segment_col, q, out, grad, lse, k, v):
+    @pl.when(now == pl.num_programs(0) * pl.num_programs(1) - 1)
+    def _():
+        for tree, out in zip(trees, outs):
+            tree.settle(3, out)
+        swap.wait()
+        for tree in trees:
+            tree.drain()
+
+
+def attend_back(segments, segment_col, q, out, grad, lse, k, v, leaving, wi, wu, wo):
     count, width = q.shape
     pairs = width // LANES
     tile = count // 4
+    devices = wi.shape[0]
+    sizes = grid_of(devices)
     tile_spec = pl.BlockSpec((tile, LANES), lambda h, i: (i, h))
     all_spec = pl.BlockSpec((count, LANES), lambda h, i: (0, h))
+    anywhere = pl.BlockSpec(memory_space=pl.ANY)
+    parts = [x.reshape(sizes + x.shape[1:]) for x in (wi, wu, wo)]
+    trees = []
+    for flip, x in zip((False, True, False), (wi, wu, wo)):
+        trees += tree_scratch(sizes, flip, *x.shape[1:])
     return pl.pallas_call(
-        partial(attend_back_kernel, segments),
+        partial(attend_back_kernel, segments, sizes),
         grid=(pairs, 4),
-        out_shape=[jax.ShapeDtypeStruct((count, width), BF16)] * 3 + [jax.ShapeDtypeStruct((8, width), F32)],
-        in_specs=[pl.BlockSpec((tile, 1), lambda h, i: (i, 0))] + [tile_spec] * 4 + [held_spec((count, 1)), all_spec, all_spec],
-        out_specs=[tile_spec, all_spec, all_spec, pl.BlockSpec((8, LANES), lambda h, i: (0, h))],
-        scratch_shapes=[pltpu.VMEM((count, LANES), BF16)] * 4 + [pltpu.VMEM((count, LANES), F32)] * 2,
-        compiler_params=params(48, "arbitrary", "arbitrary"),
+        out_shape=[jax.ShapeDtypeStruct((count, width), BF16)] * 3
+        + [jax.ShapeDtypeStruct((8, width), F32), jax.ShapeDtypeStruct((count, width), BF16)]
+        + [jax.ShapeDtypeStruct(x.shape[1:], F32) for x in (wi, wu, wo)],
+        in_specs=[pl.BlockSpec((tile, 1), lambda h, i: (i, 0))] + [tile_spec] * 4 + [held_spec((count, 1)), all_spec, all_spec]
+        + [anywhere] * 4,
+        out_specs=[tile_spec, all_spec, all_spec, pl.BlockSpec((8, LANES), lambda h, i: (0, h)), anywhere]
+        + [full_spec(x.shape[1:]) for x in (wi, wu, wo)],
+        scratch_shapes=[pltpu.VMEM((count, LANES), BF16)] * 4 + [pltpu.VMEM((count, LANES), F32)] * 2
+        + [pltpu.SemaphoreType.DMA((2, devices)), pltpu.SemaphoreType.DMA(())] + trees,
+        compiler_params=params(60, "arbitrary", "arbitrary", collective_id=2, has_side_effects=True),
         cost_estimate=pl.CostEstimate(flops=20 * count * count * width, bytes_accessed=16 * MIB, transcendentals=count * count * 12),
         name="attend_back",
-    )(segment_col, q, out, grad, lse, segment_col, k, v)
+    )(segment_col, q, out, grad, lse, segment_col, k, v, leaving, *parts)
 
 
 def normalize(hidden):
@@ -554,51 +765,96 @@
     )(place_col, rows, attended, arrived_cot, w4, wi, wu, vec, bi)
 
 
-def rows_grad_kernel(tile, where_ref, first_ref, dq_ref, dk_ref, dv_ref, wq_ref, wk_ref, wv_ref, out_ref, total_ref):
-    step = pl.program_id(0)
-    tiles = total_ref.shape[0] // tile
-
-    @pl.when(step < tiles)
-    def _():
-        total = (
-            first_ref[...]
-            + dot_nt(dq_ref[...], wq_ref[...])
-            + dot_nt(dk_ref[...], wk_ref[...])
-            + dot_nt(dv_ref[...], wv_ref[...])
-        )
-        total_ref[pl.ds(pl.multiple_of(step * tile, tile), tile), :] = total.astype(BF16)
-
-    @pl.when(step >= tiles)
-    def _():
-        count = where_ref.shape[1]
-        target = lax.broadcasted_iota(jnp.int32, (tile, count), 0) + (step - tiles) * tile
+def finish_kernel(sizes, share, where_ref, rank_ref, first_hbm, dq_hbm, dk_hbm, dv_hbm, w4_hbm, rows_hbm, returned_hbm, small_ref,
+                  layer_ref, tokens_ref, wq_out, wk_out, wv_out, small_out,
+                  first_ref, dq_ref, dk_ref, dv_ref, w_ref, rows_ref, returned_ref, load_sems,
+                  total_ref, leaving_ref, back_ref, wq_ref, wk_ref, wv_ref, swap_sems, swap_local, *tree_refs):
+    count, width = total_ref.shape
+    devices = count and sizes[0] * sizes[1] * sizes[2] * sizes[3]
+    na, nb, nc, nk = sizes
+    tile = count // 4
+    loads = [
+        pltpu.make_async_copy(source, target, load_sems.at[i])
+        for i, (source, target) in enumerate((
+            (first_hbm, first_ref), (dq_hbm, dq_ref), (w4_hbm.at[pl.ds(0, 3)], w_ref), (dk_hbm, dk_ref), (dv_hbm, dv_ref),
+            (rows_hbm, rows_ref), (returned_hbm, returned_ref),
+        ))
+    ]
+    for load in loads:
+        load.start()
+    place = Place(sizes)
+    swap = Exchange(devices, leaving_ref, back_ref, swap_sems, swap_local)
+    parts = (wq_ref, wk_ref, wv_ref, small_ref)
+    trees = [Tree(place, flip, ref, tree_refs[7 * i:7 * i + 7]) for i, (flip, ref) in enumerate(zip((False, True, False, True), parts))]
+    greet_all(devices)
+    for load in loads[:5]:
+        load.wait()
+    trees[3].start(0)
+    for at in range(0, count, tile):
+        cut = slice(at, at + tile)
+        total_ref[cut] = (
+            first_ref[cut] + dot_nt(dq_ref[cut], w_ref[0]) + dot_nt(dk_ref[cut], w_ref[1]) + dot_nt(dv_ref[cut], w_ref[2])
+        ).astype(BF16)
+    for at in range(0, count, tile):
+        target = lax.broadcasted_iota(jnp.int32, (tile, count), 0) + at
         chosen = jnp.where(where_ref[...] == target, 1.0, 0.0).astype(BF16)
-        out_ref[...] = dot_nn(chosen, total_ref[...]).astype(BF16)
-
-
-def rows_grad(where_row, first_grad, dq, dk, dv, w4):
+        leaving_ref[at:at + tile] = dot_nn(chosen, total_ref[...]).astype(BF16)
+    swap.start()
+    loads[5].wait()
+    group = 3 * LANES
+    for grad_ref, out_ref, tree in zip((dq_ref, dk_ref, dv_ref), parts, trees):
+        for at in range(0, width, group):
+            value = dot_tn(rows_ref[:, at:at + group], grad_ref[...])
+            for i in range(group // share):
+                d = at // share + i
+                index = (d // (nk * nc * nb), d // (nk * nc) % nb, d // nk % nc, d % nk)
+                out_ref[index] = value[i * share:(i + 1) * share].astype(BF16)
+        tree.start(0)
+    loads[6].wait()
+
+    def restore(out_ref, from_ref):
+        for at in range(0, count, tile):
+            lane = lax.broadcasted_iota(jnp.int32, (tile, count), 1)
+            chosen = jnp.where(rank_ref[at:at + tile] == lane, 1.0, 0.0).astype(BF16)
+            out_ref[at:at + tile] = dot_nn(chosen, from_ref[...]).astype(BF16)
+
+    for stage in range(3):
+        for tree in trees:
+            tree.settle(stage)
+            tree.start(stage + 1)
+        if stage == 0:
+            restore(layer_ref, returned_ref)
+    for tree, out in zip(trees, (wq_out, wk_out, wv_out, small_out)):
+        tree.settle(3, out)
+    swap.wait()
+    restore(tokens_ref, back_ref)
+    for tree in trees:
+        tree.drain()
+
+
+def finish(place_row, rank_col, first_grad, dq, dk, dv, w4, rows, returned, small):
     count, width = dq.shape
-    tiles = 4
-    tile = count // tiles
-    row_spec = pl.BlockSpec((tile, width), lambda i: (jnp.minimum(i, tiles - 1), 0))
-
-    def weight(n):
-        return pl.BlockSpec((pl.Squeezed(), width, width), lambda i: (n, 0, 0), pipeline_mode=pl.Buffered(1))
-
+    devices = small.shape[0]
+    sizes = grid_of(devices)
+    share = width // devices
+    anywhere = pl.BlockSpec(memory_space=pl.ANY)
+    in_vmem = pl.BlockSpec(memory_space=pltpu.VMEM)
+    whole = pltpu.VMEM((count, width), BF16)
+    trees = []
+    for flip, shape in zip((False, True, False, True), ((share, width),) * 3 + (small.shape[1:],)):
+        trees += tree_scratch(sizes, flip, *shape)
     return pl.pallas_call(
-        partial(rows_grad_kernel, tile),
-        grid=(2 * tiles,),
-        out_shape=jax.ShapeDtypeStruct((count, width), BF16),
-        in_specs=[held_spec((1, count)), row_spec, row_spec, row_spec, row_spec, weight(0), weight(1), weight(2)],
-        out_specs=pl.BlockSpec((tile, width), lambda i: (jnp.maximum(i - tiles, 0), 0)),
-        scratch_shapes=[pltpu.VMEM((count, width), BF16)],
-        compiler_params=params(40, "arbitrary"),
-        name="rows_grad",
-    )(where_row, first_grad, dq, dk, dv, w4, w4, w4)
-
-
-def scatter_sum(pieces):
-    return lax.psum_scatter(pieces, "fsdp", scatter_dimension=0, tiled=True)
+        partial(finish_kernel, sizes, share),
+        out_shape=[jax.ShapeDtypeStruct((count, width), BF16)] * 2
+        + [jax.ShapeDtypeStruct((share, width), F32)] * 3 + [jax.ShapeDtypeStruct(small.shape[1:], F32)],
+        in_specs=[in_vmem] * 2 + [anywhere] * 7 + [in_vmem],
+        out_specs=[in_vmem] * 6,
+        scratch_shapes=[pltpu.VMEM((count, width), F32)] + [whole] * 3 + [pltpu.VMEM((3, width, width), BF16)] + [whole] * 2
+        + [pltpu.SemaphoreType.DMA((7,))] + [whole] * 3 + [pltpu.VMEM(sizes + (share, width), BF16)] * 3
+        + [pltpu.SemaphoreType.DMA((2, devices)), pltpu.SemaphoreType.DMA(())] + trees,
+        compiler_params=pltpu.CompilerParams(collective_id=3, has_side_effects=True, vmem_limit_bytes=60 * MIB),
+        name="finish",
+    )(place_row, rank_col, first_grad, dq, dk, dv, w4, rows, returned, small.reshape(sizes + small.shape[1:]))
 
 
 def on_device(tokens, cotangent, packed_slot, seq_lengths, query_weight, query_bias, key_weight, value_weight,
@@ -652,36 +908,31 @@
     (result, activated, inner_low, normed_low, outer_low, branch_low, first_grad, attended_grad, sums, bi_sum) = feed_forward(
         place_col, rows, attended, arrived_cot, w4, wi, wu, vec, bi
     )
-    layer_out = unpermute_rows(rank_col, exchange(permute_rows(place_row, result)))
+    leaving = permute_rows(place_row, result)
 
     def weight_grad(left, right):
-        return dot_tn(left, right).astype(BF16)
-
-    def pieces_of(grad):
+        grad = dot_tn(left, right).astype(BF16)
         return grad.reshape(devices, -1, grad.shape[-1])
 
-    inner_grad = scatter_sum(pieces_of(weight_grad(normed_low, inner_low)))
-    outer_grad = scatter_sum(pieces_of(weight_grad(activated, outer_low)))
+    inner_grad = weight_grad(normed_low, inner_low)
+    outer_grad = weight_grad(activated, outer_low)
     wo_grad = weight_grad(attended, branch_low)
-
-    dq, dk, dv, more = attend_back(segments, segment_col, q, attended, attended_grad, lse, k, v)
-    tokens_grad = unpermute_rows(rank_col, exchange(rows_grad(place_row, first_grad, dq, dk, dv, w4)))
+    dq, dk, dv, more, returned, inner_grad, outer_grad, wo_grad = attend_back(
+        segments, segment_col, q, attended, attended_grad, lse, k, v, leaving, inner_grad, outer_grad, wo_grad
+    )
     sums = sums + more
     sums = sums.reshape(8, devices, share).transpose(1, 0, 2).reshape(devices, 8 * share)
     sums = jnp.concatenate([sums, bi_sum[0].reshape(devices, hidden_width // devices)], axis=1)
-    sums = jnp.pad(sums, ((0, 0), (0, width - used))).reshape(devices, 1, width).astype(BF16)
-    late = jnp.concatenate(
-        [pieces_of(weight_grad(rows, dq)), pieces_of(weight_grad(rows, dk)), pieces_of(weight_grad(rows, dv)),
-         pieces_of(wo_grad), sums],
-        axis=1,
+    sums = jnp.pad(sums, ((0, 0), (0, 8 * LANES - used))).reshape(devices, 8, LANES).astype(BF16)
+    layer_out, tokens_grad, wq_grad, wk_grad, wv_grad, sums = finish(
+        place_row, rank_col, first_grad, dq, dk, dv, w4, rows, returned, sums
     )
-    late = scatter_sum(late)[0].astype(F32)
-    wq_grad, wk_grad, wv_grad, wo_grad = (late[i * share:(i + 1) * share].reshape(-1) for i in range(4))
-    sums = late[4 * share]
+    wq_grad, wk_grad, wv_grad, wo_grad = (x.reshape(-1) for x in (wq_grad, wk_grad, wv_grad, wo_grad))
+    sums = sums.reshape(-1)
     small = [sums[i * share:(i + 1) * share] for i in range(8)]
     return (
         layer_out, tokens_grad, wq_grad, small[0], wk_grad, wv_grad, small[1], wo_grad, small[2], small[3], small[4],
-        inner_grad.astype(F32).reshape(-1), sums[8 * share:used], outer_grad.astype(F32).reshape(-1), small[5], small[6], small[7],
+        inner_grad.reshape(-1), sums[8 * share:used], outer_grad.reshape(-1), small[5], small[6], small[7],
     )
 
 

time: 658 us -> 496 us (0.75)
  waiting for transfers between devices: 256 us -> 34.5 us
  Pallas kernels: 278 us -> 382 us
  starting transfers between devices: 27.5 us -> 11.2 us
  local copies, waits for them, and re-layouts: 48.9 us -> 34.4 us
  between operations: 14.4 us -> 1.66 us
    reduce_scatter x3 -> x0, waiting for transfers between devices: 142 us -> none  [scatter_sum(): return lax.psum_scatter(pieces, 'fsdp', scatter_dimension=0, tiled=True)]
    pallas_call x4 -> x2, Pallas kernels: 63.7 us -> 169 us  [the longest x1 106 us: attend_back(): pl.pallas_call(partial(attend_back_kernel, segments, sizes), grid=(pairs,...]
    all_to_all x4 -> x2, waiting for transfers between devices: 114 us -> 34.5 us  [exchange(): lax.all_to_all(pieces, 'fsdp', split_axis=0, concat_axis=0, tiled=True)]
    all_to_all x4 -> x2, starting transfers between devices: 27.4 us -> 11.2 us  [exchange(): lax.all_to_all(pieces, 'fsdp', split_axis=0, concat_axis=0, tiled=True)]
    unnamed x100 -> x91, local copies, waits for them, and re-layouts: 33.8 us -> 17.8 us
    dot_general x6 -> x3, matrix products: 26.5 us -> 21.1 us  [dot_tn(): lax.dot_general(a, b, (((0,), (0,)), ((), ())), preferred_element_type=F32)]
  transfers between devices with their start and end apart: 7 -> 2, of which waited for: 5 -> 1; matrix products, arithmetic and copies ran while one was open for 6% -> 2% of each run, Pallas kernels for 35% -> 34%
where the time goes in v2:
time: 496 us; the launch traced here: 489 us
  Pallas kernels  382 us (77%)
  waiting for transfers between devices  34.5 us (7%)
  local copies, waits for them, and re-layouts  34.4 us (7%)
  matrix products  21.1 us (4%)
  starting transfers between devices  11.2 us (2%)
    pallas_call x1, Pallas kernels, gather_parameters(): pl.pallas_call(partial(gather_kernel, sizes, wu.shape[0] // 16 * 8), out_...  117 us
    pallas_call x1, Pallas kernels, attend_back(): pl.pallas_call(partial(attend_back_kernel, segments, sizes), grid=(pairs,...  106 us
    pallas_call x1, Pallas kernels, finish(): pl.pallas_call(partial(finish_kernel, sizes, share), out_shape=[jax.Shape...  63 us
    pallas_call x1, Pallas kernels, feed_forward(): pl.pallas_call(partial(feed_kernel, 512), grid=(4,), out_shape=[rows_of(w...  42.2 us
    all_to_all x2, waiting for transfers between devices, exchange(): lax.all_to_all(pieces, 'fsdp', split_axis=0, concat_axis=0, tiled=True)  34.5 us
    pallas_call x1, Pallas kernels, attend(): pl.pallas_call(partial(attend_kernel, segments), grid=(pairs, 4), out_sha...  31.4 us
    dot_general x3, matrix products, dot_tn(): lax.dot_general(a, b, (((0,), (0,)), ((), ())), preferred_element_type=F32)  21.1 us
    unnamed x91, local copies, waits for them, and re-layouts  17.8 us
  transfers between devices with their start and end apart: 2, of which 1 were waited for; matrix products, arithmetic and copies ran while one was open for 2% of the time, Pallas kernels for 34%

profile of v2, /device:TPU:0, one launch (start us, length us, event | category | flops | bytes accessed | tf_op | source)
XLA Modules:
  0.0 488.9 jit_solution(17612288936045725698)
XLA Ops:
  0.7 0.7 dynamic_slice.3
  1.9 1.4 copy-done.2
  3.3 3.2 permute_rows.3
  6.6 7.3 %all-to-all-start = ((bf16[32,32,768]{2,1,0:T(8,128)(2,1)}), bf16[32,32,768]{2,1,0:T(8,128)(2,1)S(1)}, u32[]{:S(2)}, u32[]{:S(2)}) async-start(bf16[32,32,768]{2,1,0:T(8,128)(2,1)} %bitcast.4), calls=%async_computation | async-start | bytes 3145728 | tf_op jit(solution)/shard_map/all_to_all | solution.py:874
  13.9 3.3 permute_rows.4
  17.2 34.4 %all-to-all-done = bf16[32,32,768]{2,1,0:T(8,128)(2,1)S(1)} async-done(((bf16[32,32,768]{2,1,0:T(8,128)(2,1)}), bf16[32,32,768]{2,1,0:T(8,128)(2,1)S(1)}, u32[]{:S(2)}, u32[]{:S(2)}) %all-to-all-start) | async-done | bytes 1572896 | tf_op jit(solution)/shard_map/all_to_all | solution.py:874
  51.8 3.9 all-to-all-start.1
  56.0 0.7 reshape.194.wi
  56.7 0.8 reshape.195.wu
  58.3 0.7 pad_maximum_fusion.w4
  58.9 117.3 %shard_map.314 = (bf16[4,32,24,768]{3,2,1,0:T(8,128)(2,1)}, bf16[32,24,3072]{2,1,0:T(8,128)(2,1)}, bf16[32,96,768]{2,1,0:T(8,128)(2,1)}, bf16[32,8,128]{2,1,0:T(8,128)(2,1)}) custom-call(bf16[4,24,768]{2,1,0:T(8,128)(2,1)} %pad_maximum_fusion.w4, bf16[24,3072]{1,0:T(8,128)(2,1)} %reshape.194.wi, bf16[96,768]{1,0:T(8,128)(2,1)} %reshape.195.wu, ...), custom_call_target="tpu_custom_call" | custom-call | tf_op jit(solution)/shard_map/pallas_call | solution.py:192
  176.3 0.9 copy.69
  177.2 0.7 sub.10.slots_ref
  177.9 6.5 %source_devices.1 = f32[32,32]{1,0:T(8,128)} custom-call(s32[32,1024]{1,0:T(8,128)} %sub.10.slots_ref), custom_call_target="tpu_custom_call" | custom-call | tf_op jit(solution)/shard_map/source_devices/pallas_call | solution.py:436
  184.5 0.7 convert_element_type.36
  185.2 0.7 broadcast_multiply_fusion
  187.7 0.8 reshape.207.bi_ref
  188.5 1.0 copy.64.rank_ref
  189.5 2.3 copy-done
  191.9 6.8 %project.1 = (bf16[1024,768]{1,0:T(8,128)(2,1)S(1)}, bf16[1024,768]{1,0:T(8,128)(2,1)S(1)}, bf16[1024,768]{1,0:T(8,128)(2,1)S(1)}, bf16[1024,768]{1,0:T(8,128)(2,1)S(1)}) custom-call(s32[1024,1]{1,0:T(8,128)S(1)} %copy.60.place_ref, bf16[1024,768]{1,0:T(8,128)(2,1)S(1)} %bitcast.44, bf16[4,768,768]{2,1,0:T(8,128)(2,1)S(1)} %bitcast.41, ...), custom_call_target="tpu_custom_call" | custom-call | flops 4831838208 | bytes 14680064 | tf_op jit(solution)/shard_map/project/pallas_call | solution.py:465
  198.7 1.1 copy-done.1
  199.8 31.4 %attend.1 = (bf16[1024,768]{1,0:T(8,128)(2,1)S(1)}, f32[1024,768]{1,0:T(8,128)S(1)}) custom-call(s32[1024,1]{1,0:T(8,128)S(1)} %copy.58.seg_ref.seg_all_ref, bf16[1024,768]{1,0:T(8,128)(2,1)S(1)} %get-tuple-element.54.q_ref, s32[1024,1]{1,0:T(8,128)S(1)} %copy.58.seg_ref.seg_all_ref, bf16[1024,768]{1,0:T(8,128)(2,1)S(1)} %get-tuple-element.55.k_ref, ...), custom_call_target="tpu_custom_call" | custom-call | flops 6442450944 | bytes 10485760 | tf_op jit(solution)/shard_map/attend/pallas_call | solution.py:537
  231.2 1.1 copy-done.10
  232.3 1.1 copy-done.11
  233.5 1.2 copy-done.12
  234.7 1.1 copy-done.13
  235.8 1.6 copy-done.15
  237.4 42.2 %feed_forward.1 = (bf16[1024,768]{1,0:T(8,128)(2,1)}, bf16[1024,3072]{1,0:T(8,128)(2,1)}, bf16[1024,3072]{1,0:T(8,128)(2,1)}, bf16[1024,768]{1,0:T(8,128)(2,1)},...) custom-call(s32[1024,1]{1,0:T(8,128)} %copy-done.7, ...), custom_call_target="tpu_custom_call" | custom-call | flops 28991029248 | bytes 37748736 | tf_op jit(solution)/shard_map/feed_forward/pallas_call | solution.py:746
  279.6 4.0 convolution_convert_fusion.2
  283.7 9.9 %convolution_convert_fusion = bf16[3072,768]{1,0:T(8,128)(2,1)} fusion(bf16[1024,3072]{1,0:T(8,128)(2,1)} %get-tuple-element.66, bf16[1024,768]{1,0:T(8,128)(2,1)S(1)} %copy-done.40), kind=kOutput, calls=%fused_computation | convolution fusion | flops 4834197504 | bytes 12582912 | tf_op jit(solution)/shard_map/dot_general | solution.py:29
  293.6 7.1 %convolution_convert_fusion.1 = bf16[768,3072]{1,0:T(8,128)(2,1)} fusion(bf16[1024,768]{1,0:T(8,128)(2,1)S(1)} %copy-done.39, bf16[1024,3072]{1,0:T(8,128)(2,1)S(1)} %bitcast.69), kind=kOutput, calls=%fused_computation.1 | convolution fusion | flops 4834197504 | bytes 12582912 | tf_op jit(solution)/shard_map/dot_general | solution.py:29
  300.8 2.3 permute_rows.5.leaving_ref
  303.1 1.2 copy-done.4
  304.3 105.7 %attend_back.1 = (bf16[1024,768]{1,0:T(8,128)(2,1)}, bf16[1024,768]{1,0:T(8,128)(2,1)}, bf16[1024,768]{1,0:T(8,128)(2,1)}, f32[8,768]{1,0:T(8,128)}, bf16[1024,7...) custom-call(s32[1024,1]{1,0:T(8,128)} %copy-done.6, ...), custom_call_target="tpu_custom_call" | custom-call | flops 16106127360 | bytes 16777216 | tf_op jit(solution)/shard_map/attend_back/pallas_call | solution.py:644
  410.0 0.7 add_convert_fusion
  411.0 0.9 fusion.5
  412.1 0.6 copy.66
  412.8 63.0 %finish.1 = (bf16[1024,768]{1,0:T(8,128)(2,1)}, bf16[1024,768]{1,0:T(8,128)(2,1)}, f32[24,768]{1,0:T(8,128)}, f32[24,768]{1,0:T(8,128)}, f32[24,768]{1,0:T(8,128)}, /*index=5*/f32[8,128]{1,0:T(8,128)}) custom-call(s32[1,1024]{1,0:T(1,128)} %copy-done.8, s32[1024,1]{1,0:T(8,128)} %copy.64.rank_ref, f32[1024,768]{1,0:T(8,128)} %get-tuple-element.60.first_hbm, ...), custom_call_target="tpu_custom_call" | custom-call | tf_op jit(solution)/shard_map/finish/pallas_call | solution.py:846
  475.8 1.6 fusion.6
  477.3 1.3 slice.45
  478.6 1.5 reshape.210
  480.1 1.5 reshape.212
  481.6 1.5 reshape.213
  483.2 0.8 copy.67
  483.9 0.7 reshape.216
  485.3 1.1 copy.72
  486.5 0.8 copy-done.16
  487.3 1.1 copy.73
  (107 shorter events, 4.5 us)
Async XLA Ops:
  1.9 1.4 copy-start.2
  6.6 7.3 %copy-start.3 = (bf16[1024,768]{1,0:T(8,128)(2,1)S(1)}, bf16[1024,768]{1,0:T(8,128)(2,1)}, u32[]{:S(2)}) copy-start(bf16[1024,768]{1,0:T(8,128)(2,1)} %rows_ref.3) | copy-start | bytes 4718596
  6.6 45.0 %all-to-all-start = ((bf16[32,32,768]{2,1,0:T(8,128)(2,1)}), bf16[32,32,768]{2,1,0:T(8,128)(2,1)S(1)}, u32[]{:S(2)}, u32[]{:S(2)}) async-start(bf16[32,32,768]{2,1,0:T(8,128)(2,1)} %bitcast.4), calls=%async_computation | async-start | bytes 3145728 | tf_op jit(solution)/shard_map/all_to_all | solution.py:874
  51.6 4.0 copy-start.24
  51.6 4.1 copy-start.25
  51.6 4.2 copy-start.26
  51.6 4.3 copy-start.27
  51.6 4.3 copy-start.20
  51.6 5.1 %copy-start.21 = (bf16[73728]{0:T(1024)(128)(2,1)S(1)}, bf16[73728]{0:T(1024)(128)(2,1)}, u32[]{:S(2)}) copy-start(bf16[73728]{0:T(1024)(128)(2,1)} %param.34) | copy-start | bytes 442372
  51.6 5.9 %copy-start.29 = (bf16[24]{0:T(256)(128)(2,1)S(1)}, bf16[24]{0:T(256)(128)(2,1)}, u32[]{:S(2)}) copy-start(bf16[24]{0:T(256)(128)(2,1)} %param.24) | copy-start | bytes 148
  51.7 5.9 %copy-start.30 = (bf16[24]{0:T(256)(128)(2,1)S(1)}, bf16[24]{0:T(256)(128)(2,1)}, u32[]{:S(2)}) copy-start(bf16[24]{0:T(256)(128)(2,1)} %param.27) | copy-start | bytes 148
  51.7 5.8 %copy-start.31 = (bf16[24]{0:T(256)(128)(2,1)S(1)}, bf16[24]{0:T(256)(128)(2,1)}, u32[]{:S(2)}) copy-start(bf16[24]{0:T(256)(128)(2,1)} %param.29) | copy-start | bytes 148
  51.7 5.8 %copy-start.32 = (bf16[24]{0:T(256)(128)(2,1)S(1)}, bf16[24]{0:T(256)(128)(2,1)}, u32[]{:S(2)}) copy-start(bf16[24]{0:T(256)(128)(2,1)} %param.30) | copy-start | bytes 148
  51.7 5.8 %copy-start.33 = (bf16[24]{0:T(256)(128)(2,1)S(1)}, bf16[24]{0:T(256)(128)(2,1)}, u32[]{:S(2)}) copy-start(bf16[24]{0:T(256)(128)(2,1)} %param.31) | copy-start | bytes 148
  51.7 5.8 %copy-start.34 = (bf16[24]{0:T(256)(128)(2,1)S(1)}, bf16[24]{0:T(256)(128)(2,1)}, u32[]{:S(2)}) copy-start(bf16[24]{0:T(256)(128)(2,1)} %param.35) | copy-start | bytes 148
  51.7 5.8 %copy-start.35 = (bf16[24]{0:T(256)(128)(2,1)S(1)}, bf16[24]{0:T(256)(128)(2,1)}, u32[]{:S(2)}) copy-start(bf16[24]{0:T(256)(128)(2,1)} %param.36) | copy-start | bytes 148
  51.7 5.8 %copy-start.36 = (bf16[24]{0:T(256)(128)(2,1)S(1)}, bf16[24]{0:T(256)(128)(2,1)}, u32[]{:S(2)}) copy-start(bf16[24]{0:T(256)(128)(2,1)} %param.37) | copy-start | bytes 148
  51.7 5.8 %copy-start.37 = (bf16[96]{0:T(256)(128)(2,1)S(1)}, bf16[96]{0:T(256)(128)(2,1)}, u32[]{:S(2)}) copy-start(bf16[96]{0:T(256)(128)(2,1)} %param.33) | copy-start | bytes 580
  51.8 185.7 %all-to-all-start.1 = ((bf16[32,32,768]{2,1,0:T(8,128)(2,1)}), bf16[32,32,768]{2,1,0:T(8,128)(2,1)}, u32[]{:S(2)}, u32[]{:S(2)}) async-start(bf16[32,32,768]{2,1,0:T(8,128)(2,1)} %bitcast.12), calls=%async_computation.1 | async-start | bytes 3145728 | tf_op jit(solution)/shard_map/all_to_all | solution.py:874
  55.7 121.6 %copy-start.22 = (s32[32768]{0:T(1024)S(1)}, s32[32768]{0:T(1024)}, u32[]{:S(2)}) copy-start(s32[32768]{0:T(1024)} %param.21) | copy-start | bytes 393220
  56.7 130.5 %copy-start.38 = (s32[1,4]{1,0:T(1,128)S(1)}, s32[1,4]{1,0:T(1,128)}, u32[]{:S(2)}) copy-start(s32[1,4]{1,0:T(1,128)} %param.22) | copy-start | bytes 52
  186.9 11.8 %copy-start.7 = (s32[1024,1]{1,0:T(8,128)}, s32[1024,1]{1,0:T(8,128)S(1)}, u32[]{:S(2)}) copy-start(s32[1024,1]{1,0:T(8,128)S(1)} %copy.60.place_ref) | copy-start | bytes 12292
  187.2 11.5 %copy-start.9 = (f32[8,768]{1,0:T(8,128)}, f32[8,768]{1,0:T(8,128)S(1)}, u32[]{:S(2)}) copy-start(f32[8,768]{1,0:T(8,128)S(1)} %reshape.199.vec_ref) | copy-start | bytes 73732
  187.7 12.1 %copy-start.6 = (s32[1024,1]{1,0:T(8,128)}, s32[1024,1]{1,0:T(8,128)S(1)}, u32[]{:S(2)}) copy-start(s32[1024,1]{1,0:T(8,128)S(1)} %copy.58.seg_ref.seg_all_ref) | copy-start | bytes 12292
  189.5 111.2 %copy-start.8 = (s32[1,1024]{1,0:T(1,128)}, s32[1,1024]{1,0:T(1,128)S(1)}, u32[]{:S(2)}) copy-start(s32[1,1024]{1,0:T(1,128)S(1)} %add.29.where_ref) | copy-start | bytes 12292
  189.5 2.3 copy-start
  198.7 1.1 copy-start.1
  231.2 1.1 copy-start.10
  232.3 1.1 copy-start.11
  233.5 1.2 copy-start.12
  234.7 1.1 copy-start.13
  235.8 1.6 copy-start.15
  237.4 42.2 %copy-start.14 = (bf16[1024,768]{1,0:T(8,128)(2,1)S(1)}, bf16[1024,768]{1,0:T(8,128)(2,1)}, u32[]{:S(2)}) copy-start(bf16[1024,768]{1,0:T(8,128)(2,1)} %copy-done.13) | copy-start | bytes 4718596
  279.6 4.1 copy-start.40
  279.6 14.0 %slice-start = ((s8[6291456]{0:T(1024)(128)(4,1)}), s8[4194304]{0:T(1024)(128)(4,1)S(1)}, s32[]{:S(2)}) async-start(s8[6291456]{0:T(1024)(128)(4,1)} %bitcast.68), calls=%async_computation.2 | async-start | bytes 8388608
  283.7 9.9 %slice-start.1 = ((s8[6291456]{0:T(1024)(128)(4,1)}), s8[2097152]{0:T(1024)(128)(4,1)S(1)}, s32[]{:S(2)}) async-start(s8[6291456]{0:T(1024)(128)(4,1)} %bitcast.68), calls=%async_computation.3 | async-start | bytes 4194304
  283.7 9.9 %copy-start.39 = (bf16[1024,768]{1,0:T(8,128)(2,1)S(1)}, bf16[1024,768]{1,0:T(8,128)(2,1)}, u32[]{:S(2)}) copy-start(bf16[1024,768]{1,0:T(8,128)(2,1)} %get-tuple-element.64) | copy-start | bytes 4718596
  293.6 7.1 %copy-start.5 = (bf16[1024,768]{1,0:T(8,128)(2,1)S(1)}, bf16[1024,768]{1,0:T(8,128)(2,1)}, u32[]{:S(2)}) copy-start(bf16[1024,768]{1,0:T(8,128)(2,1)} %get-tuple-element.63.rows_ref) | copy-start | bytes 4718596
  303.1 1.2 copy-start.4
  304.3 105.7 %copy-start.28 = (f32[8,768]{1,0:T(8,128)S(1)}, f32[8,768]{1,0:T(8,128)}, u32[]{:S(2)}) copy-start(f32[8,768]{1,0:T(8,128)} %get-tuple-element.73) | copy-start | bytes 73732
  412.8 70.4 %copy-start.19 = (f32[24,3072]{1,0:T(8,128)S(1)}, f32[24,3072]{1,0:T(8,128)}, u32[]{:S(2)}) copy-start(f32[24,3072]{1,0:T(8,128)} %get-tuple-element.83) | copy-start | bytes 884740
  412.8 71.2 %copy-start.18 = (f32[96,768]{1,0:T(8,128)S(1)}, f32[96,768]{1,0:T(8,128)}, u32[]{:S(2)}) copy-start(f32[96,768]{1,0:T(8,128)} %get-tuple-element.84) | copy-start | bytes 884740
  475.7 8.9 %copy-start.23 = (f32[24,768]{1,0:T(8,128)S(1)}, f32[24,768]{1,0:T(8,128)}, u32[]{:S(2)}) copy-start(f32[24,768]{1,0:T(8,128)} %get-tuple-element.82) | copy-start | bytes 221188
  475.8 9.6 %copy-start.17 = (bf16[1024,768]{1,0:T(8,128)(2,1)S(1)}, bf16[1024,768]{1,0:T(8,128)(2,1)}, u32[]{:S(2)}) copy-start(bf16[1024,768]{1,0:T(8,128)(2,1)} %get-tuple-element.110) | copy-start | bytes 4718596
  485.3 2.0 copy-start.16

commit v3 on v2

v3 whole, which is shorter than its diff:
```python
from functools import partial

import jax
import jax.numpy as jnp
from jax import lax
from jax.experimental import pallas as pl
from jax.experimental.pallas import tpu as pltpu
from jax.sharding import PartitionSpec as P

HD = 64
LANES = 128
EPSILON = 1e-12
NEG_LARGE = -1e30
MIB = 1 << 20
F32 = jnp.float32
BF16 = jnp.bfloat16
MESH = pl.DeviceIdType.MESH


def dot_nn(a, b):
    return lax.dot_general(a, b, (((1,), (0,)), ((), ())), preferred_element_type=F32)


def dot_nt(a, b):
    return lax.dot_general(a, b, (((1,), (1,)), ((), ())), preferred_element_type=F32)


def dot_tn(a, b):
    return lax.dot_general(a, b, (((0,), (0,)), ((), ())), preferred_element_type=F32)


def full_spec(shape, **kw):
    return pl.BlockSpec(shape, lambda *_: (0,) * len(shape), **kw)


def held_spec(shape):
    return full_spec(shape, pipeline_mode=pl.Buffered(1))


def params(mib, *axes, **kw):
    return pltpu.CompilerParams(
        dimension_semantics=axes or None, vmem_limit_bytes=mib * MIB, **kw
    )


def grid_of(devices):
    return {32: (4, 2, 2, 2), 128: (4, 4, 4, 2)}.get(devices, (devices, 1, 1, 1))


class Place:
    def __init__(self, sizes):
        na, nb, nc, nk = self.sizes = sizes
        self.me = me = lax.axis_index("fsdp")
        self.k = me % nk
        self.c = (me // nk) % nc
        self.b = (me // (nk * nc)) % nb
        self.a = me // (nk * nc * nb)

    def ahead(self, axis, step):
        own = (self.a, self.b, self.c, self.k)[axis]
        return (own + step) % self.sizes[axis]

    def device(self, axis, step):
        na, nb, nc, nk = self.sizes
        where = [self.a, self.b, self.c, self.k]
        where[axis] = self.ahead(axis, step)
        return ((where[0] * nb + where[1]) * nc + where[2]) * nk + where[3]


def remote(source, target, send_sem, recv_sem, peer):
    return pltpu.make_async_remote_copy(
        src_ref=source, dst_ref=target, send_sem=send_sem, recv_sem=recv_sem,
        device_id=(peer,), device_id_type=MESH,
    )


def greet_all(devices):
    me = lax.axis_index("fsdp")
    barrier = pltpu.get_barrier_semaphore()

    def signal(j, carry):
        pl.semaphore_signal(barrier, inc=1, device_id=((me + j) % devices,), device_id_type=MESH)
        return carry

    lax.fori_loop(1, devices, signal, 0)
    pl.semaphore_wait(barrier, devices - 1)


class Exchange:
    def __init__(self, devices, source, target, sems, local_sem, turns=None):
        self.devices, self.source, self.target, self.sems, self.local_sem = devices, source, target, sems, local_sem
        self.turns = turns or (1, devices)
        self.rows = source.shape[0] // devices
        self.me = lax.axis_index("fsdp")

    def block(self, ref, device):
        return ref.at[pl.ds(pl.multiple_of(device * self.rows, self.rows), self.rows)]

    def own(self):
        return pltpu.make_async_copy(self.block(self.source, self.me), self.block(self.target, self.me), self.local_sem)

    def outgoing(self, j):
        peer = (self.me + j) % self.devices
        return remote(self.block(self.source, peer), self.block(self.target, self.me), self.sems.at[0, j], self.sems.at[1, j], peer)

    def incoming(self, j):
        peer = (self.me + self.devices - j) % self.devices
        block = self.block(self.target, peer)
        return remote(block, block, self.sems.at[0, j], self.sems.at[1, j], peer)

    def over(self, act):
        def body(j, carry):
            act((j * 13) % self.devices)
            return carry

        lax.fori_loop(*self.turns, body, 0)

    def start(self):
        self.own().start()
        self.start_remote()

    def start_remote(self):
        self.over(lambda j: self.outgoing(j).start())

    def wait(self):
        self.wait_remote()
        self.own().wait()

    def wait_remote(self):
        self.over(lambda j: self.incoming(j).wait_recv())
        self.over(lambda j: self.outgoing(j).wait_send())


def greet_peers(place):
    barrier = pltpu.get_barrier_semaphore()
    count = 0
    for axis, size in enumerate(place.sizes):
        for j in range(1, size):
            pl.semaphore_signal(barrier, inc=1, device_id=(place.device(axis, j),), device_id_type=MESH)
            count += 1
    pl.semaphore_wait(barrier, count)


def spread_scratch(sizes):
    return [pltpu.SemaphoreType.DMA((2, 4, max(sizes))), pltpu.SemaphoreType.DMA(())]


class Spread:
    def __init__(self, place, flip, own, out, scratch, lead=()):
        self.place, self.flip, self.mine, self.out, self.lead = place, flip, own, out, lead
        self.sems, self.local_sem = scratch
        self.axes = (0, 1, 2, 3) if flip else (0, 2, 1, 3)

    def region(self, stage, step=0):
        place, every = self.place, slice(None)
        where = [place.a, place.b, place.c, place.k]
        axis = self.axes[stage]
        where[axis] = place.ahead(axis, step)
        for done in self.axes[:stage]:
            where[done] = every
        return self.out.at[self.lead + tuple(where)]

    def local(self):
        return pltpu.make_async_copy(self.mine, self.region(0), self.local_sem)

    def outgoing(self, stage):
        axis = self.axes[stage]
        source = self.mine if stage == 0 else self.region(stage)
        return [
            remote(source, self.region(stage), self.sems.at[0, stage, j], self.sems.at[1, stage, j], self.place.device(axis, j))
            for j in range(1, self.place.sizes[axis])
        ]

    def start(self, stage):
        for copy in self.outgoing(stage):
            copy.start()
        if stage == 0:
            self.local().start()

    def settle(self, stage):
        axis = self.axes[stage]
        if stage == 0:
            self.local().wait()
        for j in range(1, self.place.sizes[axis]):
            block = self.region(stage, self.place.sizes[axis] - j)
            remote(block, block, self.sems.at[0, stage, j], self.sems.at[1, stage, j], self.place.device(axis, j)).wait_recv()

    def drain(self):
        for stage in range(4):
            for copy in self.outgoing(stage):
                copy.wait_send()


def store_flat(ref, base, value):
    rows, columns = value.shape
    width = ref.shape[0] // rows
    for j in range(columns // LANES):
        ref[pl.ds(base + j, rows, stride=width), :] = value[:, j * LANES:(j + 1) * LANES]


def tree_scratch(sizes, flip, rows, columns):
    na, nb, nc, nk = sizes
    one, two = (nb, nc) if flip else (nc, nb)
    shapes = [(na, nb, nc), (nk - 1, na, nb, nc), (one - 1, na, two), (two - 1, na), (na - 1,)]
    return [pltpu.VMEM(shape + (rows, columns), BF16) for shape in shapes] + [
        pltpu.SemaphoreType.DMA((2, 4, max(sizes))),
        pltpu.SemaphoreType.DMA(()),
    ]


class Tree:
    def __init__(self, place, flip, parts, scratch):
        self.place, self.flip, self.parts = place, flip, parts
        self.held, *self.landing, self.sems, self.local_sem = scratch
        order = (3, 1, 2, 0) if flip else (3, 2, 1, 0)
        self.axes = order

    def own(self):
        return pltpu.make_async_copy(self.parts.at[:, :, :, self.place.k], self.held, self.local_sem)

    def outgoing(self, stage):
        place, held = self.place, self.held
        axis = self.axes[stage]
        copies = []
        for j in range(1, place.sizes[axis]):
            other = place.ahead(axis, j)
            if stage == 0:
                source = self.parts.at[:, :, :, other]
            elif stage == 1:
                source = held.at[:, other] if self.flip else held.at[:, :, other]
            elif stage == 2:
                source = held.at[:, place.b, other] if self.flip else held.at[:, other, place.c]
            else:
                source = held.at[other, place.b, place.c]
            copies.append(
                remote(source, self.landing[stage].at[j - 1], self.sems.at[0, stage, j], self.sems.at[1, stage, j], place.device(axis, j))
            )
        return copies

    def start(self, stage):
        if stage == 0:
            self.own().start()
        for copy in self.outgoing(stage):
            copy.start()

    def settle(self, stage, out=None):
        place, held, landing = self.place, self.held, self.landing[stage]
        na, nb, nc, nk = place.sizes
        if stage == 0:
            self.own().wait()
        for copy in self.outgoing(stage):
            copy.wait_recv()
        count = place.sizes[self.axes[stage]] - 1

        def total(own, index):
            value = own.astype(F32)
            for j in range(count):
                value = value + landing[(j,) + index].astype(F32)
            return value

        if stage == 0:
            def add(i, carry):
                held[i] = total(held[i], (i,)).astype(BF16)
                return carry
            lax.fori_loop(0, na, add, 0)
        elif stage == 1:
            two = nc if self.flip else nb
            def add(i, carry):
                for t in range(two):
                    at = (i, place.b, t) if self.flip else (i, t, place.c)
                    held[at] = total(held[at], (i, t)).astype(BF16)
                return carry
            lax.fori_loop(0, na, add, 0)
        elif stage == 2:
            def add(i, carry):
                at = (i, place.b, place.c)
                held[at] = total(held[at], (i,)).astype(BF16)
                return carry
            lax.fori_loop(0, na, add, 0)
        else:
            out(total(held[place.a, place.b, place.c], ()))

    def drain(self):
        for stage in range(4):
            for copy in self.outgoing(stage):
                copy.wait_send()


LOW = 32


def select_rows(chosen, rows_ref):
    return dot_nn(jnp.where(chosen, 1.0, 0.0).astype(BF16), rows_ref[...]).astype(BF16)


def count_true(mask, axis):
    return jnp.sum(jnp.where(mask, 1.0, 0.0), axis=axis, keepdims=True)


def load_flat(ref, base_ref, width, store):
    total = ref.shape[0]
    base_ref[0:total, :] = ref[...].astype(F32)
    per_row = width // LANES
    for j in range(per_row):
        store(j * LANES, base_ref[pl.ds(j, total // per_row, stride=per_row), :].astype(BF16))


def arrive_kernel(sizes, lengths_ref, *refs):
    given, outs, held = refs[:18], refs[18:28], refs[28:46]
    leaving_ref, flat_ref, w4_hbm, wi_own, lines_ref, vec_hbm, load_sems, swap_sems, swap_local, *spread_refs = refs[46:]
    arrived_ref, cot_out, g4, gv, gi, place_row, place_col, rank_out, segment_out, wu_out = outs
    w4_refs, small_refs = held[:4], held[4:13]
    slots_ref, tokens_ref, cot_ref, wi_ref, wu_ref = held[13:]
    loads = [pltpu.make_async_copy(source, target, load_sems.at[i]) for i, (source, target) in enumerate(zip(given, held))]
    for load in loads:
        load.start()
    for load in loads:
        load.wait()
    count = tokens_ref.shape[0]
    devices = slots_ref.shape[0]
    peer_rows = count // devices
    tile = count // 4
    place = Place(sizes)
    me = place.me
    spreads = [
        Spread(place, False, w4_hbm.at[pl.ds(0, 2)], g4, spread_refs[0:2], (pl.ds(0, 2),)),
        Spread(place, True, w4_hbm.at[pl.ds(2, 2)], g4, spread_refs[2:4], (pl.ds(2, 2),)),
        Spread(place, True, vec_hbm, gv, spread_refs[4:6]),
    ]
    half = wi_own.shape[1] // 2
    for i in range(2):
        cut = pl.ds(i * half, half)
        spreads.append(Spread(place, i == 1, wi_own.at[:, cut], gi.at[:, :, :, :, :, cut], spread_refs[6 + 2 * i:8 + 2 * i]))
    swap = Exchange(devices, leaving_ref, arrived_ref, swap_sems, swap_local)
    width = tokens_ref.shape[1]
    for i, ref in enumerate(w4_refs):
        def put(at, value, i=i):
            w4_hbm[i, :, at:at + LANES] = value
        load_flat(ref, flat_ref, width, put)
    def put_inner(at, value):
        wi_own[:, at:at + LANES] = value

    load_flat(wi_ref, flat_ref, wi_own.shape[1], put_inner)
    lines_ref[...] = jnp.zeros_like(lines_ref)
    for i, ref in enumerate(small_refs):
        lines_ref[i:i + 1, 0:ref.shape[1]] = ref[...].astype(F32)
    vec_hbm[...] = lines_ref[...].astype(BF16)
    greet_all(devices)
    for spread in spreads:
        spread.start(0)

    cuts = [(at, slice(at, at + tile)) for at in range(0, count, tile)]
    row_at = [lax.broadcasted_iota(jnp.int32, (tile, count), 0) + at for at, _ in cuts]
    lane = lax.broadcasted_iota(jnp.int32, (tile, count), 1)
    own_row = slots_ref[pl.ds(me, 1), :]
    own_float = own_row.astype(F32)
    own_col = [jnp.sum(jnp.where(lane == row, own_float, 0.0), axis=1, keepdims=True) for row in row_at]
    rank_row = sum(count_true(col < own_float, 0) for col in own_col).astype(jnp.int32)
    for (_, cut), row in zip(cuts, row_at):
        leaving_ref[cut] = select_rows(rank_row == row, tokens_ref)
    swap.start()
    for (_, cut), row, col in zip(cuts, row_at, own_col):
        cot_out[cut] = select_rows(rank_row == row, cot_ref)
        rank_out[cut] = count_true(own_float < col, 1).astype(jnp.int32)

    def put_outer(at, value):
        wu_out[:, at:at + LANES] = value

    load_flat(wu_ref, flat_ref, width, put_outer)
    row = lax.broadcasted_iota(jnp.int32, (count, 1), 0)
    end, segment = 0, jnp.zeros((count, 1), jnp.int32)
    for i in range(lengths_ref.shape[1]):
        end = end + lengths_ref[0, i]
        segment = segment + jnp.where(row >= end, 1, 0)
    segment_out[...] = segment

    high = count // LOW

    def body(s, total):
        local = slots_ref[pl.ds(s, 1), :] - me * count
        in_high = lax.broadcasted_iota(jnp.int32, (high, count), 0) == (local >> 5)
        in_low = lax.broadcasted_iota(jnp.int32, (LOW, count), 0) == (local & (LOW - 1))
        weight = jnp.where(in_high, s.astype(F32), 0.0).astype(BF16)
        return total + dot_nt(weight, jnp.where(in_low, 1.0, 0.0).astype(BF16))

    source = lax.fori_loop(0, devices, body, jnp.zeros((high, LOW), F32)).astype(BF16)
    wide = lax.broadcasted_iota(jnp.int32, (high, count), 1)
    picked = dot_tn(source, jnp.where((wide >> 5) == lax.broadcasted_iota(jnp.int32, (high, count), 0), 1.0, 0.0).astype(BF16))
    low_row = lax.broadcasted_iota(jnp.int32, (LOW, count), 0)
    low_wide = lax.broadcasted_iota(jnp.int32, (LOW, count), 1) & (LOW - 1)
    source_row = jnp.sum(jnp.where(low_row == low_wide, picked, 0.0), axis=0, keepdims=True)
    places = source_row * peer_rows
    for (_, cut), row in zip(cuts, row_at):
        source_col = jnp.sum(jnp.where(lane == row, source_row, 0.0), axis=1, keepdims=True)
        same = source_col == source_row
        place_col[cut] = (source_col * peer_rows + count_true(same & (lane < row), 1)).astype(jnp.int32)
        places = places + count_true(same & (row < lane), 0)
    place_row[...] = places.astype(jnp.int32)

    for stage in range(4):
        for spread in spreads:
            spread.settle(stage)
            if stage < 3:
                spread.start(stage + 1)
    swap.wait()
    for spread in spreads:
        spread.drain()


def arrive(seq_lengths, packed_slot, tokens, cotangent, w4, wi, wu, small):
    devices, count = packed_slot.shape
    width = tokens.shape[1]
    hidden_width = small[-1].shape[0] * devices
    sizes = grid_of(devices)
    share = width // devices
    anywhere = pl.BlockSpec(memory_space=pl.ANY)
    in_vmem = pl.BlockSpec(memory_space=pltpu.VMEM)

    def shape(*dims, dtype=BF16):
        return jax.ShapeDtypeStruct(dims, dtype)

    flat = [w.reshape(-1, LANES) for w in w4]
    given = flat + [x.reshape(1, -1) for x in small] + [packed_slot, tokens, cotangent, wi.reshape(-1, LANES), wu.reshape(-1, LANES)]
    return pl.pallas_call(
        partial(arrive_kernel, sizes),
        out_shape=[shape(count, width), shape(count, width), shape(4, *sizes, share, width), shape(*sizes, 16, LANES),
                   shape(*sizes, share, hidden_width), shape(1, count, dtype=jnp.int32)] + [shape(count, 1, dtype=jnp.int32)] * 3
        + [shape(hidden_width // devices, width)],
        in_specs=[pl.BlockSpec(memory_space=pltpu.SMEM)] + [anywhere] * len(given),
        out_specs=[in_vmem] * 2 + [anywhere] * 3 + [in_vmem] * 5,
        scratch_shapes=[pltpu.VMEM(x.shape, x.dtype) for x in given]
        + [pltpu.VMEM((count, width), BF16), pltpu.VMEM(given[-1].shape, F32), pltpu.VMEM((4, share, width), BF16),
           pltpu.VMEM((share, hidden_width), BF16), pltpu.VMEM((16, LANES), F32), pltpu.VMEM((16, LANES), BF16), pltpu.SemaphoreType.DMA((len(given),)),
           pltpu.SemaphoreType.DMA((2, devices)), pltpu.SemaphoreType.DMA(())] + spread_scratch(sizes) * 5,
        compiler_params=pltpu.CompilerParams(collective_id=1, has_side_effects=True, vmem_limit_bytes=56 * MIB),
        name="arrive",
    )(seq_lengths, *given)


def split3(column):
    high = column.astype(BF16).astype(F32)
    rest = column - high
    mid = rest.astype(BF16).astype(F32)
    return high, mid, rest - mid


def feature_lanes(rows):
    lane = lax.broadcasted_iota(jnp.int32, (rows, LANES), 1)
    return lane < HD, lane & (HD - 1)


def key_features(lane, segment, segments):
    return jnp.where(lane == segment, 1.0, jnp.where((lane >= segments) & (lane < segments + 3), 1.0, 0.0))


def query_features(lane, segment, segments):
    return jnp.where((lane < segments) & (lane != segment), NEG_LARGE, 0.0)


def with_column(features, lane, start, column):
    high, mid, last = split3(column)
    features = jnp.where(lane == start, high, features)
    features = jnp.where(lane == start + 1, mid, features)
    return jnp.where(lane == start + 2, last, features)


def attend_kernel(segments, sizes, cuts, tiles, place_ref, arrived_ref, w4_hbm, vec_ref, seg_ref, wu_hbm, cot_hbm,
                  out_ref, lse_ref, rows_hbm, q_hbm, k_hbm, v_hbm, gu, cot_out,
                  w_ref, rows_ref, q_ref, k_ref, v_ref, k0, k1, load_sem, save_sems, swap_sems, swap_local, *spread_refs):
    count = arrived_ref.shape[0]
    tile = count // tiles
    now, last = pl.program_id(0), pl.num_programs(0) - 1
    place = Place(sizes)
    every = (slice(None),) * 5
    spreads = []
    for i, (base, columns, flip) in enumerate(cuts):
        cut = pl.ds(base, columns)
        spreads.append(Spread(place, flip, wu_hbm.at[:, cut], gu.at[every + (cut,)], spread_refs[2 * i:2 * i + 2]))
    devices = sizes[0] * sizes[1] * sizes[2] * sizes[3]
    swap = Exchange(devices, cot_hbm, cot_out, swap_sems, swap_local, (1, devices // 2))
    load = pltpu.make_async_copy(w4_hbm.at[pl.ds(0, 3)], w_ref, load_sem)
    saves = [
        pltpu.make_async_copy(source, target, save_sems.at[i])
        for i, (source, target) in enumerate(((rows_ref, rows_hbm), (q_ref, q_hbm), (k_ref, k_hbm), (v_ref, v_hbm)))
    ]

    @pl.when(now == 0)
    def _():
        load.start()
        greet_all(devices)
        for spread in spreads[:2]:
            spread.start(0)
        load.wait()

    def hook(at, act):
        @pl.when(now == at)
        def _():
            act()

    def onward(pair, stage, then=None):
        for spread in spreads[2 * pair:2 * pair + 2]:
            spread.settle(stage)
        if then is not None:
            for spread in spreads[2 * then:2 * then + 2]:
                spread.start(0)
        for spread in spreads[2 * pair:2 * pair + 2]:
            if stage < 3:
                spread.start(stage + 1)

    hook(4, lambda: (onward(0, 0, 1), swap.start_remote()))
    hook(9, lambda: (onward(0, 1), onward(1, 0)))
    hook(16, lambda: (onward(0, 2), onward(1, 1)))
    hook(21, lambda: onward(1, 2))

    @pl.when(now < tiles)
    def _():
        cut = pl.ds(pl.multiple_of(now * tile, tile), tile)
        lane = lax.broadcasted_iota(jnp.int32, (tile, count), 1)
        rows = select_rows(place_ref[cut, :] == lane, arrived_ref)
        rows_ref[cut, :] = rows
        vec = vec_ref[...]
        q_ref[cut, :] = ((dot_nn(rows, w_ref[0]) + vec[0:1]).astype(BF16).astype(F32) * 0.125).astype(BF16)
        k_ref[cut, :] = dot_nn(rows, w_ref[1]).astype(BF16)
        v_ref[cut, :] = (dot_nn(rows, w_ref[2]) + vec[1:2]).astype(BF16)

    @pl.when(now == tiles)
    def _():
        for save in saves:
            save.start()

    work = now - tiles
    columns = pl.ds(pl.multiple_of(jnp.maximum(work, 0) // tiles * LANES, LANES), LANES)

    @pl.when((now >= tiles) & (work % tiles == 0))
    def _():
        first_all, lane_all = feature_lanes(count)
        extra = key_features(lane_all, seg_ref[...], segments).astype(BF16)
        keys = k_ref[:, columns]
        k0[...] = jnp.where(first_all, keys, extra)
        k1[...] = jnp.where(first_all, extra, keys)

    @pl.when(now >= tiles)
    def _():
        cut = pl.ds(pl.multiple_of(work % tiles * tile, tile), tile)
        first, lane = feature_lanes(tile)
        extra = query_features(lane, seg_ref[cut, :], segments).astype(BF16)
        queries = q_ref[cut, columns]
        values = v_ref[:, columns]
        outs, logs = [], []
        for mask, keys in ((first, k0), (~first, k1)):
            scores = dot_nt(jnp.where(mask, queries, extra), keys[...])
            top = jnp.max(scores, axis=1, keepdims=True)
            raised = jnp.exp(scores - top)
            total = jnp.sum(raised, axis=1, keepdims=True)
            outs.append(dot_nn(raised.astype(BF16), values) * (1.0 / total))
            logs.append(top + jnp.log(total))
        out_ref[...] = jnp.where(first, outs[0], outs[1]).astype(BF16)
        lse_ref[...] = jnp.where(first, logs[0], logs[1])

    @pl.when(now == last)
    def _():
        onward(0, 3)
        onward(1, 3)
        for spread in spreads:
            spread.drain()
        swap.wait_remote()
        for save in saves:
            save.wait()


def attend(devices, segments, place_col, arrived, w4, vec, segment_col, wu, leaving_cot):
    count, width = arrived.shape
    pairs = width // LANES
    tiles = 4
    tile = count // tiles
    sizes = grid_of(devices)
    anywhere = pl.BlockSpec(memory_space=pl.ANY)
    part = wu.shape[1] // 6
    cuts = [(0, 2 * part, False), (2 * part, 2 * part, True), (4 * part, part, False), (5 * part, part, True)]

    def tile_at(i):
        work = jnp.maximum(i - tiles, 0)
        return work % tiles, work // tiles

    tile_spec = pl.BlockSpec((tile, LANES), tile_at)
    whole = jax.ShapeDtypeStruct((count, width), BF16)
    held = pltpu.VMEM((count, width), BF16)
    return pl.pallas_call(
        partial(attend_kernel, segments, sizes, cuts, tiles),
        grid=(tiles + pairs * tiles,),
        out_shape=[whole, jax.ShapeDtypeStruct((count, width), F32)] + [whole] * 4
        + [jax.ShapeDtypeStruct(sizes + wu.shape, BF16), whole],
        in_specs=[held_spec((count, 1)), held_spec((count, width)), anywhere, held_spec(vec.shape), held_spec((count, 1))] + [anywhere] * 2,
        out_specs=[tile_spec, tile_spec] + [anywhere] * 6,
        scratch_shapes=[pltpu.VMEM((3, width, width), BF16)] + [held] * 4 + [pltpu.VMEM((count, LANES), BF16)] * 2
        + [pltpu.SemaphoreType.DMA(()), pltpu.SemaphoreType.DMA((4,)),
           pltpu.SemaphoreType.DMA((2, devices)), pltpu.SemaphoreType.DMA(())] + spread_scratch(sizes) * len(cuts),
        compiler_params=params(56, "arbitrary", collective_id=4, has_side_effects=True),
        cost_estimate=pl.CostEstimate(flops=8 * count * count * width, bytes_accessed=10 * MIB, transcendentals=count * count * 12),
        name="attend",
    )(place_col, arrived, w4, vec, segment_col, wu, leaving_cot)


def attend_back_kernel(segments, sizes, cuts, seg_ref, q_ref, o_ref, g_ref, lse_ref, seg_all_ref, k_ref, v_ref,
                       wi_ref, wu_ref, wo_ref,
                       dq_ref, dk_ref, dv_ref, sums_ref, wi_out, wu_out, wo_out,
                       k0, k1, v0, v1, dk_sum, dv_sum, *tree_refs):
    count, tile = k_ref.shape[0], q_ref.shape[0]
    first_all, lane_all = feature_lanes(count)
    step, last = pl.program_id(1), pl.num_programs(1) - 1
    now = pl.program_id(0) * pl.num_programs(1) + step

    place = Place(sizes)
    outs = {0: wi_out, 1: wu_out, 2: wo_out}
    every = (slice(None),) * 5
    trees, ends = [], []
    for i, (which, base, columns, flip) in enumerate(cuts):
        parts = (wi_ref, wu_ref, wo_ref)[which].at[every + (pl.ds(base, columns),)]
        trees.append(Tree(place, flip, parts, tree_refs[7 * i:7 * i + 7]))
        ends.append(partial(store_flat, outs[which], base // LANES))

    @pl.when(now == 0)
    def _():
        greet_peers(place)
        for tree in trees[:3]:
            tree.start(0)

    groups = (slice(0, 3), slice(3, 5), slice(5, 7))

    def onward(group, stage, then=None):
        for tree, end in zip(trees[groups[group]], ends[groups[group]]):
            tree.settle(stage, end)
            if stage < 3:
                tree.start(stage + 1)
        if then is not None:
            for tree in trees[groups[then]]:
                tree.start(0)

    def hook(at, act):
        @pl.when(now == at)
        def _():
            act()

    hook(2, lambda: onward(0, 0, 1))
    hook(7, lambda: (onward(0, 1), onward(1, 0, 2)))
    hook(10, lambda: onward(0, 2))
    hook(15, lambda: (onward(1, 1), onward(2, 0)))
    hook(18, lambda: onward(0, 3))
    hook(19, lambda: (onward(1, 2), onward(2, 1)))
    hook(22, lambda: onward(2, 2))

    @pl.when(step == 0)
    def _():
        extra = key_features(lane_all, seg_all_ref[...], segments).astype(BF16)
        k0[...] = jnp.where(first_all, k_ref[...], extra)
        k1[...] = jnp.where(first_all, extra, k_ref[...])
        v0[...] = jnp.where(first_all, v_ref[...], extra)
        v1[...] = jnp.where(first_all, extra, v_ref[...])
        dk_sum[...] = jnp.zeros_like(dk_sum)
        dv_sum[...] = jnp.zeros_like(dv_sum)
        sums_ref[...] = jnp.zeros_like(sums_ref)

    first, lane = feature_lanes(tile)
    hidden = query_features(lane, seg_ref[...], segments)
    queries, grads = q_ref[...], g_ref[...]
    product = grads.astype(F32) * o_ref[...].astype(F32)
    lses = lse_ref[...]
    dqs, dks, dvs = [], [], []
    for mask, keys, values, at in ((first, k0, v0, 0), (~first, k1, v1, HD)):
        lse = lses[:, at:at + 1]
        delta = jnp.sum(jnp.where(mask, product, 0.0), axis=1, keepdims=True)
        query = jnp.where(mask, queries, with_column(hidden, lane, segments, -lse).astype(BF16))
        grad = jnp.where(mask, grads, with_column(jnp.zeros_like(hidden), lane, segments, -delta).astype(BF16))
        probs = jnp.exp(dot_nt(keys[...], query))
        score = (probs * dot_nt(values[...], grad)).astype(BF16)
        dvs.append(dot_nn(probs.astype(BF16), grad))
        dks.append(dot_nn(score, query))
        dqs.append(dot_tn(score, keys[...]))
    dq = (jnp.where(first, dqs[0], dqs[1]) * 0.125).astype(BF16)
    dq_ref[...] = dq
    dk_sum[...] += jnp.where(first_all, dks[0], dks[1])
    dv_sum[...] += jnp.where(first_all, dvs[0], dvs[1])
    sums_ref[0:1, :] += jnp.sum(dq.astype(F32), axis=0, keepdims=True)

    @pl.when(step == last)
    def _():
        dk_ref[...] = dk_sum[...].astype(BF16)
        dv = dv_sum[...].astype(BF16)
        dv_ref[...] = dv
        sums_ref[1:2, :] += jnp.sum(dv.astype(F32), axis=0, keepdims=True)

    @pl.when(now == pl.num_programs(0) * pl.num_programs(1) - 1)
    def _():
        onward(1, 3)
        onward(2, 3)
        for tree in trees:
            tree.drain()


def attend_back(segments, segment_col, q, out, grad, lse, k, v, wi, wu, wo):
    count, width = q.shape
    pairs = width // LANES
    tile = count // 4
    devices = wi.shape[0]
    sizes = grid_of(devices)
    tile_spec = pl.BlockSpec((tile, LANES), lambda h, i: (i, h))
    all_spec = pl.BlockSpec((count, LANES), lambda h, i: (0, h))
    anywhere = pl.BlockSpec(memory_space=pl.ANY)
    parts = [x.reshape(sizes + x.shape[1:]) for x in (wi, wu, wo)]
    cuts, part = [], wi.shape[2] // 6
    for base, size in ((0, 2), (2, 3), (5, 1)):
        cuts.append((0, base * part, size * part, False))
        cuts.append((1, base * wu.shape[2] // 6, size * wu.shape[2] // 6, True))
        if base == 0:
            cuts.append((2, 0, wo.shape[2], False))
    trees = []
    for which, _, columns, flip in cuts:
        trees += tree_scratch(sizes, flip, (wi, wu, wo)[which].shape[1], columns)
    flats = [(x.shape[1] * x.shape[2] // LANES, LANES) for x in (wi, wu, wo)]
    return pl.pallas_call(
        partial(attend_back_kernel, segments, sizes, cuts),
        grid=(pairs, 4),
        out_shape=[jax.ShapeDtypeStruct((count, width), BF16)] * 3
        + [jax.ShapeDtypeStruct((8, width), F32)]
        + [jax.ShapeDtypeStruct(flat, F32) for flat in flats],
        in_specs=[pl.BlockSpec((tile, 1), lambda h, i: (i, 0))] + [tile_spec] * 4 + [held_spec((count, 1)), all_spec, all_spec]
        + [anywhere] * 3,
        out_specs=[tile_spec, all_spec, all_spec, pl.BlockSpec((8, LANES), lambda h, i: (0, h))]
        + [full_spec(flat) for flat in flats],
        scratch_shapes=[pltpu.VMEM((count, LANES), BF16)] * 4 + [pltpu.VMEM((count, LANES), F32)] * 2
        + trees,
        compiler_params=params(60, "arbitrary", "arbitrary", collective_id=2, has_side_effects=True),
        cost_estimate=pl.CostEstimate(flops=20 * count * count * width, bytes_accessed=16 * MIB, transcendentals=count * count * 12),
        name="attend_back",
    )(segment_col, q, out, grad, lse, segment_col, k, v, *parts)


def normalize(hidden):
    centered = hidden - jnp.mean(hidden, axis=1, keepdims=True)
    variance = jnp.mean(centered * centered, axis=1, keepdims=True)
    inverse = lax.rsqrt(variance + EPSILON)
    return centered * inverse, inverse


def normalize_back(grad, normal, inverse):
    return inverse * (
        grad
        - jnp.mean(grad, axis=1, keepdims=True)
        - normal * jnp.mean(grad * normal, axis=1, keepdims=True)
    )


def column_sum(matrix):
    return jnp.sum(matrix.astype(F32), axis=0, keepdims=True)


def feed_kernel(sizes, tiles, chunk, where_ref, place_ref, rows_hbm, att_hbm, cot_hbm, early_hbm, w4_hbm, wi_hbm, wu_hbm, vec_ref, bi_ref,
                first_ref, agrad_ref, returned_hbm, dwi_ref, dwu_ref, dwo_ref, sums_ref, bisum_ref,
                act_ref, inner_ref, slope_ref, turned_ref, outer_ref, low_ref, normal1_ref, normal2_ref, inverse1_ref, inverse2_ref,
                cot_ref, result_ref, leaving_ref, rows_ref, att_ref, wo_ref, wi_ref, wu_ref, load_sems, early_sems, swap_sems, swap_local):
    count = att_ref.shape[0]
    tile = count // tiles
    hidden_width = wi_ref.shape[1]
    devices = sizes[0] * sizes[1] * sizes[2] * sizes[3]
    step, last = pl.program_id(0), pl.num_programs(0) - 1
    vec = vec_ref[...]
    bo, ga, sa, bu, gf, sf = (vec[i:i + 1] for i in range(2, 8))
    enter = Exchange(devices, cot_hbm, cot_ref, swap_sems.at[0], swap_local.at[0], (devices // 2, devices))
    early = Exchange(devices, early_hbm, cot_ref, None, None, (1, devices // 2))
    loads = [
        pltpu.make_async_copy(source, target, load_sems.at[i])
        for i, (source, target) in enumerate((
            (att_hbm, att_ref), (w4_hbm.at[3], wo_ref), (rows_hbm, rows_ref), (wi_hbm, wi_ref), (wu_hbm, wu_ref)
        ))
    ]

    def early_block(j):
        peer = (early.me + devices - j) % devices
        return pltpu.make_async_copy(early.block(early_hbm, peer), early.block(cot_ref, peer), early_sems.at[j])

    leave = Exchange(devices, leaving_ref, returned_hbm, swap_sems.at[1], swap_local.at[1])

    @pl.when(step == 0)
    def _():
        for load in loads:
            load.start()
        greet_all(devices)
        enter.start()
        early.over(lambda j: early_block(j).start())
        sums_ref[...] = jnp.zeros_like(sums_ref)
        bisum_ref[...] = jnp.zeros_like(bisum_ref)
        for load in loads:
            load.wait()

    @pl.when(step < tiles)
    def _():
        cut = pl.ds(pl.multiple_of(step * tile, tile), tile)
        first_sum = rows_ref[cut, :].astype(F32) + dot_nn(att_ref[cut, :], wo_ref[...]) + bo
        normal1, inverse1 = normalize(first_sum)
        normal1_ref[cut, :] = normal1
        inverse1_ref[cut, :] = inverse1
        normed = normal1 * ga + sa
        normed_low = normed.astype(BF16)
        turned_ref[:, cut] = normed.T.astype(BF16)
        second = normed + bu
        for at in range(0, hidden_width, chunk):
            pre = dot_nn(normed_low, wi_ref[:, at:at + chunk]) + bi_ref[:, at:at + chunk]
            share = 0.5 + 0.5 * lax.erf(pre * 0.7071067811865476)
            act = (pre * share).astype(BF16)
            act_ref[cut, at:at + chunk] = act
            slope_ref[cut, at:at + chunk] = (share + pre * (jnp.exp(pre * pre * -0.5) * 0.3989422804014327)).astype(BF16)
            second = second + dot_nn(act, wu_ref[at:at + chunk, :])
        normal2, inverse2 = normalize(second)
        normal2_ref[cut, :] = normal2
        inverse2_ref[cut, :] = inverse2
        result_ref[cut, :] = (normal2 * gf + sf).astype(BF16)

    @pl.when(step == tiles)
    def _():
        for at in range(0, count, tile):
            target = lax.broadcasted_iota(jnp.int32, (tile, count), 0) + at
            leaving_ref[at:at + tile] = select_rows(where_ref[...] == target, result_ref)
        early.over(lambda j: early_block(j).wait())
        enter.wait()
        leave.start()

    @pl.when((step >= tiles) & (step < 2 * tiles))
    def _():
        cut = pl.ds(pl.multiple_of((step - tiles) * tile, tile), tile)
        lane = lax.broadcasted_iota(jnp.int32, (tile, count), 1)
        chosen = jnp.where(place_ref[...] == lane, 1.0, 0.0).astype(BF16)
        cot = dot_nn(chosen, cot_ref[...])
        normal1, normal2 = normal1_ref[cut, :], normal2_ref[cut, :]
        second_grad = normalize_back(cot * gf, normal2, inverse2_ref[cut, :])
        outer_low = second_grad.astype(BF16)
        outer_ref[cut, :] = outer_low
        normed_grad = second_grad
        for at in range(0, hidden_width, chunk):
            act_grad = dot_nt(outer_low, wu_ref[at:at + chunk, :])
            inner_low = (act_grad * slope_ref[cut, at:at + chunk].astype(F32)).astype(BF16)
            inner_ref[cut, at:at + chunk] = inner_low
            bisum_ref[0:1, at:at + chunk] += column_sum(inner_low)
            normed_grad = normed_grad + dot_nt(inner_low, wi_ref[:, at:at + chunk])
        first_grad = normalize_back(normed_grad * ga, normal1, inverse1_ref[cut, :])
        first_ref[...] = first_grad
        branch_low = first_grad.astype(BF16)
        low_ref[cut, :] = branch_low
        agrad_ref[...] = dot_nt(branch_low, wo_ref[...]).astype(BF16)
        sums_ref[2:3, :] += column_sum(branch_low)
        sums_ref[3:4, :] += column_sum(normed_grad * normal1)
        sums_ref[4:5, :] += column_sum(normed_grad)
        sums_ref[5:6, :] += column_sum(outer_low)
        sums_ref[6:7, :] += column_sum(cot * normal2)
        sums_ref[7:8, :] += column_sum(cot)

    @pl.when(step >= 2 * tiles)
    def _():
        cut = pl.ds(pl.multiple_of((step - 2 * tiles) * chunk, chunk), chunk)
        dwi_ref[...] = dot_nn(turned_ref[...], inner_ref[:, cut]).astype(BF16)
        dwu_ref[...] = dot_tn(act_ref[:, cut], outer_ref[...]).astype(BF16)

    @pl.when(step == last)
    def _():
        dwo_ref[...] = dot_tn(att_ref[...], low_ref[...]).astype(BF16)
        leave.wait()


def feed_forward(devices, place_row, place_col, rows, attended, leaving_cot, early_cot, w4, wi, wu, vec, bi):
    count, width = rows.shape
    hidden_width = wi.shape[1]
    tiles, chunk = 4, 512
    tile = count // tiles
    anywhere = pl.BlockSpec(memory_space=pl.ANY)
    back_spec = pl.BlockSpec((tile, width), lambda i: (jnp.clip(i - tiles, 0, tiles - 1), 0))
    parts = hidden_width // chunk

    def part(i):
        return jnp.clip(i - 2 * tiles, 0, parts - 1)

    def held(n, dtype=BF16):
        return pltpu.VMEM((count, n), dtype)

    return pl.pallas_call(
        partial(feed_kernel, grid_of(devices), tiles, chunk),
        grid=(2 * tiles + parts,),
        out_shape=[
            jax.ShapeDtypeStruct((count, width), F32), jax.ShapeDtypeStruct((count, width), BF16), jax.ShapeDtypeStruct((count, width), BF16),
            jax.ShapeDtypeStruct((width, hidden_width), BF16), jax.ShapeDtypeStruct((hidden_width, width), BF16),
            jax.ShapeDtypeStruct((width, width), BF16), jax.ShapeDtypeStruct((8, width), F32), jax.ShapeDtypeStruct((8, hidden_width), F32),
        ],
        in_specs=[
            held_spec((1, count)), pl.BlockSpec((tile, 1), lambda i: (jnp.clip(i - tiles, 0, tiles - 1), 0)),
            anywhere, anywhere, anywhere, anywhere, anywhere, anywhere, anywhere, held_spec(vec.shape), held_spec(bi.shape),
        ],
        out_specs=[
            back_spec, back_spec, anywhere,
            pl.BlockSpec((width, chunk), lambda i: (0, part(i))), pl.BlockSpec((chunk, width), lambda i: (part(i), 0)),
            full_spec((width, width)), full_spec((8, width)), full_spec((8, hidden_width)),
        ],
        scratch_shapes=[
            held(hidden_width), held(hidden_width), held(hidden_width), pltpu.VMEM((width, count), BF16), held(width), held(width),
            held(width, F32), held(width, F32), held(1, F32), held(1, F32), held(width), held(width), held(width),
            held(width), held(width), pltpu.VMEM((width, width), BF16), pltpu.VMEM(wi.shape, BF16), pltpu.VMEM(wu.shape, BF16),
            pltpu.SemaphoreType.DMA((5,)), pltpu.SemaphoreType.DMA((devices,)), pltpu.SemaphoreType.DMA((2, 2, devices)), pltpu.SemaphoreType.DMA((2,)),
        ],
        compiler_params=params(62, "arbitrary", collective_id=5, has_side_effects=True),
        cost_estimate=pl.CostEstimate(flops=20 * count * width * hidden_width, bytes_accessed=36 * MIB, transcendentals=2 * count * hidden_width),
        name="feed_forward",
    )(place_row, place_col, rows, attended, leaving_cot, early_cot, w4, wi, wu, vec, bi)


def finish_kernel(sizes, share, where_ref, rank_ref, first_hbm, dq_hbm, dk_hbm, dv_hbm, w4_hbm, rows_hbm, returned_hbm, sums_ref, more_ref, bisum_ref,
                  layer_ref, back_ref, wq_out, wk_out, wv_out, *refs):
    finish_body(sizes, share, where_ref, rank_ref, first_hbm, dq_hbm, dk_hbm, dv_hbm, w4_hbm, rows_hbm, returned_hbm, sums_ref, more_ref, bisum_ref,
                layer_ref, back_ref, wq_out, wk_out, wv_out, refs[:9], *refs[9:])


def finish_body(sizes, share, where_ref, rank_ref, first_hbm, dq_hbm, dk_hbm, dv_hbm, w4_hbm, rows_hbm, returned_hbm, sums_ref, more_ref, bisum_ref,
                  layer_ref, back_ref, wq_out, wk_out, wv_out, small_outs,
                  first_ref, dq_ref, dk_ref, dv_ref, w_ref, rows_ref, returned_ref, load_sems,
                  total_ref, leaving_ref, wq_ref, wk_ref, wv_ref, lines_ref, small_ref, swap_sems, swap_local, *tree_refs):
    count, width = total_ref.shape
    devices = sizes[0] * sizes[1] * sizes[2] * sizes[3]
    na, nb, nc, nk = sizes
    tile = count // 4
    loads = [
        pltpu.make_async_copy(source, target, load_sems.at[i])
        for i, (source, target) in enumerate((
            (first_hbm, first_ref), (dq_hbm, dq_ref), (w4_hbm.at[pl.ds(0, 3)], w_ref), (dk_hbm, dk_ref), (dv_hbm, dv_ref),
            (rows_hbm, rows_ref), (returned_hbm, returned_ref),
        ))
    ]
    for load in loads:
        load.start()
    place = Place(sizes)
    swap = Exchange(devices, leaving_ref, back_ref, swap_sems, swap_local)
    parts = (wq_ref, wk_ref, wv_ref, small_ref)
    trees = [Tree(place, flip, ref, tree_refs[7 * i:7 * i + 7]) for i, (flip, ref) in enumerate(zip((False, True, False, True), parts))]
    greet_all(devices)
    for load in loads[:5]:
        load.wait()
    for at in range(0, count, tile):
        cut = slice(at, at + tile)
        total_ref[cut] = (
            first_ref[cut] + dot_nt(dq_ref[cut], w_ref[0]) + dot_nt(dk_ref[cut], w_ref[1]) + dot_nt(dv_ref[cut], w_ref[2])
        ).astype(BF16)
    for at in range(0, count, tile):
        target = lax.broadcasted_iota(jnp.int32, (tile, count), 0) + at
        chosen = jnp.where(where_ref[...] == target, 1.0, 0.0).astype(BF16)
        leaving_ref[at:at + tile] = dot_nn(chosen, total_ref[...]).astype(BF16)
    swap.start()

    def by_device(line, share):
        count = line.shape[1]
        start = lax.broadcasted_iota(jnp.int32, (devices, count), 0) * share
        lane = lax.broadcasted_iota(jnp.int32, (devices, count), 1)
        left = jnp.where((lane >= start) & (lane < start + share), line, 0.0).astype(BF16)
        at = lax.broadcasted_iota(jnp.int32, (count, LANES), 0).astype(F32)
        inside = at - jnp.floor((at + 0.5) * (1.0 / share)) * share
        right = jnp.where(inside == lax.broadcasted_iota(jnp.int32, (count, LANES), 1).astype(F32), 1.0, 0.0).astype(BF16)
        return dot_nn(left, right)

    lines_ref[...] = jnp.zeros_like(lines_ref)
    for i in range(8):
        lines_ref[i] = by_device(sums_ref[i:i + 1, :] + more_ref[i:i + 1, :], share)
    lines_ref[8] = by_device(bisum_ref[0:1, :], bisum_ref.shape[1] // devices)
    for d in range(devices):
        index = (d // (nk * nc * nb), d // (nk * nc) % nb, d // nk % nc, d % nk)
        small_ref[index] = lines_ref[:, d, :].astype(BF16)
    trees[3].start(0)
    loads[5].wait()
    group = 3 * LANES
    for grad_ref, out_ref, tree in zip((dq_ref, dk_ref, dv_ref), parts, trees):
        for at in range(0, width, group):
            value = dot_tn(rows_ref[:, at:at + group], grad_ref[...])
            for i in range(group // share):
                d = at // share + i
                index = (d // (nk * nc * nb), d // (nk * nc) % nb, d // nk % nc, d % nk)
                out_ref[index] = value[i * share:(i + 1) * share].astype(BF16)
        tree.start(0)
    loads[6].wait()

    def restore(out_ref, from_ref):
        for at in range(0, count, tile):
            lane = lax.broadcasted_iota(jnp.int32, (tile, count), 1)
            chosen = jnp.where(rank_ref[at:at + tile] == lane, 1.0, 0.0).astype(BF16)
            out_ref[at:at + tile] = dot_nn(chosen, from_ref[...]).astype(BF16)

    for stage in range(3):
        for tree in trees:
            tree.settle(stage)
            tree.start(stage + 1)
        if stage == 0:
            restore(layer_ref, returned_ref)
    for tree, out in zip(trees, (wq_out, wk_out, wv_out)):
        tree.settle(3, partial(store_flat, out, 0))

    def store_small(value):
        for i, out in enumerate(small_outs):
            out[...] = value[i:i + 1, :out.shape[1]]

    trees[3].settle(3, store_small)
    swap.wait()
    for tree in trees:
        tree.drain()


def emit_kernel(rank_ref, back_hbm, *refs):
    count = (len(refs) - 3) // 2
    given, tokens_ref, outs, (back_ref, sems) = refs[:count], refs[count], refs[count + 1:2 * count + 1], refs[2 * count + 1:]
    load = pltpu.make_async_copy(back_hbm, back_ref, sems.at[count])
    load.start()
    copies = [pltpu.make_async_copy(source, target, sems.at[i]) for i, (source, target) in enumerate(zip(given, outs))]
    for copy in copies:
        copy.start()
    load.wait()
    rows = back_ref.shape[0]
    tile = rows // 4
    for at in range(0, rows, tile):
        lane = lax.broadcasted_iota(jnp.int32, (tile, rows), 1)
        tokens_ref[at:at + tile] = select_rows(rank_ref[at:at + tile] == lane, back_ref)
    for copy in copies:
        copy.wait()


def emit(rank_col, back, others):
    anywhere = pl.BlockSpec(memory_space=pl.ANY)
    in_vmem = pl.BlockSpec(memory_space=pltpu.VMEM)
    return pl.pallas_call(
        emit_kernel,
        out_shape=[jax.ShapeDtypeStruct(x.shape, x.dtype) for x in (back, *others)],
        in_specs=[in_vmem] + [anywhere] * (1 + len(others)),
        out_specs=[in_vmem] * (1 + len(others)),
        scratch_shapes=[pltpu.VMEM(back.shape, BF16), pltpu.SemaphoreType.DMA((len(others) + 1,))],
        compiler_params=pltpu.CompilerParams(vmem_limit_bytes=56 * MIB),
        name="emit",
    )(rank_col, back, *others)


def finish(devices, place_row, rank_col, first_grad, dq, dk, dv, w4, rows, returned, sums, more, bi_sum):
    count, width = dq.shape
    sizes = grid_of(devices)
    share = width // devices
    anywhere = pl.BlockSpec(memory_space=pl.ANY)
    in_vmem = pl.BlockSpec(memory_space=pltpu.VMEM)
    whole = pltpu.VMEM((count, width), BF16)
    trees = []
    for flip, shape in zip((False, True, False, True), ((share, width),) * 3 + ((16, LANES),)):
        trees += tree_scratch(sizes, flip, *shape)
    return pl.pallas_call(
        partial(finish_kernel, sizes, share),
        out_shape=[jax.ShapeDtypeStruct((count, width), BF16)] * 2
        + [jax.ShapeDtypeStruct((share * width // LANES, LANES), F32)] * 3
        + [jax.ShapeDtypeStruct((1, share), F32)] * 8 + [jax.ShapeDtypeStruct((1, bi_sum.shape[1] // devices), F32)],
        in_specs=[in_vmem] * 2 + [anywhere] * 7 + [in_vmem] * 3,
        out_specs=[in_vmem] * 14,
        scratch_shapes=[pltpu.VMEM((count, width), F32)] + [whole] * 3 + [pltpu.VMEM((3, width, width), BF16)] + [whole] * 2
        + [pltpu.SemaphoreType.DMA((7,))] + [whole] * 2 + [pltpu.VMEM(sizes + (share, width), BF16)] * 3
        + [pltpu.VMEM((16, devices, LANES), F32), pltpu.VMEM(sizes + (16, LANES), BF16)]
        + [pltpu.SemaphoreType.DMA((2, devices)), pltpu.SemaphoreType.DMA(())] + trees,
        compiler_params=pltpu.CompilerParams(collective_id=3, has_side_effects=True, vmem_limit_bytes=60 * MIB),
        name="finish",
    )(place_row, rank_col, first_grad, dq, dk, dv, w4, rows, returned, sums, more, bi_sum)


def on_device(tokens, cotangent, packed_slot, seq_lengths, query_weight, query_bias, key_weight, value_weight,
              value_bias, output_weight, output_bias, attention_gain, attention_shift, inner_weight, inner_bias,
              outer_weight, outer_bias, final_gain, final_shift):
    devices = lax.axis_size("fsdp")
    count, width = tokens.shape
    hidden_width = inner_bias.shape[0] * devices
    segments = seq_lengths.shape[1]
    share = width // devices
    small = (query_bias, value_bias, output_bias, attention_gain, attention_shift, outer_bias, final_gain, final_shift, inner_bias)
    arrived, leaving_cot, g4, gv, gi, place_row, place_col, rank_col, segment_col, wu_own = arrive(
        seq_lengths, packed_slot.reshape(devices, count), tokens, cotangent,
        (query_weight, key_weight, value_weight, output_weight), inner_weight, outer_weight, small,
    )
    w4 = g4.reshape(4, width, width)
    flat = gv.reshape(devices, 16, LANES).astype(F32)
    vec = flat[:, :8, :share].transpose(1, 0, 2).reshape(8, width)
    bi = flat[:, 8, :hidden_width // devices].reshape(1, hidden_width)

    attended, lse, rows, q, k, v, gu, early_cot = attend(devices, segments, place_col, arrived, w4, vec, segment_col, wu_own, leaving_cot)
    wi = gi.reshape(width, hidden_width)
    wu = gu.reshape(hidden_width, width)
    first_grad, attended_grad, returned, inner_grad, outer_grad, wo_grad, sums, bi_sum = feed_forward(
        devices, place_row, place_col, rows, attended, leaving_cot, early_cot, w4, wi, wu, vec, bi
    )
    inner_grad, outer_grad, wo_grad = (x.reshape(devices, -1, x.shape[-1]) for x in (inner_grad, outer_grad, wo_grad))
    dq, dk, dv, more, inner_grad, outer_grad, wo_grad = attend_back(
        segments, segment_col, q, attended, attended_grad, lse, k, v, inner_grad, outer_grad, wo_grad
    )
    layer_out, back, wq_grad, wk_grad, wv_grad, *small = finish(
        devices, place_row, rank_col, first_grad, dq, dk, dv, w4, rows, returned, sums, more, bi_sum
    )
    tokens_grad, layer_out, wq_grad, wk_grad, wv_grad, wo_grad, inner_grad, outer_grad, *small = emit(
        rank_col, back, (layer_out, wq_grad, wk_grad, wv_grad, wo_grad, inner_grad, outer_grad, *small)
    )
    wq_grad, wk_grad, wv_grad, wo_grad, wi_grad, wu_grad = (
        x.reshape(-1) for x in (wq_grad, wk_grad, wv_grad, wo_grad, inner_grad, outer_grad)
    )
    bq, bv, bo, ga, sa, bu, gf, sf, bi = (x.reshape(-1) for x in small)
    return (layer_out, tokens_grad, wq_grad, bq, wk_grad, wv_grad, bv, wo_grad, bo, ga, sa, wi_grad, bi, wu_grad, bu, gf, sf)


def solution(mesh):
    split, rows = P("fsdp"), P("fsdp", None)
    return jax.shard_map(
        on_device,
        mesh=mesh,
        in_specs=(rows, rows, P(), rows) + (split,) * 15,
        out_specs=(rows, rows) + (split,) * 15,
        check_vma=False,
    )
```

time: 496 us -> 378 us (0.76)
  waiting for transfers between devices: 34.5 us -> 0 us
  local copies, waits for them, and re-layouts: 34.4 us -> 3.04 us
  matrix products: 21.1 us -> 0 us
  Pallas kernels: 382 us -> 365 us
  starting transfers between devices: 11.2 us -> 0 us
    all_to_all x2 -> x0, waiting for transfers between devices: 34.5 us -> none  [exchange(): lax.all_to_all(pieces, 'fsdp', split_axis=0, concat_axis=0, tiled=True)]
    dot_general x3 -> x0, matrix products: 21.1 us -> none  [dot_tn(): lax.dot_general(a, b, (((0,), (0,)), ((), ())), preferred_element_type=F32)]
    unnamed x91 -> x1, local copies, waits for them, and re-layouts: 17.8 us -> 0.03 us
    pallas_call x9 -> x5, Pallas kernels: 319 us -> 304 us  [the longest x1 90.8 us: arrive(): pl.pallas_call(partial(arrive_kernel, sizes), out_shape=[shape(count, wid...]
    all_to_all x2 -> x0, starting transfers between devices: 11.2 us -> none  [exchange(): lax.all_to_all(pieces, 'fsdp', split_axis=0, concat_axis=0, tiled=True)]
    reshape x15 -> x2, local copies, waits for them, and re-layouts: 10.5 us -> 2.31 us  [the longest x1 1.59 us: on_device(): packed_slot.reshape(devices, count)]
  transfers between devices with their start and end apart: 2 -> 0, of which waited for: 1 -> 0; matrix products, arithmetic and copies ran while one was open for 2% -> 0% of each run, Pallas kernels for 34% -> 0%
where the time goes in v3:
time: 378 us; the launch traced here: 370 us
  Pallas kernels  365 us (97%)
    pallas_call x1, Pallas kernels, arrive(): pl.pallas_call(partial(arrive_kernel, sizes), out_shape=[shape(count, wid...  90.8 us
    pallas_call x1, Pallas kernels, attend_back(): pl.pallas_call(partial(attend_back_kernel, segments, sizes, cuts), grid=(...  73.4 us
    pallas_call x1, Pallas kernels, attend(): pl.pallas_call(partial(attend_kernel, segments, sizes, cuts, tiles), grid...  66.9 us
    pallas_call x1, Pallas kernels, feed_forward(): pl.pallas_call(partial(feed_kernel, grid_of(devices), tiles, chunk), grid...  66.5 us
    pallas_call x1, Pallas kernels, finish(): pl.pallas_call(partial(finish_kernel, sizes, share), out_shape=[jax.Shape...  61 us

profile of v3, /device:TPU:0, one launch (start us, length us, event | category | flops | bytes accessed | tf_op | source)
XLA Modules:
  0.0 370.3 jit_solution(5704566043848612043)
XLA Ops:
  0.7 1.6 reshape.155.refs_13_
  2.2 90.8 %arrive.1 = (bf16[1024,768]{1,0:T(8,128)(2,1)}, bf16[1024,768]{1,0:T(8,128)(2,1)}, bf16[4,4,2,2,2,24,768]{6,5,4,3,2,1,0:T(8,128)(2,1)}, bf16[4,2,2,2,16,128]{5,4...) custom-call(s32[1,4]{1,0:T(1,128)} %lengths_ref.1, ...), custom_call_target="tpu_custom_call" | custom-call | tf_op jit(solution)/shard_map/arrive/pallas_call | solution.py:424
  93.1 0.9 bitcast_convert_fusion
  94.1 0.7 reshape.159.vec_ref
  94.8 0.7 reshape_squeeze.3.bi_ref
  95.5 66.9 %attend.1 = (bf16[1024,768]{1,0:T(8,128)(2,1)}, f32[1024,768]{1,0:T(8,128)}, bf16[1024,768]{1,0:T(8,128)(2,1)}, bf16[1024,768]{1,0:T(8,128)(2,1)}, bf16[1024,768...) custom-call(s32[1024,1]{1,0:T(8,128)} %get-tuple-element.83.place_re, ...), custom_call_target="tpu_custom_call" | custom-call | flops 6442450944 | bytes 10485760 | tf_op jit(solution)/shard_map/attend/pallas_call | solution.py:588
  162.4 66.5 %feed_forward.1 = (f32[1024,768]{1,0:T(8,128)}, bf16[1024,768]{1,0:T(8,128)(2,1)}, bf16[1024,768]{1,0:T(8,128)(2,1)}, bf16[768,3072]{1,0:T(8,128)(2,1)}, bf16[30...) custom-call(s32[1,1024]{1,0:T(1,128)} %get-tuple-element.82.where_ref, ...), custom_call_target="tpu_custom_call" | custom-call | flops 48318382080 | bytes 37748736 | tf_op jit(solution)/shard_map/feed_forward/pallas_call | solution.py:883
  228.9 73.4 %attend_back.1 = (bf16[1024,768]{1,0:T(8,128)(2,1)}, bf16[1024,768]{1,0:T(8,128)(2,1)}, bf16[1024,768]{1,0:T(8,128)(2,1)}, f32[8,768]{1,0:T(8,128)}, f32[576,128...) custom-call(s32[1024,1]{1,0:T(8,128)} %get-tuple-element.87.seg_ref.seg_all_ref, ...), custom_call_target="tpu_custom_call" | custom-call | flops 16106127360 | bytes 16777216 | tf_op jit(solution)/shard_map/attend_back/pallas_call | solution.py:720
  302.3 61.0 %finish.1 = (bf16[1024,768]{1,0:T(8,128)(2,1)}, bf16[1024,768]{1,0:T(8,128)(2,1)}, f32[144,128]{1,0:T(8,128)}, f32[144,128]{1,0:T(8,128)}, f32[144,128]{1,0:T(8,...) custom-call(s32[1,1024]{1,0:T(1,128)} %get-tuple-element.82.where_re, ...), custom_call_target="tpu_custom_call" | custom-call | tf_op jit(solution)/shard_map/finish/pallas_call | solution.py:1050
  363.3 6.5 %emit.1 = (bf16[1024,768]{1,0:T(8,128)(2,1)}, bf16[1024,768]{1,0:T(8,128)(2,1)}, f32[144,128]{1,0:T(8,128)}, f32[144,128]{1,0:T(8,128)}, f32[144,128]{1,0:T(8,12...) custom-call(s32[1024,1]{1,0:T(8,128)} %get-tuple-element.81.rank_ref, ...), custom_call_target="tpu_custom_call" | custom-call | tf_op jit(solution)/shard_map/emit/pallas_call | solution.py:1029
  (3 shorter events, 0.0 us)

commit v4 on v3

v4 whole, which is shorter than its diff:
```python
from functools import partial

import jax
import jax.numpy as jnp
from jax import lax
from jax.experimental import pallas as pl
from jax.experimental.pallas import tpu as pltpu
from jax.sharding import PartitionSpec as P

HD = 64
LANES = 128
EPSILON = 1e-12
NEG_LARGE = -1e30
MIB = 1 << 20
F32 = jnp.float32
BF16 = jnp.bfloat16
MESH = pl.DeviceIdType.MESH


def dot_nn(a, b):
    return lax.dot_general(a, b, (((1,), (0,)), ((), ())), preferred_element_type=F32)


def dot_nt(a, b):
    return lax.dot_general(a, b, (((1,), (1,)), ((), ())), preferred_element_type=F32)


def dot_tn(a, b):
    return lax.dot_general(a, b, (((0,), (0,)), ((), ())), preferred_element_type=F32)


def full_spec(shape, **kw):
    return pl.BlockSpec(shape, lambda *_: (0,) * len(shape), **kw)


def held_spec(shape):
    return full_spec(shape, pipeline_mode=pl.Buffered(1))


def params(mib, *axes, **kw):
    return pltpu.CompilerParams(
        dimension_semantics=axes or None, vmem_limit_bytes=mib * MIB, **kw
    )


def grid_of(devices):
    return {32: (4, 2, 2, 2), 128: (4, 4, 4, 2)}.get(devices, (devices, 1, 1, 1))


class Place:
    def __init__(self, sizes):
        na, nb, nc, nk = self.sizes = sizes
        self.me = me = lax.axis_index("fsdp")
        self.k = me % nk
        self.c = (me // nk) % nc
        self.b = (me // (nk * nc)) % nb
        self.a = me // (nk * nc * nb)

    def ahead(self, axis, step):
        own = (self.a, self.b, self.c, self.k)[axis]
        return (own + step) % self.sizes[axis]

    def device(self, axis, step):
        na, nb, nc, nk = self.sizes
        where = [self.a, self.b, self.c, self.k]
        where[axis] = self.ahead(axis, step)
        return ((where[0] * nb + where[1]) * nc + where[2]) * nk + where[3]


def remote(source, target, send_sem, recv_sem, peer):
    return pltpu.make_async_remote_copy(
        src_ref=source, dst_ref=target, send_sem=send_sem, recv_sem=recv_sem,
        device_id=(peer,), device_id_type=MESH,
    )


def greet_all(devices):
    me = lax.axis_index("fsdp")
    barrier = pltpu.get_barrier_semaphore()

    def signal(j, carry):
        pl.semaphore_signal(barrier, inc=1, device_id=((me + j) % devices,), device_id_type=MESH)
        return carry

    lax.fori_loop(1, devices, signal, 0)
    pl.semaphore_wait(barrier, devices - 1)


class Exchange:
    def __init__(self, devices, source, target, sems, local_sem, turns=None):
        self.devices, self.source, self.target, self.sems, self.local_sem = devices, source, target, sems, local_sem
        self.turns = turns or (1, devices)
        self.rows = source.shape[0] // devices
        self.me = lax.axis_index("fsdp")

    def block(self, ref, device):
        return ref.at[pl.ds(pl.multiple_of(device * self.rows, self.rows), self.rows)]

    def own(self):
        return pltpu.make_async_copy(self.block(self.source, self.me), self.block(self.target, self.me), self.local_sem)

    def outgoing(self, j):
        peer = (self.me + j) % self.devices
        return remote(self.block(self.source, peer), self.block(self.target, self.me), self.sems.at[0, j], self.sems.at[1, j], peer)

    def incoming(self, j):
        peer = (self.me + self.devices - j) % self.devices
        block = self.block(self.target, peer)
        return remote(block, block, self.sems.at[0, j], self.sems.at[1, j], peer)

    def over(self, act):
        def body(j, carry):
            act((j * 13) % self.devices)
            return carry

        lax.fori_loop(*self.turns, body, 0)

    def start(self):
        self.own().start()
        self.start_remote()

    def start_remote(self):
        self.over(lambda j: self.outgoing(j).start())

    def wait(self):
        self.wait_remote()
        self.own().wait()

    def wait_remote(self):
        self.over(lambda j: self.incoming(j).wait_recv())
        self.over(lambda j: self.outgoing(j).wait_send())


def greet_peers(place):
    barrier = pltpu.get_barrier_semaphore()
    count = 0
    for axis, size in enumerate(place.sizes):
        for j in range(1, size):
            pl.semaphore_signal(barrier, inc=1, device_id=(place.device(axis, j),), device_id_type=MESH)
            count += 1
    pl.semaphore_wait(barrier, count)


def spread_scratch(sizes):
    return [pltpu.SemaphoreType.DMA((2, 4, max(sizes))), pltpu.SemaphoreType.DMA(())]


class Spread:
    def __init__(self, place, flip, own, out, scratch, lead=()):
        self.place, self.flip, self.mine, self.out, self.lead = place, flip, own, out, lead
        self.sems, self.local_sem = scratch
        self.axes = (0, 1, 2, 3) if flip else (0, 2, 1, 3)

    def region(self, stage, step=0):
        place, every = self.place, slice(None)
        where = [place.a, place.b, place.c, place.k]
        axis = self.axes[stage]
        where[axis] = place.ahead(axis, step)
        for done in self.axes[:stage]:
            where[done] = every
        return self.out.at[self.lead + tuple(where)]

    def local(self):
        return pltpu.make_async_copy(self.mine, self.region(0), self.local_sem)

    def outgoing(self, stage):
        axis = self.axes[stage]
        source = self.mine if stage == 0 else self.region(stage)
        return [
            remote(source, self.region(stage), self.sems.at[0, stage, j], self.sems.at[1, stage, j], self.place.device(axis, j))
            for j in range(1, self.place.sizes[axis])
        ]

    def start(self, stage):
        for copy in self.outgoing(stage):
            copy.start()
        if stage == 0:
            self.local().start()

    def settle(self, stage):
        axis = self.axes[stage]
        if stage == 0:
            self.local().wait()
        for j in range(1, self.place.sizes[axis]):
            block = self.region(stage, self.place.sizes[axis] - j)
            remote(block, block, self.sems.at[0, stage, j], self.sems.at[1, stage, j], self.place.device(axis, j)).wait_recv()

    def drain(self):
        for stage in range(4):
            for copy in self.outgoing(stage):
                copy.wait_send()


def store_flat(ref, base, value):
    rows, columns = value.shape
    width = ref.shape[0] // rows
    for j in range(columns // LANES):
        ref[pl.ds(base + j, rows, stride=width), :] = value[:, j * LANES:(j + 1) * LANES]


def tree_scratch(sizes, flip, rows, columns):
    na, nb, nc, nk = sizes
    one, two = (nb, nc) if flip else (nc, nb)
    shapes = [(na, nb, nc), (nk - 1, na, nb, nc), (one - 1, na, two), (two - 1, na), (na - 1,)]
    return [pltpu.VMEM(shape + (rows, columns), BF16) for shape in shapes] + [
        pltpu.SemaphoreType.DMA((2, 4, max(sizes))),
        pltpu.SemaphoreType.DMA(()),
    ]


class Tree:
    def __init__(self, place, flip, parts, scratch):
        self.place, self.flip, self.parts = place, flip, parts
        self.held, *self.landing, self.sems, self.local_sem = scratch
        order = (3, 1, 2, 0) if flip else (3, 2, 1, 0)
        self.axes = order

    def own(self):
        return pltpu.make_async_copy(self.parts.at[:, :, :, self.place.k], self.held, self.local_sem)

    def outgoing(self, stage):
        place, held = self.place, self.held
        axis = self.axes[stage]
        copies = []
        for j in range(1, place.sizes[axis]):
            other = place.ahead(axis, j)
            if stage == 0:
                source = self.parts.at[:, :, :, other]
            elif stage == 1:
                source = held.at[:, other] if self.flip else held.at[:, :, other]
            elif stage == 2:
                source = held.at[:, place.b, other] if self.flip else held.at[:, other, place.c]
            else:
                source = held.at[other, place.b, place.c]
            copies.append(
                remote(source, self.landing[stage].at[j - 1], self.sems.at[0, stage, j], self.sems.at[1, stage, j], place.device(axis, j))
            )
        return copies

    def start(self, stage):
        if stage == 0:
            self.own().start()
        for copy in self.outgoing(stage):
            copy.start()

    def settle(self, stage, out=None):
        out = out if stage == 3 else None
        place, held, landing = self.place, self.held, self.landing[stage]
        na, nb, nc, nk = place.sizes
        if stage == 0:
            self.own().wait()
        for copy in self.outgoing(stage):
            copy.wait_recv()
        count = place.sizes[self.axes[stage]] - 1

        def total(own, index):
            if count == 1 and out is None:
                return own + landing[(0,) + index]
            value = own.astype(F32)
            for j in range(count):
                value = value + landing[(j,) + index].astype(F32)
            return value

        if stage == 0:
            def add(i, carry):
                held[i] = total(held[i], (i,)).astype(BF16)
                return carry
            lax.fori_loop(0, na, add, 0)
        elif stage == 1:
            two = nc if self.flip else nb
            def add(i, carry):
                for t in range(two):
                    at = (i, place.b, t) if self.flip else (i, t, place.c)
                    held[at] = total(held[at], (i, t)).astype(BF16)
                return carry
            lax.fori_loop(0, na, add, 0)
        elif stage == 2:
            def add(i, carry):
                at = (i, place.b, place.c)
                held[at] = total(held[at], (i,)).astype(BF16)
                return carry
            lax.fori_loop(0, na, add, 0)
        else:
            out(total(held[place.a, place.b, place.c], ()))

    def drain(self):
        for stage in range(4):
            for copy in self.outgoing(stage):
                copy.wait_send()


LOW = 32
EARLY = 2


def select_rows(chosen, rows_ref):
    return dot_nn(jnp.where(chosen, 1.0, 0.0).astype(BF16), rows_ref[...]).astype(BF16)


def count_true(mask, axis):
    return jnp.sum(jnp.where(mask, 1.0, 0.0), axis=axis, keepdims=True)


def load_flat(ref, base_ref, width, store):
    total = ref.shape[0]
    base_ref[0:total, :] = ref[...].astype(F32)
    per_row = width // LANES
    for j in range(per_row):
        store(j * LANES, base_ref[pl.ds(j, total // per_row, stride=per_row), :].astype(BF16))


def block_lanes(rows, columns, share):
    lane = lax.broadcasted_iota(jnp.int32, (rows, columns), 1).astype(F32)
    inside = lane - jnp.floor((lane + 0.5) * (1.0 / share)) * share
    return inside == lax.broadcasted_iota(jnp.int32, (rows, columns), 0).astype(F32)


def line_of(blocks, share):
    devices = blocks.shape[0]
    columns = devices * share
    spread = dot_nn(blocks, jnp.where(block_lanes(LANES, columns, share), 1.0, 0.0).astype(BF16))
    start = lax.broadcasted_iota(jnp.int32, (devices, columns), 0) * share
    lane = lax.broadcasted_iota(jnp.int32, (devices, columns), 1)
    return jnp.sum(jnp.where((lane >= start) & (lane < start + share), spread, 0.0), axis=0, keepdims=True)


def split3(column):
    high = column.astype(BF16).astype(F32)
    rest = column - high
    mid = rest.astype(BF16).astype(F32)
    return high, mid, rest - mid


def feature_lanes(rows):
    lane = lax.broadcasted_iota(jnp.int32, (rows, LANES), 1)
    return lane < HD, lane & (HD - 1)


def key_features(lane, segment, segments):
    return jnp.where(lane == segment, 1.0, jnp.where((lane >= segments) & (lane < segments + 3), 1.0, 0.0))


def query_features(lane, segment, segments):
    return jnp.where((lane < segments) & (lane != segment), NEG_LARGE, 0.0)


def with_column(features, lane, start, column):
    high, mid, last = split3(column)
    features = jnp.where(lane == start, high, features)
    features = jnp.where(lane == start + 1, mid, features)
    return jnp.where(lane == start + 2, last, features)


def front_kernel(segments, sizes, cuts, lengths_ref, *refs):
    given, outs, held = refs[:18], refs[18:35], refs[35:53]
    (out_ref, lse_ref, rows_hbm, q_hbm, k_hbm, v_hbm, g4, gi, gu, cot_hbm, cot_out,
     place_row, place_col, rank_out, segment_out, vec_out, bi_out) = outs
    (leaving_ref, arrived_ref, cot_leaving, flat_ref, w4_own, wi_own, wu_own, lines_ref, vec_own, gv, blocks_ref, w_ref, rows_ref, q_ref, k_ref, v_ref,
     load_sems, save_sems, w_sem, swap_sems, swap_local, *spread_refs) = refs[53:]
    w4_refs, small_refs = held[:4], held[4:13]
    slots_ref, tokens_ref, cot_ref, wi_ref, wu_ref = held[13:]
    loads = [pltpu.make_async_copy(source, target, load_sems.at[i]) for i, (source, target) in enumerate(zip(given, held))]
    count, width = tokens_ref.shape
    devices = slots_ref.shape[0]
    peer_rows = count // devices
    share = width // devices
    tile = count // 4
    now, last = pl.program_id(0), pl.num_programs(0) - 1
    place = Place(sizes)
    me = place.me
    spreads = [
        Spread(place, False, w4_own.at[pl.ds(0, 2)], g4, spread_refs[0:2], (pl.ds(0, 2),)),
        Spread(place, True, w4_own.at[pl.ds(2, 2)], g4, spread_refs[2:4], (pl.ds(2, 2),)),
        Spread(place, True, vec_own, gv, spread_refs[4:6]),
    ]
    wide = []
    for i, (which, base, columns, flip) in enumerate(cuts):
        own, whole = ((wi_own, gi), (wu_own, gu))[which]
        cut = pl.ds(base, columns)
        wide.append(Spread(place, flip, own.at[:, cut], whole.at[:, :, :, :, :, cut], spread_refs[6 + 2 * i:8 + 2 * i]))
    swap = Exchange(devices, leaving_ref, arrived_ref, swap_sems.at[0], swap_local)
    early = Exchange(devices, cot_leaving, cot_out, swap_sems.at[1], swap_local, (1, devices // EARLY))
    w_load = pltpu.make_async_copy(g4.at[pl.ds(0, 3)], w_ref, w_sem)
    saves = [
        pltpu.make_async_copy(source, target, save_sems.at[i])
        for i, (source, target) in enumerate(((rows_ref, rows_hbm), (q_ref, q_hbm), (k_ref, k_hbm), (v_ref, v_hbm), (cot_leaving, cot_hbm)))
    ]

    def onward(group, stage):
        for spread in group:
            spread.settle(stage)
            if stage < 3:
                spread.start(stage + 1)

    def pair(i):
        return wide[2 * i:2 * i + 2]

    def begin(i):
        for spread in pair(i):
            spread.start(0)

    @pl.when(now == 0)
    def _():
        for load in loads:
            load.start()
        for load in loads[:13]:
            load.wait()
        for i, ref in enumerate(w4_refs):
            def put(at, value, i=i):
                w4_own[i, :, at:at + LANES] = value
            load_flat(ref, flat_ref, width, put)
        lines_ref[...] = jnp.zeros_like(lines_ref)
        for i, ref in enumerate(small_refs):
            lines_ref[i:i + 1, 0:ref.shape[1]] = ref[...].astype(F32)
        vec_own[...] = lines_ref[...].astype(BF16)
        greet_all(devices)
        for spread in spreads:
            spread.start(0)
        for load in loads[13:]:
            load.wait()

        cuts = [(at, slice(at, at + tile)) for at in range(0, count, tile)]
        row_at = [lax.broadcasted_iota(jnp.int32, (tile, count), 0) + at for at, _ in cuts]
        lane = lax.broadcasted_iota(jnp.int32, (tile, count), 1)
        own_row = slots_ref[pl.ds(me, 1), :]
        own_float = own_row.astype(F32)
        own_col = [jnp.sum(jnp.where(lane == row, own_float, 0.0), axis=1, keepdims=True) for row in row_at]
        rank_row = sum(count_true(col < own_float, 0) for col in own_col).astype(jnp.int32)
        for (_, cut), row in zip(cuts, row_at):
            leaving_ref[cut] = select_rows(rank_row == row, tokens_ref)
        swap.start()
        onward(spreads, 0)

        def put_inner(at, value):
            wi_own[:, at:at + LANES] = value

        def put_outer(at, value):
            wu_own[:, at:at + LANES] = value

        load_flat(wi_ref, flat_ref, wi_own.shape[1], put_inner)
        load_flat(wu_ref, flat_ref, width, put_outer)
        for (_, cut), row, col in zip(cuts, row_at, own_col):
            cot_leaving[cut] = select_rows(rank_row == row, cot_ref)
            rank_out[cut] = count_true(own_float < col, 1).astype(jnp.int32)
        saves[4].start()
        row = lax.broadcasted_iota(jnp.int32, (count, 1), 0)
        end, segment = 0, jnp.zeros((count, 1), jnp.int32)
        for i in range(lengths_ref.shape[1]):
            end = end + lengths_ref[0, i]
            segment = segment + jnp.where(row >= end, 1, 0)
        segment_out[...] = segment
        onward(spreads, 1)
        begin(0)

        high = count // LOW

        def body(s, total):
            local = slots_ref[pl.ds(s, 1), :] - me * count
            in_high = lax.broadcasted_iota(jnp.int32, (high, count), 0) == (local >> 5)
            in_low = lax.broadcasted_iota(jnp.int32, (LOW, count), 0) == (local & (LOW - 1))
            weight = jnp.where(in_high, s.astype(F32), 0.0).astype(BF16)
            return total + dot_nt(weight, jnp.where(in_low, 1.0, 0.0).astype(BF16))

        source = lax.fori_loop(0, devices, body, jnp.zeros((high, LOW), F32)).astype(BF16)
        over = lax.broadcasted_iota(jnp.int32, (high, count), 1)
        picked = dot_tn(source, jnp.where((over >> 5) == lax.broadcasted_iota(jnp.int32, (high, count), 0), 1.0, 0.0).astype(BF16))
        low_row = lax.broadcasted_iota(jnp.int32, (LOW, count), 0)
        low_wide = lax.broadcasted_iota(jnp.int32, (LOW, count), 1) & (LOW - 1)
        source_row = jnp.sum(jnp.where(low_row == low_wide, picked, 0.0), axis=0, keepdims=True)
        onward(spreads, 2)
        places = source_row * peer_rows
        for (_, cut), row in zip(cuts, row_at):
            source_col = jnp.sum(jnp.where(lane == row, source_row, 0.0), axis=1, keepdims=True)
            same = source_col == source_row
            place_col[cut] = (source_col * peer_rows + count_true(same & (lane < row), 1)).astype(jnp.int32)
            places = places + count_true(same & (row < lane), 0)
        place_row[...] = places.astype(jnp.int32)
        onward(spreads, 3)
        w_load.start()
        for i, line in enumerate(small_refs):
            for d in range(devices):
                nk, nc, nb = sizes[3], sizes[2], sizes[1]
                blocks_ref[d:d + 1, :] = gv[d // (nk * nc * nb), d // (nk * nc) % nb, d // nk % nc, d % nk].astype(F32)[i:i + 1, :]
            value = line_of(blocks_ref[...].astype(BF16), line.shape[1])
            if i < 8:
                vec_out[i:i + 1, :] = value
            else:
                bi_out[...] = value
        w_load.wait()
        onward(pair(0), 0)
        begin(1)
        swap.wait()
        vec = vec_out[...]
        wq, wk, wv = (w_ref[i].astype(F32).reshape(width, width).astype(BF16) for i in range(3))
        for at, cut in cuts:
            rows = select_rows(place_col[cut] == lane, arrived_ref)
            rows_ref[cut] = rows
            q_ref[cut] = ((dot_nn(rows, wq) + vec[0:1]).astype(BF16).astype(F32) * 0.125).astype(BF16)
            k_ref[cut] = dot_nn(rows, wk).astype(BF16)
            v_ref[cut] = (dot_nn(rows, wv) + vec[1:2]).astype(BF16)
        for save in saves[:4]:
            save.start()

    columns = pl.ds(pl.multiple_of(jnp.maximum(now - 1, 0) * LANES, LANES), LANES)
    first, feature = feature_lanes(count)

    def head(mask):
        seg = segment_out[...]
        keys = jnp.where(mask, k_ref[:, columns], key_features(feature, seg, segments).astype(BF16))
        query = jnp.where(mask, q_ref[:, columns], query_features(feature, seg, segments).astype(BF16))
        scores = dot_nt(query, keys)
        top = jnp.max(scores, axis=1, keepdims=True)
        raised = jnp.exp(scores - top)
        total = jnp.sum(raised, axis=1, keepdims=True)
        return dot_nn(raised.astype(BF16), v_ref[:, columns]) * (1.0 / total), top + jnp.log(total)

    def hook(at, act):
        @pl.when(now == at)
        def _():
            act()

    @pl.when(now > 0)
    def _():
        out0, log0 = head(first)
        out1, log1 = head(~first)
        out_ref[...] = jnp.where(first, out0, out1).astype(BF16)
        lse_ref[...] = jnp.where(first, log0, log1)

    hook(0, lambda: (onward(pair(0), 1), begin(2)))
    hook(1, lambda: (onward(pair(1), 0), early.start_remote()))
    hook(2, lambda: onward(pair(2), 0))
    hook(3, lambda: (onward(pair(0), 2), onward(pair(1), 1)))
    hook(4, lambda: onward(pair(2), 1))
    hook(5, lambda: onward(pair(1), 2))

    @pl.when(now == last)
    def _():
        onward(pair(0), 3)
        onward(pair(2), 2)
        onward(pair(1), 3)
        onward(pair(2), 3)
        for spread in spreads + wide:
            spread.drain()
        early.wait_remote()
        for save in saves:
            save.wait()


def front(segments, seq_lengths, packed_slot, tokens, cotangent, w4, wi, wu, small):
    devices, count = packed_slot.shape
    width = tokens.shape[1]
    hidden_width = small[-1].shape[0] * devices
    sizes = grid_of(devices)
    share = width // devices
    pairs = width // LANES
    anywhere = pl.BlockSpec(memory_space=pl.ANY)
    pair_spec = pl.BlockSpec((count, LANES), lambda i: (0, jnp.maximum(i - 1, 0)))

    def shape(*dims, dtype=BF16):
        return jax.ShapeDtypeStruct(dims, dtype)

    def held(*dims, dtype=BF16):
        return pltpu.VMEM(dims, dtype)

    part = width // 6
    cuts = [(0, 0, hidden_width // 2, False), (0, hidden_width // 2, hidden_width // 2, True),
            (1, 0, 2 * part, False), (1, 2 * part, 2 * part, True), (1, 4 * part, part, False), (1, 5 * part, part, True)]
    flat = [w.reshape(-1, LANES) for w in w4]
    given = flat + [x.reshape(1, -1) for x in small] + [packed_slot, tokens, cotangent, wi.reshape(-1, LANES), wu.reshape(-1, LANES)]
    whole = shape(count, width)
    lines = [shape(1, count, dtype=jnp.int32)] + [shape(count, 1, dtype=jnp.int32)] * 3 + [shape(8, width, dtype=F32), shape(1, hidden_width, dtype=F32)]
    return pl.pallas_call(
        partial(front_kernel, segments, sizes, cuts),
        grid=(1 + pairs,),
        out_shape=[whole, shape(count, width, dtype=F32)] + [whole] * 4
        + [shape(4, *sizes, share, width), shape(*sizes, share, hidden_width), shape(*sizes, hidden_width // devices, width), whole, whole] + lines,
        in_specs=[pl.BlockSpec(memory_space=pltpu.SMEM)] + [anywhere] * len(given),
        out_specs=[pair_spec, pair_spec] + [anywhere] * 9 + [full_spec(x.shape) for x in lines],
        scratch_shapes=[pltpu.VMEM(x.shape, x.dtype) for x in given]
        + [held(count, width)] * 3 + [held(*given[-1].shape, dtype=F32), held(4, share, width), held(share, hidden_width),
           held(hidden_width // devices, width), held(16, LANES, dtype=F32), held(16, LANES), held(*sizes, 16, LANES), held(devices, LANES, dtype=F32),
           held(3, *sizes, share, width)] + [held(count, width)] * 4
        + [pltpu.SemaphoreType.DMA((len(given),)), pltpu.SemaphoreType.DMA((5,)), pltpu.SemaphoreType.DMA(()),
           pltpu.SemaphoreType.DMA((2, 2, devices)), pltpu.SemaphoreType.DMA(())] + spread_scratch(sizes) * (3 + len(cuts)),
        compiler_params=params(60, "arbitrary", collective_id=1, has_side_effects=True),
        cost_estimate=pl.CostEstimate(flops=16 * count * count * width, bytes_accessed=30 * MIB, transcendentals=count * count * 12),
        name="front",
    )(seq_lengths, *given)


def normalize(hidden):
    centered = hidden - jnp.mean(hidden, axis=1, keepdims=True)
    variance = jnp.mean(centered * centered, axis=1, keepdims=True)
    inverse = lax.rsqrt(variance + EPSILON)
    return centered * inverse, inverse


def normalize_back(grad, normal, inverse):
    return inverse * (
        grad
        - jnp.mean(grad, axis=1, keepdims=True)
        - normal * jnp.mean(grad * normal, axis=1, keepdims=True)
    )


def column_sum(matrix):
    return jnp.sum(matrix.astype(F32), axis=0, keepdims=True)


def feed_kernel(sizes, tiles, chunk, where_ref, place_ref, rows_hbm, att_hbm, cot_hbm, early_hbm, w4_hbm, wi_hbm, wu_hbm, vec_ref, bi_ref,
                first_ref, agrad_ref, returned_hbm, dwi_ref, dwu_ref, dwo_ref, sums_ref, bisum_ref,
                act_ref, inner_ref, slope_ref, turned_ref, outer_ref, low_ref, normal1_ref, normal2_ref, inverse1_ref, inverse2_ref,
                cot_ref, result_ref, leaving_ref, rows_ref, att_ref, wo_ref, wi_ref, wu_ref, load_sems, early_sems, swap_sems, swap_local):
    count = att_ref.shape[0]
    tile = count // tiles
    hidden_width = wi_ref.shape[1]
    devices = sizes[0] * sizes[1] * sizes[2] * sizes[3]
    step, last = pl.program_id(0), pl.num_programs(0) - 1
    vec = vec_ref[...]
    bo, ga, sa, bu, gf, sf = (vec[i:i + 1] for i in range(2, 8))
    enter = Exchange(devices, cot_hbm, cot_ref, swap_sems.at[0], swap_local.at[0], (devices // EARLY, devices))
    early = Exchange(devices, early_hbm, cot_ref, None, None, (1, devices // EARLY))
    loads = [
        pltpu.make_async_copy(source, target, load_sems.at[i])
        for i, (source, target) in enumerate((
            (att_hbm, att_ref), (w4_hbm.at[3], wo_ref), (rows_hbm, rows_ref), (wi_hbm, wi_ref), (wu_hbm, wu_ref)
        ))
    ]

    def early_block(j):
        peer = (early.me + devices - j) % devices
        return pltpu.make_async_copy(early.block(early_hbm, peer), early.block(cot_ref, peer), early_sems.at[j])

    leave = Exchange(devices, leaving_ref, returned_hbm, swap_sems.at[1], swap_local.at[1])

    @pl.when(step == 0)
    def _():
        for load in loads:
            load.start()
        greet_all(devices)
        enter.start()
        early.over(lambda j: early_block(j).start())
        sums_ref[...] = jnp.zeros_like(sums_ref)
        bisum_ref[...] = jnp.zeros_like(bisum_ref)
        for load in loads:
            load.wait()

    @pl.when(step < tiles)
    def _():
        cut = pl.ds(pl.multiple_of(step * tile, tile), tile)
        first_sum = rows_ref[cut, :].astype(F32) + dot_nn(att_ref[cut, :], wo_ref[...]) + bo
        normal1, inverse1 = normalize(first_sum)
        normal1_ref[cut, :] = normal1
        inverse1_ref[cut, :] = inverse1
        normed = normal1 * ga + sa
        normed_low = normed.astype(BF16)
        turned_ref[:, cut] = normed.T.astype(BF16)
        second = normed + bu
        for at in range(0, hidden_width, chunk):
            pre = dot_nn(normed_low, wi_ref[:, at:at + chunk]) + bi_ref[:, at:at + chunk]
            share = 0.5 + 0.5 * lax.erf(pre * 0.7071067811865476)
            act = (pre * share).astype(BF16)
            act_ref[cut, at:at + chunk] = act
            slope_ref[cut, at:at + chunk] = (share + pre * (jnp.exp(pre * pre * -0.5) * 0.3989422804014327)).astype(BF16)
            second = second + dot_nn(act, wu_ref[at:at + chunk, :])
        normal2, inverse2 = normalize(second)
        normal2_ref[cut, :] = normal2
        inverse2_ref[cut, :] = inverse2
        result_ref[cut, :] = (normal2 * gf + sf).astype(BF16)

    @pl.when(step == tiles)
    def _():
        for at in range(0, count, tile):
            target = lax.broadcasted_iota(jnp.int32, (tile, count), 0) + at
            leaving_ref[at:at + tile] = select_rows(where_ref[...] == target, result_ref)
        early.over(lambda j: early_block(j).wait())
        enter.wait()
        leave.start()

    @pl.when((step >= tiles) & (step < 2 * tiles))
    def _():
        cut = pl.ds(pl.multiple_of((step - tiles) * tile, tile), tile)
        lane = lax.broadcasted_iota(jnp.int32, (tile, count), 1)
        chosen = jnp.where(place_ref[...] == lane, 1.0, 0.0).astype(BF16)
        cot = dot_nn(chosen, cot_ref[...])
        normal1, normal2 = normal1_ref[cut, :], normal2_ref[cut, :]
        second_grad = normalize_back(cot * gf, normal2, inverse2_ref[cut, :])
        outer_low = second_grad.astype(BF16)
        outer_ref[cut, :] = outer_low
        normed_grad = second_grad
        for at in range(0, hidden_width, chunk):
            act_grad = dot_nt(outer_low, wu_ref[at:at + chunk, :])
            inner_low = (act_grad * slope_ref[cut, at:at + chunk].astype(F32)).astype(BF16)
            inner_ref[cut, at:at + chunk] = inner_low
            bisum_ref[0:1, at:at + chunk] += column_sum(inner_low)
            normed_grad = normed_grad + dot_nt(inner_low, wi_ref[:, at:at + chunk])
        first_grad = normalize_back(normed_grad * ga, normal1, inverse1_ref[cut, :])
        first_ref[...] = first_grad
        branch_low = first_grad.astype(BF16)
        low_ref[cut, :] = branch_low
        agrad_ref[...] = dot_nt(branch_low, wo_ref[...]).astype(BF16)
        sums_ref[2:3, :] += column_sum(branch_low)
        sums_ref[3:4, :] += column_sum(normed_grad * normal1)
        sums_ref[4:5, :] += column_sum(normed_grad)
        sums_ref[5:6, :] += column_sum(outer_low)
        sums_ref[6:7, :] += column_sum(cot * normal2)
        sums_ref[7:8, :] += column_sum(cot)

    @pl.when(step >= 2 * tiles)
    def _():
        cut = pl.ds(pl.multiple_of((step - 2 * tiles) * chunk, chunk), chunk)
        dwi_ref[...] = dot_nn(turned_ref[...], inner_ref[:, cut]).astype(BF16)
        dwu_ref[...] = dot_tn(act_ref[:, cut], outer_ref[...]).astype(BF16)

    @pl.when(step == last)
    def _():
        dwo_ref[...] = dot_tn(att_ref[...], low_ref[...]).astype(BF16)
        leave.wait()


def feed_forward(devices, place_row, place_col, rows, attended, leaving_cot, early_cot, w4, wi, wu, vec, bi):
    count, width = rows.shape
    hidden_width = wi.shape[1]
    tiles, chunk = 4, 768
    tile = count // tiles
    anywhere = pl.BlockSpec(memory_space=pl.ANY)
    back_spec = pl.BlockSpec((tile, width), lambda i: (jnp.clip(i - tiles, 0, tiles - 1), 0))
    parts = hidden_width // chunk

    def part(i):
        return jnp.clip(i - 2 * tiles, 0, parts - 1)

    def held(n, dtype=BF16):
        return pltpu.VMEM((count, n), dtype)

    return pl.pallas_call(
        partial(feed_kernel, grid_of(devices), tiles, chunk),
        grid=(2 * tiles + parts,),
        out_shape=[
            jax.ShapeDtypeStruct((count, width), F32), jax.ShapeDtypeStruct((count, width), BF16), jax.ShapeDtypeStruct((count, width), BF16),
            jax.ShapeDtypeStruct((width, hidden_width), BF16), jax.ShapeDtypeStruct((hidden_width, width), BF16),
            jax.ShapeDtypeStruct((width, width), BF16), jax.ShapeDtypeStruct((8, width), F32), jax.ShapeDtypeStruct((8, hidden_width), F32),
        ],
        in_specs=[
            held_spec((1, count)), pl.BlockSpec((tile, 1), lambda i: (jnp.clip(i - tiles, 0, tiles - 1), 0)),
            anywhere, anywhere, anywhere, anywhere, anywhere, anywhere, anywhere, held_spec(vec.shape), held_spec(bi.shape),
        ],
        out_specs=[
            back_spec, back_spec, anywhere,
            pl.BlockSpec((width, chunk), lambda i: (0, part(i))), pl.BlockSpec((chunk, width), lambda i: (part(i), 0)),
            full_spec((width, width)), full_spec((8, width)), full_spec((8, hidden_width)),
        ],
        scratch_shapes=[
            held(hidden_width), held(hidden_width), held(hidden_width), pltpu.VMEM((width, count), BF16), held(width), held(width),
            held(width, F32), held(width, F32), held(1, F32), held(1, F32), held(width), held(width), held(width),
            held(width), held(width), pltpu.VMEM((width, width), BF16), pltpu.VMEM(wi.shape, BF16), pltpu.VMEM(wu.shape, BF16),
            pltpu.SemaphoreType.DMA((5,)), pltpu.SemaphoreType.DMA((devices,)), pltpu.SemaphoreType.DMA((2, 2, devices)), pltpu.SemaphoreType.DMA((2,)),
        ],
        compiler_params=params(62, "arbitrary", collective_id=5, has_side_effects=True),
        cost_estimate=pl.CostEstimate(flops=20 * count * width * hidden_width, bytes_accessed=36 * MIB, transcendentals=2 * count * hidden_width),
        name="feed_forward",
    )(place_row, place_col, rows, attended, leaving_cot, early_cot, w4, wi, wu, vec, bi)


def by_device(line, devices, share):
    count = line.shape[1]
    start = lax.broadcasted_iota(jnp.int32, (devices, count), 0) * share
    lane = lax.broadcasted_iota(jnp.int32, (devices, count), 1)
    left = jnp.where((lane >= start) & (lane < start + share), line, 0.0).astype(BF16)
    return dot_nt(left, jnp.where(block_lanes(LANES, count, share), 1.0, 0.0).astype(BF16))


def back_kernel(segments, sizes, share, cuts, seg_ref, where_ref, q_ref, o_ref, g_ref, lse_ref, k_ref, v_ref, sums_ref, bisum_ref,
                wi_ref, wu_ref, wo_ref, first_hbm, w4_hbm, rows_hbm, *refs):
    back_ref, wi_out, wu_out, wo_out, wq_out, wk_out, wv_out, *small_outs = refs[:16]
    (dq_ref, dk_ref, dv_ref, first_ref, w_ref, rows_ref, load_sems, total_ref, leaving_ref, wq_part, wk_part, wv_part,
     lines_ref, small_part, swap_sems, swap_local, *tree_refs) = refs[16:]
    count, width = total_ref.shape
    na, nb, nc, nk = sizes
    devices = na * nb * nc * nk
    tile = count // 4
    now, last = pl.program_id(0), pl.num_programs(0) - 1
    place = Place(sizes)
    loads = [
        pltpu.make_async_copy(source, target, load_sems.at[i])
        for i, (source, target) in enumerate(((first_hbm, first_ref), (w4_hbm.at[pl.ds(0, 3)], w_ref), (rows_hbm, rows_ref)))
    ]
    swap = Exchange(devices, leaving_ref, back_ref, swap_sems, swap_local)
    outs = {0: wi_out, 1: wu_out, 2: wo_out}
    every = (slice(None),) * 5
    trees, ends = [], []
    for i, (which, base, columns, flip) in enumerate(cuts):
        parts = (wi_ref, wu_ref, wo_ref)[which].at[every + (pl.ds(base, columns),)]
        trees.append(Tree(place, flip, parts, tree_refs[7 * i:7 * i + 7]))
        ends.append(partial(store_flat, outs[which], base // LANES))
    late_parts = (wq_part, wk_part, wv_part, small_part)
    late = [
        Tree(place, i % 2 == 1, part, tree_refs[7 * (len(cuts) + i):7 * (len(cuts) + i) + 7])
        for i, part in enumerate(late_parts)
    ]

    @pl.when(now == 0)
    def _():
        greet_all(devices)
        for tree in trees[:3]:
            tree.start(0)
        for load in loads:
            load.start()

    groups = (slice(0, 3), slice(3, 5), slice(5, 7), slice(7, 9))

    def onward(group, stage, then=None):
        for tree, end in zip(trees[groups[group]], ends[groups[group]]):
            tree.settle(stage, end)
            if stage < 3:
                tree.start(stage + 1)
        if then is not None:
            for tree in trees[groups[then]]:
                tree.start(0)

    def hook(at, act):
        @pl.when(now == at)
        def _():
            act()

    first, lane = feature_lanes(count)
    columns = pl.ds(pl.multiple_of(now * LANES, LANES), LANES)

    def head(mask, at):
        seg, grads = seg_ref[...], g_ref[...]
        ones = key_features(lane, seg, segments).astype(BF16)
        keys = jnp.where(mask, k_ref[...], ones)
        values = jnp.where(mask, v_ref[...], ones)
        lse = lse_ref[:, at:at + 1]
        product = grads.astype(F32) * o_ref[...].astype(F32)
        delta = jnp.sum(jnp.where(mask, product, 0.0), axis=1, keepdims=True)
        hidden = query_features(lane, seg, segments)
        query = jnp.where(mask, q_ref[...], with_column(hidden, lane, segments, -lse).astype(BF16))
        grad = jnp.where(mask, grads, with_column(jnp.zeros_like(hidden), lane, segments, -delta).astype(BF16))
        dqs, dk, dv = [], 0.0, 0.0
        for top in range(0, count, count // PARTS):
            cut = slice(top, top + count // PARTS)
            probs = jnp.exp(dot_nt(keys, query[cut]))
            score = (probs * dot_nt(values, grad[cut])).astype(BF16)
            dv = dv + dot_nn(probs.astype(BF16), grad[cut])
            dk = dk + dot_nn(score, query[cut])
            dqs.append(dot_tn(score, keys))
        return (jnp.concatenate(dqs) * 0.125).astype(BF16), dk.astype(BF16), dv.astype(BF16)

    for ref, value in zip((dq_ref, dk_ref, dv_ref), head(first, 0)):
        ref[:, columns] = value

    hook(0, lambda: onward(0, 0, 1))
    hook(3, lambda: onward(0, 2))
    hook(4, lambda: (onward(1, 1), onward(2, 0, 3)))
    hook(5, lambda: (onward(1, 2), onward(2, 1), onward(3, 0)))

    for ref, value in zip((dq_ref, dk_ref, dv_ref), head(~first, HD)):
        ref[:, columns] = jnp.where(first, ref[:, columns], value)

    hook(1, lambda: (onward(0, 1), onward(1, 0, 2)))

    @pl.when(now == last)
    def _():
        for load in loads:
            load.wait()
        for at in range(0, count, tile):
            cut = slice(at, at + tile)
            total_ref[cut] = (
                first_ref[cut] + dot_nt(dq_ref[cut], w_ref[0]) + dot_nt(dk_ref[cut], w_ref[1]) + dot_nt(dv_ref[cut], w_ref[2])
            ).astype(BF16)
        onward(2, 2)
        onward(3, 1)
        for at in range(0, count, tile):
            target = lax.broadcasted_iota(jnp.int32, (tile, count), 0) + at
            leaving_ref[at:at + tile] = select_rows(where_ref[...] == target, total_ref)
        onward(0, 3)
        onward(3, 2)
        group = 3 * LANES
        for grad_ref, part, tree in zip((dq_ref, dk_ref, dv_ref), late_parts, late):
            for at in range(0, width, group):
                value = dot_tn(rows_ref[:, at:at + group], grad_ref[...])
                for i in range(group // share):
                    d = at // share + i
                    index = (d // (nk * nc * nb), d // (nk * nc) % nb, d // nk % nc, d % nk)
                    part[index] = value[i * share:(i + 1) * share].astype(BF16)
            tree.start(0)
        onward(1, 3)
        onward(2, 3)
        lines_ref[...] = jnp.zeros_like(lines_ref)
        lines_ref[0] = by_device(column_sum(dq_ref[...]), devices, share)
        lines_ref[1] = by_device(column_sum(dv_ref[...]), devices, share)
        for i in range(2, 8):
            lines_ref[i] = by_device(sums_ref[i:i + 1, :], devices, share)
        lines_ref[8] = by_device(bisum_ref[0:1, :], devices, bisum_ref.shape[1] // devices)
        for d in range(devices):
            index = (d // (nk * nc * nb), d // (nk * nc) % nb, d // nk % nc, d % nk)
            small_part[index] = lines_ref[:, d, :].astype(BF16)
        late[3].start(0)
        onward(3, 3)
        swap.start()
        for stage in range(3):
            for tree in late:
                tree.settle(stage)
                tree.start(stage + 1)
        for tree, out in zip(late, (wq_out, wk_out, wv_out)):
            tree.settle(3, partial(store_flat, out, 0))

        def store_small(value):
            for i, out in enumerate(small_outs):
                out[...] = value[i:i + 1, :out.shape[1]]

        late[3].settle(3, store_small)
        swap.wait()
        for tree in trees + late:
            tree.drain()


PARTS = 1


def backward(segments, segment_col, place_row, q, out, grad, lse, k, v, sums, bi_sum, wi, wu, wo, first_grad, w4, rows):
    count, width = q.shape
    pairs = width // LANES
    devices = wi.shape[0]
    share = width // devices
    sizes = grid_of(devices)
    pair_spec = pl.BlockSpec((count, LANES), lambda h: (0, h))
    anywhere = pl.BlockSpec(memory_space=pl.ANY)
    parts = [x.reshape(sizes + x.shape[1:]) for x in (wi, wu, wo)]
    cuts = []
    for base, size in ((0, 2), (2, 2), (4, 1), (5, 1)):
        for which, x in ((0, wi), (1, wu)):
            cuts.append((which, base * x.shape[2] // 6, size * x.shape[2] // 6, which == 1))
        if base == 0:
            cuts.append((2, 0, wo.shape[2], False))
    trees = []
    for which, _, columns, flip in cuts:
        trees += tree_scratch(sizes, flip, (wi, wu, wo)[which].shape[1], columns)
    for i, shape in enumerate(((share, width),) * 3 + ((16, LANES),)):
        trees += tree_scratch(sizes, i % 2 == 1, *shape)
    flats = [(x.shape[1] * x.shape[2] // LANES, LANES) for x in (wi, wu, wo)] + [(share * width // LANES, LANES)] * 3
    flats += [(1, share)] * 8 + [(1, bi_sum.shape[1] // devices)]
    whole = pltpu.VMEM((count, width), BF16)
    return pl.pallas_call(
        partial(back_kernel, segments, sizes, share, cuts),
        grid=(pairs,),
        out_shape=[jax.ShapeDtypeStruct((count, width), BF16)] + [jax.ShapeDtypeStruct(flat, F32) for flat in flats],
        in_specs=[held_spec((count, 1)), held_spec((1, count))] + [pair_spec] * 6 + [held_spec(sums.shape), held_spec(bi_sum.shape)]
        + [anywhere] * 6,
        out_specs=[anywhere] + [full_spec(flat) for flat in flats],
        scratch_shapes=[whole] * 3 + [pltpu.VMEM((count, width), F32), pltpu.VMEM((3, width, width), BF16), whole, pltpu.SemaphoreType.DMA((3,))]
        + [whole] * 2 + [pltpu.VMEM(sizes + (share, width), BF16)] * 3
        + [pltpu.VMEM((16, devices, LANES), F32), pltpu.VMEM(sizes + (16, LANES), BF16)]
        + [pltpu.SemaphoreType.DMA((2, devices)), pltpu.SemaphoreType.DMA(())] + trees,
        compiler_params=params(63, "arbitrary", collective_id=2, has_side_effects=True),
        cost_estimate=pl.CostEstimate(flops=20 * count * count * width, bytes_accessed=16 * MIB, transcendentals=count * count * 12),
        name="backward",
    )(segment_col, place_row, q, out, grad, lse, k, v, sums, bi_sum, *parts, first_grad, w4, rows)


def emit_kernel(rank_ref, back_hbm, layer_hbm, *refs):
    count = (len(refs) - 5) // 2
    given, tokens_ref, layer_ref, outs, (back_ref, held_ref, sems) = refs[:count], refs[count], refs[count + 1], refs[count + 2:2 * count + 2], refs[2 * count + 2:]
    moved = [
        pltpu.make_async_copy(source, target, sems.at[i])
        for i, (source, target) in enumerate(zip((back_hbm, layer_hbm, *given), (back_ref, held_ref, *outs)))
    ]
    for copy in moved:
        copy.start()
    rows = back_ref.shape[0]
    tile = rows // 4
    for copy in moved[:2]:
        copy.wait()
    for at in range(0, rows, tile):
        lane = lax.broadcasted_iota(jnp.int32, (tile, rows), 1)
        chosen = rank_ref[at:at + tile] == lane
        tokens_ref[at:at + tile] = select_rows(chosen, back_ref)
        layer_ref[at:at + tile] = select_rows(chosen, held_ref)
    for copy in moved[2:]:
        copy.wait()


def emit(rank_col, back, layer, others):
    anywhere = pl.BlockSpec(memory_space=pl.ANY)
    in_vmem = pl.BlockSpec(memory_space=pltpu.VMEM)
    return pl.pallas_call(
        emit_kernel,
        out_shape=[jax.ShapeDtypeStruct(x.shape, x.dtype) for x in (back, layer, *others)],
        in_specs=[in_vmem] + [anywhere] * (2 + len(others)),
        out_specs=[in_vmem] * (2 + len(others)),
        scratch_shapes=[pltpu.VMEM(back.shape, BF16)] * 2 + [pltpu.SemaphoreType.DMA((len(others) + 2,))],
        compiler_params=pltpu.CompilerParams(vmem_limit_bytes=56 * MIB),
        name="emit",
    )(rank_col, back, layer, *others)


def on_device(tokens, cotangent, packed_slot, seq_lengths, query_weight, query_bias, key_weight, value_weight,
              value_bias, output_weight, output_bias, attention_gain, attention_shift, inner_weight, inner_bias,
              outer_weight, outer_bias, final_gain, final_shift):
    devices = lax.axis_size("fsdp")
    count, width = tokens.shape
    hidden_width = inner_bias.shape[0] * devices
    segments = seq_lengths.shape[1]
    share = width // devices
    small = (query_bias, value_bias, output_bias, attention_gain, attention_shift, outer_bias, final_gain, final_shift, inner_bias)
    (attended, lse, rows, q, k, v, g4, gi, gu, leaving_cot, early_cot, place_row, place_col, rank_col, segment_col, vec, bi) = front(
        segments, seq_lengths, packed_slot.reshape(devices, count), tokens, cotangent,
        (query_weight, key_weight, value_weight, output_weight), inner_weight, outer_weight, small,
    )
    w4 = g4.reshape(4, width, width)
    wi = gi.reshape(width, hidden_width)
    wu = gu.reshape(hidden_width, width)
    first_grad, attended_grad, returned, inner_grad, outer_grad, wo_grad, sums, bi_sum = feed_forward(
        devices, place_row, place_col, rows, attended, leaving_cot, early_cot, w4, wi, wu, vec, bi
    )
    inner_grad, outer_grad, wo_grad = (x.reshape(devices, -1, x.shape[-1]) for x in (inner_grad, outer_grad, wo_grad))
    back, inner_grad, outer_grad, wo_grad, wq_grad, wk_grad, wv_grad, *small = backward(
        segments, segment_col, place_row, q, attended, attended_grad, lse, k, v, sums, bi_sum,
        inner_grad, outer_grad, wo_grad, first_grad, w4, rows,
    )
    tokens_grad, layer_out, wq_grad, wk_grad, wv_grad, wo_grad, inner_grad, outer_grad, *small = emit(
        rank_col, back, returned, (wq_grad, wk_grad, wv_grad, wo_grad, inner_grad, outer_grad, *small)
    )
    wq_grad, wk_grad, wv_grad, wo_grad, wi_grad, wu_grad = (
        x.reshape(-1) for x in (wq_grad, wk_grad, wv_grad, wo_grad, inner_grad, outer_grad)
    )
    bq, bv, bo, ga, sa, bu, gf, sf, bi = (x.reshape(-1) for x in small)
    return (layer_out, tokens_grad, wq_grad, bq, wk_grad, wv_grad, bv, wo_grad, bo, ga, sa, wi_grad, bi, wu_grad, bu, gf, sf)


def solution(mesh):
    split, rows = P("fsdp"), P("fsdp", None)
    return jax.shard_map(
        on_device,
        mesh=mesh,
        in_specs=(rows, rows, P(), rows) + (split,) * 15,
        out_specs=(rows, rows) + (split,) * 15,
        check_vma=False,
    )
```

time: 378 us -> 342 us (0.905)
  Pallas kernels: 365 us -> 334 us
    pallas_call x4 -> x2, Pallas kernels: 292 us -> 260 us  [the longest x1 133 us: backward(): pl.pallas_call(partial(back_kernel, segments, sizes, share, cuts), grid=(...]
where the time goes in v4:
time: 342 us; the launch traced here: 337 us
  Pallas kernels  334 us (98%)
    pallas_call x1, Pallas kernels, backward(): pl.pallas_call(partial(back_kernel, segments, sizes, share, cuts), grid=(...  133 us
    pallas_call x1, Pallas kernels, front(): pl.pallas_call(partial(front_kernel, segments, sizes, cuts), grid=(1 + pa...  127 us
    pallas_call x1, Pallas kernels, feed_forward(): pl.pallas_call(partial(feed_kernel, grid_of(devices), tiles, chunk), grid...  65.2 us
    pallas_call x1, Pallas kernels, emit(): pl.pallas_call(emit_kernel, out_shape=[jax.ShapeDtypeStruct(x.shape, x.dt...  8.61 us

profile of v4, /device:TPU:0, one launch (start us, length us, event | category | flops | bytes accessed | tf_op | source)
XLA Modules:
  0.0 336.6 jit_solution(5019471457925595999)
XLA Ops:
  0.7 1.6 reshape.149.refs_13_
  2.2 126.8 %front.1 = (bf16[1024,768]{1,0:T(8,128)(2,1)}, f32[1024,768]{1,0:T(8,128)}, bf16[1024,768]{1,0:T(8,128)(2,1)}, bf16[1024,768]{1,0:T(8,128)(2,1)}, bf16[1024,768]...) custom-call(s32[1,4]{1,0:T(1,128)} %lengths_ref.1, ...), custom_call_target="tpu_custom_call" | custom-call | flops 12884901888 | bytes 31457280 | tf_op jit(solution)/shard_map/front/pallas_call | solution.py:572
  129.0 65.2 %feed_forward.1 = (f32[1024,768]{1,0:T(8,128)}, bf16[1024,768]{1,0:T(8,128)(2,1)}, bf16[1024,768]{1,0:T(8,128)(2,1)}, bf16[768,3072]{1,0:T(8,128)(2,1)}, bf16[30...) custom-call(s32[1,1024]{1,0:T(1,128)} %get-tuple-element.77.where_ref, ...), custom_call_target="tpu_custom_call" | custom-call | flops 48318382080 | bytes 37748736 | tf_op jit(solution)/shard_map/feed_forward/pallas_call | solution.py:736
  194.3 133.4 %backward.1 = (bf16[1024,768]{1,0:T(8,128)(2,1)}, f32[576,128]{1,0:T(8,128)}, f32[576,128]{1,0:T(8,128)}, f32[144,128]{1,0:T(8,128)}, f32[144,128]{1,0:T(8,128)}...) custom-call(s32[1024,1]{1,0:T(8,128)} %get-tuple-element.76.seg_ref,, ...), custom_call_target="tpu_custom_call" | custom-call | flops 16106127360 | bytes 16777216 | tf_op jit(solution)/shard_map/backward/pallas_call | solution.py:945
  327.7 8.6 %emit.1 = (bf16[1024,768]{1,0:T(8,128)(2,1)}, bf16[1024,768]{1,0:T(8,128)(2,1)}, f32[144,128]{1,0:T(8,128)}, f32[144,128]{1,0:T(8,128)}, f32[144,128]{1,0:T(8,12...) custom-call(s32[1024,1]{1,0:T(8,128)} %get-tuple-element.75.rank_ref, ...), custom_call_target="tpu_custom_call" | custom-call | tf_op jit(solution)/shard_map/emit/pallas_call | solution.py:987

commit v5 on v4

--- a/solution.py
+++ b/solution.py
@@ -301,6 +301,15 @@
     return jnp.sum(jnp.where(mask, 1.0, 0.0), axis=axis, keepdims=True)
 
 
+def each_tile(tile, count, act):
+    def body(t, carry):
+        at = pl.multiple_of(t * tile, tile)
+        act(pl.ds(at, tile), lax.broadcasted_iota(jnp.int32, (tile, count), 0) + at)
+        return carry
+
+    lax.fori_loop(0, count // tile, body, 0)
+
+
 def load_flat(ref, base_ref, width, store):
     total = ref.shape[0]
     base_ref[0:total, :] = ref[...].astype(F32)
@@ -355,7 +364,7 @@
     given, outs, held = refs[:18], refs[18:35], refs[35:53]
     (out_ref, lse_ref, rows_hbm, q_hbm, k_hbm, v_hbm, g4, gi, gu, cot_hbm, cot_out,
      place_row, place_col, rank_out, segment_out, vec_out, bi_out) = outs
-    (leaving_ref, arrived_ref, cot_leaving, flat_ref, w4_own, wi_own, wu_own, lines_ref, vec_own, gv, blocks_ref, w_ref, rows_ref, q_ref, k_ref, v_ref,
+    (leaving_ref, arrived_ref, cot_leaving, flat_ref, w4_own, wi_own, wu_own, lines_ref, vec_own, gv, blocks_ref, w_ref, flat_w, rows_ref, q_ref, k_ref, v_ref,
      load_sems, save_sems, w_sem, swap_sems, swap_local, *spread_refs) = refs[53:]
     w4_refs, small_refs = held[:4], held[4:13]
     slots_ref, tokens_ref, cot_ref, wi_ref, wu_ref = held[13:]
@@ -419,15 +428,23 @@
         for load in loads[13:]:
             load.wait()
 
-        cuts = [(at, slice(at, at + tile)) for at in range(0, count, tile)]
-        row_at = [lax.broadcasted_iota(jnp.int32, (tile, count), 0) + at for at, _ in cuts]
         lane = lax.broadcasted_iota(jnp.int32, (tile, count), 1)
         own_row = slots_ref[pl.ds(me, 1), :]
         own_float = own_row.astype(F32)
-        own_col = [jnp.sum(jnp.where(lane == row, own_float, 0.0), axis=1, keepdims=True) for row in row_at]
-        rank_row = sum(count_true(col < own_float, 0) for col in own_col).astype(jnp.int32)
-        for (_, cut), row in zip(cuts, row_at):
-            leaving_ref[cut] = select_rows(rank_row == row, tokens_ref)
+
+        def column_of(row, line):
+            return jnp.sum(jnp.where(lane == row, line, 0.0), axis=1, keepdims=True)
+
+        def rank_tile(t, total):
+            row = lax.broadcasted_iota(jnp.int32, (tile, count), 0) + t * tile
+            return total + count_true(column_of(row, own_float) < own_float, 0)
+
+        rank_row = lax.fori_loop(0, count // tile, rank_tile, jnp.zeros((1, count), F32)).astype(jnp.int32)
+
+        def leave(cut, row):
+            leaving_ref[cut, :] = select_rows(rank_row == row, tokens_ref)
+
+        each_tile(tile, count, leave)
         swap.start()
         onward(spreads, 0)
 
@@ -439,9 +456,12 @@
 
         load_flat(wi_ref, flat_ref, wi_own.shape[1], put_inner)
         load_flat(wu_ref, flat_ref, width, put_outer)
-        for (_, cut), row, col in zip(cuts, row_at, own_col):
-            cot_leaving[cut] = select_rows(rank_row == row, cot_ref)
-            rank_out[cut] = count_true(own_float < col, 1).astype(jnp.int32)
+
+        def leave_cot(cut, row):
+            cot_leaving[cut, :] = select_rows(rank_row == row, cot_ref)
+            rank_out[cut, :] = count_true(own_float < column_of(row, own_float), 1).astype(jnp.int32)
+
+        each_tile(tile, count, leave_cot)
         saves[4].start()
         row = lax.broadcasted_iota(jnp.int32, (count, 1), 0)
         end, segment = 0, jnp.zeros((count, 1), jnp.int32)
@@ -468,13 +488,16 @@
         low_wide = lax.broadcasted_iota(jnp.int32, (LOW, count), 1) & (LOW - 1)
         source_row = jnp.sum(jnp.where(low_row == low_wide, picked, 0.0), axis=0, keepdims=True)
         onward(spreads, 2)
-        places = source_row * peer_rows
-        for (_, cut), row in zip(cuts, row_at):
-            source_col = jnp.sum(jnp.where(lane == row, source_row, 0.0), axis=1, keepdims=True)
+
+        def place_tile(t, places):
+            at = pl.multiple_of(t * tile, tile)
+            row = lax.broadcasted_iota(jnp.int32, (tile, count), 0) + at
+            source_col = column_of(row, source_row)
             same = source_col == source_row
-            place_col[cut] = (source_col * peer_rows + count_true(same & (lane < row), 1)).astype(jnp.int32)
-            places = places + count_true(same & (row < lane), 0)
-        place_row[...] = places.astype(jnp.int32)
+            place_col[pl.ds(at, tile), :] = (source_col * peer_rows + count_true(same & (lane < row), 1)).astype(jnp.int32)
+            return places + count_true(same & (row < lane), 0)
+
+        place_row[...] = lax.fori_loop(0, count // tile, place_tile, source_row * peer_rows).astype(jnp.int32)
         onward(spreads, 3)
         w_load.start()
         for i, line in enumerate(small_refs):
@@ -492,12 +515,17 @@
         swap.wait()
         vec = vec_out[...]
         wq, wk, wv = (w_ref[i].astype(F32).reshape(width, width).astype(BF16) for i in range(3))
-        for at, cut in cuts:
-            rows = select_rows(place_col[cut] == lane, arrived_ref)
-            rows_ref[cut] = rows
-            q_ref[cut] = ((dot_nn(rows, wq) + vec[0:1]).astype(BF16).astype(F32) * 0.125).astype(BF16)
-            k_ref[cut] = dot_nn(rows, wk).astype(BF16)
-            v_ref[cut] = (dot_nn(rows, wv) + vec[1:2]).astype(BF16)
+        for i, w in enumerate((wq, wk, wv)):
+            flat_w[i] = w
+
+        def project(cut, _):
+            rows = select_rows(place_col[cut, :] == lane, arrived_ref)
+            rows_ref[cut, :] = rows
+            q_ref[cut, :] = ((dot_nn(rows, flat_w[0]) + vec[0:1]).astype(BF16).astype(F32) * 0.125).astype(BF16)
+            k_ref[cut, :] = dot_nn(rows, flat_w[1]).astype(BF16)
+            v_ref[cut, :] = (dot_nn(rows, flat_w[2]) + vec[1:2]).astype(BF16)
+
+        each_tile(tile, count, project)
         for save in saves[:4]:
             save.start()
 
@@ -579,7 +607,7 @@
         scratch_shapes=[pltpu.VMEM(x.shape, x.dtype) for x in given]
         + [held(count, width)] * 3 + [held(*given[-1].shape, dtype=F32), held(4, share, width), held(share, hidden_width),
            held(hidden_width // devices, width), held(16, LANES, dtype=F32), held(16, LANES), held(*sizes, 16, LANES), held(devices, LANES, dtype=F32),
-           held(3, *sizes, share, width)] + [held(count, width)] * 4
+           held(3, *sizes, share, width), held(3, width, width)] + [held(count, width)] * 4
         + [pltpu.SemaphoreType.DMA((len(given),)), pltpu.SemaphoreType.DMA((5,)), pltpu.SemaphoreType.DMA(()),
            pltpu.SemaphoreType.DMA((2, 2, devices)), pltpu.SemaphoreType.DMA(())] + spread_scratch(sizes) * (3 + len(cuts)),
         compiler_params=params(60, "arbitrary", collective_id=1, has_side_effects=True),
@@ -670,9 +698,10 @@
 
     @pl.when(step == tiles)
     def _():
-        for at in range(0, count, tile):
-            target = lax.broadcasted_iota(jnp.int32, (tile, count), 0) + at
-            leaving_ref[at:at + tile] = select_rows(where_ref[...] == target, result_ref)
+        def leave_tile(cut, target):
+            leaving_ref[cut, :] = select_rows(where_ref[...] == target, result_ref)
+
+        each_tile(tile, count, leave_tile)
         early.over(lambda j: early_block(j).wait())
         enter.wait()
         leave.start()
@@ -799,14 +828,6 @@
         for i, part in enumerate(late_parts)
     ]
 
-    @pl.when(now == 0)
-    def _():
-        greet_all(devices)
-        for tree in trees[:3]:
-            tree.start(0)
-        for load in loads:
-            load.start()
-
     groups = (slice(0, 3), slice(3, 5), slice(5, 7), slice(7, 9))
 
     def onward(group, stage, then=None):
@@ -822,6 +843,13 @@
         @pl.when(now == at)
         def _():
             act()
+
+    @pl.when(now == 0)
+    def _():
+        greet_all(devices)
+        for tree in trees[groups[0]]:
+            tree.start(0)
+        onward(0, 0, 1)
 
     first, lane = feature_lanes(count)
     columns = pl.ds(pl.multiple_of(now * LANES, LANES), LANES)
@@ -847,46 +875,48 @@
             dqs.append(dot_tn(score, keys))
         return (jnp.concatenate(dqs) * 0.125).astype(BF16), dk.astype(BF16), dv.astype(BF16)
 
-    for ref, value in zip((dq_ref, dk_ref, dv_ref), head(first, 0)):
-        ref[:, columns] = value
-
-    hook(0, lambda: onward(0, 0, 1))
-    hook(3, lambda: onward(0, 2))
-    hook(4, lambda: (onward(1, 1), onward(2, 0, 3)))
-    hook(5, lambda: (onward(1, 2), onward(2, 1), onward(3, 0)))
-
-    for ref, value in zip((dq_ref, dk_ref, dv_ref), head(~first, HD)):
-        ref[:, columns] = jnp.where(first, ref[:, columns], value)
+    for ref, one, two in zip((dq_ref, dk_ref, dv_ref), head(first, 0), head(~first, HD)):
+        ref[:, columns] = jnp.where(first, one, two)
 
     hook(1, lambda: (onward(0, 1), onward(1, 0, 2)))
+    hook(3, lambda: (onward(0, 2), onward(1, 1), onward(2, 0, 3), [load.start() for load in loads]))
+    hook(4, lambda: (onward(1, 2), onward(2, 1), onward(3, 0)))
+    hook(5, lambda: (onward(2, 2), onward(3, 1)))
 
     @pl.when(now == last)
     def _():
         for load in loads:
             load.wait()
-        for at in range(0, count, tile):
-            cut = slice(at, at + tile)
-            total_ref[cut] = (
-                first_ref[cut] + dot_nt(dq_ref[cut], w_ref[0]) + dot_nt(dk_ref[cut], w_ref[1]) + dot_nt(dv_ref[cut], w_ref[2])
+
+        def total_tile(cut, _):
+            total_ref[cut, :] = (
+                first_ref[cut, :] + dot_nt(dq_ref[cut, :], w_ref[0]) + dot_nt(dk_ref[cut, :], w_ref[1]) + dot_nt(dv_ref[cut, :], w_ref[2])
             ).astype(BF16)
-        onward(2, 2)
-        onward(3, 1)
-        for at in range(0, count, tile):
-            target = lax.broadcasted_iota(jnp.int32, (tile, count), 0) + at
-            leaving_ref[at:at + tile] = select_rows(where_ref[...] == target, total_ref)
+
+        each_tile(tile, count, total_tile)
+        onward(3, 2)
         onward(0, 3)
-        onward(3, 2)
+
+        def leave(cut, target):
+            leaving_ref[cut, :] = select_rows(where_ref[...] == target, total_ref)
+
+        each_tile(tile, count, leave)
+        onward(1, 3)
+        onward(2, 3)
+        onward(3, 3)
+        swap.start()
         group = 3 * LANES
         for grad_ref, part, tree in zip((dq_ref, dk_ref, dv_ref), late_parts, late):
-            for at in range(0, width, group):
-                value = dot_tn(rows_ref[:, at:at + group], grad_ref[...])
+            def weight_tile(t, carry, grad_ref=grad_ref, part=part):
+                value = dot_tn(rows_ref[:, pl.ds(pl.multiple_of(t * group, group), group)], grad_ref[...])
                 for i in range(group // share):
-                    d = at // share + i
+                    d = t * (group // share) + i
                     index = (d // (nk * nc * nb), d // (nk * nc) % nb, d // nk % nc, d % nk)
                     part[index] = value[i * share:(i + 1) * share].astype(BF16)
+                return carry
+
+            lax.fori_loop(0, width // group, weight_tile, 0)
             tree.start(0)
-        onward(1, 3)
-        onward(2, 3)
         lines_ref[...] = jnp.zeros_like(lines_ref)
         lines_ref[0] = by_device(column_sum(dq_ref[...]), devices, share)
         lines_ref[1] = by_device(column_sum(dv_ref[...]), devices, share)
@@ -897,8 +927,6 @@
             index = (d // (nk * nc * nb), d // (nk * nc) % nb, d // nk % nc, d % nk)
             small_part[index] = lines_ref[:, d, :].astype(BF16)
         late[3].start(0)
-        onward(3, 3)
-        swap.start()
         for stage in range(3):
             for tree in late:
                 tree.settle(stage)
@@ -972,11 +1000,14 @@
     tile = rows // 4
     for copy in moved[:2]:
         copy.wait()
-    for at in range(0, rows, tile):
-        lane = lax.broadcasted_iota(jnp.int32, (tile, rows), 1)
-        chosen = rank_ref[at:at + tile] == lane
-        tokens_ref[at:at + tile] = select_rows(chosen, back_ref)
-        layer_ref[at:at + tile] = select_rows(chosen, held_ref)
+    lane = lax.broadcasted_iota(jnp.int32, (tile, rows), 1)
+
+    def restore(cut, _):
+        chosen = rank_ref[cut, :] == lane
+        tokens_ref[cut, :] = select_rows(chosen, back_ref)
+        layer_ref[cut, :] = select_rows(chosen, held_ref)
+
+    each_tile(tile, rows, restore)
     for copy in moved[2:]:
         copy.wait()
 

time: 342 us -> 324 us (0.947); the launches traced: 337 us -> 324 us
  Pallas kernels: 334 us -> 321 us
    pallas_call x1, Pallas kernels: 133 us -> 119 us  [backward(): pl.pallas_call(partial(back_kernel, segments, sizes, share, cuts), grid=(...]
where the time goes in v5:
time: 324 us
  Pallas kernels  321 us (99%)
    pallas_call x1, Pallas kernels, front(): pl.pallas_call(partial(front_kernel, segments, sizes, cuts), grid=(1 + pa...  127 us
    pallas_call x1, Pallas kernels, backward(): pl.pallas_call(partial(back_kernel, segments, sizes, share, cuts), grid=(...  119 us
    pallas_call x1, Pallas kernels, feed_forward(): pl.pallas_call(partial(feed_kernel, grid_of(devices), tiles, chunk), grid...  66 us
    pallas_call x1, Pallas kernels, emit(): pl.pallas_call(emit_kernel, out_shape=[jax.ShapeDtypeStruct(x.shape, x.dt...  9.33 us

profile of v5, /device:TPU:0, one launch (start us, length us, event | category | flops | bytes accessed | tf_op | source)
XLA Modules:
  0.0 323.7 jit_solution(3453360550709138272)
XLA Ops:
  0.7 1.6 reshape.149.refs_13_
  2.2 126.5 %front.1 = (bf16[1024,768]{1,0:T(8,128)(2,1)}, f32[1024,768]{1,0:T(8,128)}, bf16[1024,768]{1,0:T(8,128)(2,1)}, bf16[1024,768]{1,0:T(8,128)(2,1)}, bf16[1024,768]...) custom-call(s32[1,4]{1,0:T(1,128)} %lengths_ref.1, ...), custom_call_target="tpu_custom_call" | custom-call | flops 12884901888 | bytes 31457280 | tf_op jit(solution)/shard_map/front/pallas_call | solution.py:600
  128.8 66.0 %feed_forward.1 = (f32[1024,768]{1,0:T(8,128)}, bf16[1024,768]{1,0:T(8,128)(2,1)}, bf16[1024,768]{1,0:T(8,128)(2,1)}, bf16[768,3072]{1,0:T(8,128)(2,1)}, bf16[30...) custom-call(s32[1,1024]{1,0:T(1,128)} %get-tuple-element.77.where_ref, ...), custom_call_target="tpu_custom_call" | custom-call | flops 48318382080 | bytes 37748736 | tf_op jit(solution)/shard_map/feed_forward/pallas_call | solution.py:765
  194.8 119.4 %backward.1 = (bf16[1024,768]{1,0:T(8,128)(2,1)}, f32[576,128]{1,0:T(8,128)}, f32[576,128]{1,0:T(8,128)}, f32[144,128]{1,0:T(8,128)}, f32[144,128]{1,0:T(8,128)}...) custom-call(s32[1024,1]{1,0:T(8,128)} %get-tuple-element.76.seg_ref,, ...), custom_call_target="tpu_custom_call" | custom-call | flops 16106127360 | bytes 16777216 | tf_op jit(solution)/shard_map/backward/pallas_call | solution.py:973
  314.2 9.3 %emit.1 = (bf16[1024,768]{1,0:T(8,128)(2,1)}, bf16[1024,768]{1,0:T(8,128)(2,1)}, f32[144,128]{1,0:T(8,128)}, f32[144,128]{1,0:T(8,128)}, f32[144,128]{1,0:T(8,12...) custom-call(s32[1024,1]{1,0:T(8,128)} %get-tuple-element.75.rank_ref, ...), custom_call_target="tpu_custom_call" | custom-call | tf_op jit(solution)/shard_map/emit/pallas_call | solution.py:1018

commit v6 on v5

--- a/solution.py
+++ b/solution.py
@@ -364,10 +364,10 @@
     given, outs, held = refs[:18], refs[18:35], refs[35:53]
     (out_ref, lse_ref, rows_hbm, q_hbm, k_hbm, v_hbm, g4, gi, gu, cot_hbm, cot_out,
      place_row, place_col, rank_out, segment_out, vec_out, bi_out) = outs
-    (leaving_ref, arrived_ref, cot_leaving, flat_ref, w4_own, wi_own, wu_own, lines_ref, vec_own, gv, blocks_ref, w_ref, flat_w, rows_ref, q_ref, k_ref, v_ref,
+    (leaving_ref, arrived_ref, cot_leaving, flat_ref, w4_own, wi_own, wu_own, lines_ref, vec_own, gv, blocks_ref, w_ref, flat_w, slots_ref, rows_ref, q_ref, k_ref, v_ref,
      load_sems, save_sems, w_sem, swap_sems, swap_local, *spread_refs) = refs[53:]
     w4_refs, small_refs = held[:4], held[4:13]
-    slots_ref, tokens_ref, cot_ref, wi_ref, wu_ref = held[13:]
+    slots_flat, tokens_ref, cot_ref, wi_ref, wu_ref = held[13:]
     loads = [pltpu.make_async_copy(source, target, load_sems.at[i]) for i, (source, target) in enumerate(zip(given, held))]
     count, width = tokens_ref.shape
     devices = slots_ref.shape[0]
@@ -427,6 +427,9 @@
             spread.start(0)
         for load in loads[13:]:
             load.wait()
+        per_row = count // LANES
+        for j in range(per_row):
+            slots_ref[:, j * LANES:(j + 1) * LANES] = slots_flat[pl.ds(j, devices, stride=per_row), :]
 
         lane = lax.broadcasted_iota(jnp.int32, (tile, count), 1)
         own_row = slots_ref[pl.ds(me, 1), :]
@@ -575,8 +578,9 @@
 
 
 def front(segments, seq_lengths, packed_slot, tokens, cotangent, w4, wi, wu, small):
-    devices, count = packed_slot.shape
     width = tokens.shape[1]
+    count = tokens.shape[0]
+    devices = packed_slot.shape[0] // count
     hidden_width = small[-1].shape[0] * devices
     sizes = grid_of(devices)
     share = width // devices
@@ -594,7 +598,7 @@
     cuts = [(0, 0, hidden_width // 2, False), (0, hidden_width // 2, hidden_width // 2, True),
             (1, 0, 2 * part, False), (1, 2 * part, 2 * part, True), (1, 4 * part, part, False), (1, 5 * part, part, True)]
     flat = [w.reshape(-1, LANES) for w in w4]
-    given = flat + [x.reshape(1, -1) for x in small] + [packed_slot, tokens, cotangent, wi.reshape(-1, LANES), wu.reshape(-1, LANES)]
+    given = flat + [x.reshape(1, -1) for x in small] + [packed_slot.reshape(-1, LANES), tokens, cotangent, wi.reshape(-1, LANES), wu.reshape(-1, LANES)]
     whole = shape(count, width)
     lines = [shape(1, count, dtype=jnp.int32)] + [shape(count, 1, dtype=jnp.int32)] * 3 + [shape(8, width, dtype=F32), shape(1, hidden_width, dtype=F32)]
     return pl.pallas_call(
@@ -607,7 +611,7 @@
         scratch_shapes=[pltpu.VMEM(x.shape, x.dtype) for x in given]
         + [held(count, width)] * 3 + [held(*given[-1].shape, dtype=F32), held(4, share, width), held(share, hidden_width),
            held(hidden_width // devices, width), held(16, LANES, dtype=F32), held(16, LANES), held(*sizes, 16, LANES), held(devices, LANES, dtype=F32),
-           held(3, *sizes, share, width), held(3, width, width)] + [held(count, width)] * 4
+           held(3, *sizes, share, width), held(3, width, width), held(devices, count, dtype=jnp.int32)] + [held(count, width)] * 4
         + [pltpu.SemaphoreType.DMA((len(given),)), pltpu.SemaphoreType.DMA((5,)), pltpu.SemaphoreType.DMA(()),
            pltpu.SemaphoreType.DMA((2, 2, devices)), pltpu.SemaphoreType.DMA(())] + spread_scratch(sizes) * (3 + len(cuts)),
         compiler_params=params(60, "arbitrary", collective_id=1, has_side_effects=True),
@@ -702,9 +706,9 @@
             leaving_ref[cut, :] = select_rows(where_ref[...] == target, result_ref)
 
         each_tile(tile, count, leave_tile)
+        leave.start()
         early.over(lambda j: early_block(j).wait())
         enter.wait()
-        leave.start()
 
     @pl.when((step >= tiles) & (step < 2 * tiles))
     def _():
@@ -1036,7 +1040,7 @@
     share = width // devices
     small = (query_bias, value_bias, output_bias, attention_gain, attention_shift, outer_bias, final_gain, final_shift, inner_bias)
     (attended, lse, rows, q, k, v, g4, gi, gu, leaving_cot, early_cot, place_row, place_col, rank_col, segment_col, vec, bi) = front(
-        segments, seq_lengths, packed_slot.reshape(devices, count), tokens, cotangent,
+        segments, seq_lengths, packed_slot, tokens, cotangent,
         (query_weight, key_weight, value_weight, output_weight), inner_weight, outer_weight, small,
     )
     w4 = g4.reshape(4, width, width)

time: 324 us -> 322 us (level)
  no operation moved by 1% of the time
where the time goes in v6:
time: 322 us
  Pallas kernels  321 us (100%)
    pallas_call x1, Pallas kernels, front(): pl.pallas_call(partial(front_kernel, segments, sizes, cuts), grid=(1 + pa...  127 us
    pallas_call x1, Pallas kernels, backward(): pl.pallas_call(partial(back_kernel, segments, sizes, share, cuts), grid=(...  120 us
    pallas_call x1, Pallas kernels, feed_forward(): pl.pallas_call(partial(feed_kernel, grid_of(devices), tiles, chunk), grid...  64.8 us
    pallas_call x1, Pallas kernels, emit(): pl.pallas_call(emit_kernel, out_shape=[jax.ShapeDtypeStruct(x.shape, x.dt...  9.33 us

profile of v6, /device:TPU:0, one launch (start us, length us, event | category | flops | bytes accessed | tf_op | source)
XLA Modules:
  0.0 321.6 jit_solution(17643100337935457117)
XLA Ops:
  0.7 126.6 %front.1 = (bf16[1024,768]{1,0:T(8,128)(2,1)}, f32[1024,768]{1,0:T(8,128)}, bf16[1024,768]{1,0:T(8,128)(2,1)}, bf16[1024,768]{1,0:T(8,128)(2,1)}, bf16[1024,768]...) custom-call(s32[1,4]{1,0:T(1,128)} %lengths_ref.1, ...), custom_call_target="tpu_custom_call" | custom-call | flops 12884901888 | bytes 31457280 | tf_op jit(solution)/shard_map/front/pallas_call | solution.py:604
  127.3 64.8 %feed_forward.1 = (f32[1024,768]{1,0:T(8,128)}, bf16[1024,768]{1,0:T(8,128)(2,1)}, bf16[1024,768]{1,0:T(8,128)(2,1)}, bf16[768,3072]{1,0:T(8,128)(2,1)}, bf16[30...) custom-call(s32[1,1024]{1,0:T(1,128)} %get-tuple-element.77.where_ref, ...), custom_call_target="tpu_custom_call" | custom-call | flops 48318382080 | bytes 37748736 | tf_op jit(solution)/shard_map/feed_forward/pallas_call | solution.py:769
  192.1 120.0 %backward.1 = (bf16[1024,768]{1,0:T(8,128)(2,1)}, f32[576,128]{1,0:T(8,128)}, f32[576,128]{1,0:T(8,128)}, f32[144,128]{1,0:T(8,128)}, f32[144,128]{1,0:T(8,128)}...) custom-call(s32[1024,1]{1,0:T(8,128)} %get-tuple-element.76.seg_ref,, ...), custom_call_target="tpu_custom_call" | custom-call | flops 16106127360 | bytes 16777216 | tf_op jit(solution)/shard_map/backward/pallas_call | solution.py:977
  312.1 9.3 %emit.1 = (bf16[1024,768]{1,0:T(8,128)(2,1)}, bf16[1024,768]{1,0:T(8,128)(2,1)}, f32[144,128]{1,0:T(8,128)}, f32[144,128]{1,0:T(8,128)}, f32[144,128]{1,0:T(8,12...) custom-call(s32[1024,1]{1,0:T(8,128)} %get-tuple-element.75.rank_ref, ...), custom_call_target="tpu_custom_call" | custom-call | tf_op jit(solution)/shard_map/emit/pallas_call | solution.py:1022

commit v7 on v6

--- a/solution.py
+++ b/solution.py
@@ -991,40 +991,51 @@
     )(segment_col, place_row, q, out, grad, lse, k, v, sums, bi_sum, *parts, first_grad, w4, rows)
 
 
-def emit_kernel(rank_ref, back_hbm, layer_hbm, *refs):
-    count = (len(refs) - 5) // 2
-    given, tokens_ref, layer_ref, outs, (back_ref, held_ref, sems) = refs[:count], refs[count], refs[count + 1], refs[count + 2:2 * count + 2], refs[2 * count + 2:]
+def emit_kernel(count, rank_ref, back_hbm, layer_hbm, *refs):
+    given, tokens_hbm, layer_out, outs = refs[:count], refs[count], refs[count + 1], refs[count + 2:2 * count + 2]
+    back_ref, held_ref, tokens_ref, layer_ref, *staged, sems, save_sems = refs[2 * count + 2:]
     moved = [
         pltpu.make_async_copy(source, target, sems.at[i])
-        for i, (source, target) in enumerate(zip((back_hbm, layer_hbm, *given), (back_ref, held_ref, *outs)))
+        for i, (source, target) in enumerate(zip((back_hbm, layer_hbm, *given), (back_ref, held_ref, *staged)))
+    ]
+    saves = [
+        pltpu.make_async_copy(source, target, save_sems.at[i])
+        for i, (source, target) in enumerate(zip((tokens_ref, layer_ref, *staged), (tokens_hbm, layer_out, *outs)))
     ]
     for copy in moved:
         copy.start()
     rows = back_ref.shape[0]
     tile = rows // 4
-    for copy in moved[:2]:
+    lane = lax.broadcasted_iota(jnp.int32, (tile, rows), 1)
+
+    def restore(source, target):
+        def act(cut, _):
+            target[cut, :] = select_rows(rank_ref[cut, :] == lane, source)
+        return act
+
+    moved[0].wait()
+    each_tile(tile, rows, restore(back_ref, tokens_ref))
+    saves[0].start()
+    for copy, save in zip(moved[2:], saves[2:]):
         copy.wait()
-    lane = lax.broadcasted_iota(jnp.int32, (tile, rows), 1)
-
-    def restore(cut, _):
-        chosen = rank_ref[cut, :] == lane
-        tokens_ref[cut, :] = select_rows(chosen, back_ref)
-        layer_ref[cut, :] = select_rows(chosen, held_ref)
-
-    each_tile(tile, rows, restore)
-    for copy in moved[2:]:
-        copy.wait()
+        save.start()
+    moved[1].wait()
+    each_tile(tile, rows, restore(held_ref, layer_ref))
+    saves[1].start()
+    for save in saves:
+        save.wait()
 
 
 def emit(rank_col, back, layer, others):
     anywhere = pl.BlockSpec(memory_space=pl.ANY)
     in_vmem = pl.BlockSpec(memory_space=pltpu.VMEM)
     return pl.pallas_call(
-        emit_kernel,
+        partial(emit_kernel, len(others)),
         out_shape=[jax.ShapeDtypeStruct(x.shape, x.dtype) for x in (back, layer, *others)],
         in_specs=[in_vmem] + [anywhere] * (2 + len(others)),
-        out_specs=[in_vmem] * (2 + len(others)),
-        scratch_shapes=[pltpu.VMEM(back.shape, BF16)] * 2 + [pltpu.SemaphoreType.DMA((len(others) + 2,))],
+        out_specs=[anywhere] * (2 + len(others)),
+        scratch_shapes=[pltpu.VMEM(back.shape, BF16)] * 4 + [pltpu.VMEM(x.shape, x.dtype) for x in others]
+        + [pltpu.SemaphoreType.DMA((len(others) + 2,))] * 2,
         compiler_params=pltpu.CompilerParams(vmem_limit_bytes=56 * MIB),
         name="emit",
     )(rank_col, back, layer, *others)

time: 322 us -> 334 us (1.037)
  Pallas kernels: 321 us -> 331 us
    pallas_call x1, Pallas kernels: 120 us -> 130 us  [backward(): pl.pallas_call(partial(back_kernel, segments, sizes, share, cuts), grid=(...]
where the time goes in v7:
time: 334 us; the launch traced here: 332 us
  Pallas kernels  331 us (99%)
    pallas_call x1, Pallas kernels, backward(): pl.pallas_call(partial(back_kernel, segments, sizes, share, cuts), grid=(...  130 us
    pallas_call x1, Pallas kernels, front(): pl.pallas_call(partial(front_kernel, segments, sizes, cuts), grid=(1 + pa...  127 us
    pallas_call x1, Pallas kernels, feed_forward(): pl.pallas_call(partial(feed_kernel, grid_of(devices), tiles, chunk), grid...  64.9 us
    pallas_call x1, Pallas kernels, emit(): pl.pallas_call(partial(emit_kernel, len(others)), out_shape=[jax.ShapeDty...  9.29 us

profile of v7, /device:TPU:0, one launch (start us, length us, event | category | flops | bytes accessed | tf_op | source)
XLA Modules:
  0.0 331.6 jit_solution(12283711070247754701)
XLA Ops:
  0.7 126.6 %front.1 = (bf16[1024,768]{1,0:T(8,128)(2,1)}, f32[1024,768]{1,0:T(8,128)}, bf16[1024,768]{1,0:T(8,128)(2,1)}, bf16[1024,768]{1,0:T(8,128)(2,1)}, bf16[1024,768]...) custom-call(s32[1,4]{1,0:T(1,128)} %lengths_ref.1, ...), custom_call_target="tpu_custom_call" | custom-call | flops 12884901888 | bytes 31457280 | tf_op jit(solution)/shard_map/front/pallas_call | solution.py:604
  127.3 64.9 %feed_forward.1 = (f32[1024,768]{1,0:T(8,128)}, bf16[1024,768]{1,0:T(8,128)(2,1)}, bf16[1024,768]{1,0:T(8,128)(2,1)}, bf16[768,3072]{1,0:T(8,128)(2,1)}, bf16[30...) custom-call(s32[1,1024]{1,0:T(1,128)} %get-tuple-element.77.where_ref, ...), custom_call_target="tpu_custom_call" | custom-call | flops 48318382080 | bytes 37748736 | tf_op jit(solution)/shard_map/feed_forward/pallas_call | solution.py:769
  192.1 130.0 %backward.1 = (bf16[1024,768]{1,0:T(8,128)(2,1)}, f32[576,128]{1,0:T(8,128)}, f32[576,128]{1,0:T(8,128)}, f32[144,128]{1,0:T(8,128)}, f32[144,128]{1,0:T(8,128)}...) custom-call(s32[1024,1]{1,0:T(8,128)} %get-tuple-element.76.seg_ref,, ...), custom_call_target="tpu_custom_call" | custom-call | flops 16106127360 | bytes 16777216 | tf_op jit(solution)/shard_map/backward/pallas_call | solution.py:977
  322.1 9.3 %emit.1 = (bf16[1024,768]{1,0:T(8,128)(2,1)}, bf16[1024,768]{1,0:T(8,128)(2,1)}, f32[144,128]{1,0:T(8,128)}, f32[144,128]{1,0:T(8,128)}, f32[144,128]{1,0:T(8,12...) custom-call(s32[1024,1]{1,0:T(8,128)} %get-tuple-element.75.rank_ref, ...), custom_call_target="tpu_custom_call" | custom-call | tf_op jit(solution)/shard_map/emit/pallas_call | solution.py:1032
